TPU v7x, 256 devices: a whole 4x4x8 slice. The times are simulated.
256 devices in a mesh: cp: 32 (over y_hi, z, core), vocab: 8 (over y_lo, x).
Axes of the slice: x: 4, y: 4 (y_hi: 2, y_lo: 2; y = y_hi * 2 + y_lo), z: 8, core: 2. Of those that a mesh axis runs over, the one named last changes fastest.
Arguments:
- queries: bfloat16 [4096, 4096], P('cp', 'vocab'), may hold values from -160 to 160
- key_states: bfloat16 [4096, 1024], P('cp', 'vocab'), may hold values from -6 to 6
- value_states: bfloat16 [4096, 1024], P('cp', 'vocab'), may hold values from -6 to 6
- out_grad: bfloat16 [4096, 4096], P('cp', 'vocab'), may hold values from -6 to 6
- o_weight: bfloat16 [4096, 4096], P('vocab'), may hold values from -0.09375 to 0.09375
- span_order: int32 [64], replicated, may hold values from 0 to 63, each once
Outputs:
- query_grad: float32 [4096, 4096], P('cp', 'vocab')
- key_grad: float32 [4096, 1024], P('cp', 'vocab')
- value_grad: float32 [4096, 1024], P('cp', 'vocab')
Inputs may be any that keep to these rules, and one draw needn't show every extreme that they name: `span_order`: each of the 64 span indices once.
All inputs are finite; a program needn't handle non-finite values.
Results may differ from a plain program's by a relative error of at most 0.014.
Values may be sent and summed in bfloat16 or wider, within the bound.
No kernel may reach another device: no remote copies, remote signals or barrier semaphores. Data moves between devices by JAX's collectives and lax.ppermute only.
A program may use at most 64 MiB of HBM per device.

v0:
```python
import jax
import jax.numpy as jnp
from jax import lax
from jax.sharding import Mesh
from jax.sharding import PartitionSpec as P

HEADS = 32
KV_HEADS = 8
HEAD_DIM = 128
CP = ("cp_0", "cp_1", "cp_2")


def joined_along(blocks, dim):
    blocks = jnp.moveaxis(blocks, 0, dim)
    shape = blocks.shape
    return blocks.reshape(*shape[:dim], shape[dim] * shape[dim + 1], *shape[dim + 2 :])


def from_everyone(value, axis):
    peers = lax.axis_size(axis)
    return lax.all_to_all(
        jnp.broadcast_to(value[None], (peers, *value.shape)), axis, 0, 0, tiled=True
    )


def collect(value, axis, dim):
    return joined_along(from_everyone(value, axis), dim)


def whole_of(value, axes, dim):
    far, near = axes
    leading = from_everyone(value, far)
    blocks = jnp.swapaxes(from_everyone(leading, near), 0, 1)
    return joined_along(blocks.reshape(-1, *value.shape), dim)


def sent_together(arrays, axis, dim, along):
    both = jnp.concatenate(arrays, axis=along)
    whole, at, gathered = (whole_of(both, axis, dim), 0, [])
    for a in arrays:
        gathered.append(lax.slice_in_dim(whole, at, at + a.shape[along], axis=along))
        at += a.shape[along]
    return tuple(gathered)


def in_blocks(value, dim, peers):
    before, after = (value.shape[:dim], value.shape[dim + 1 :])
    return jnp.moveaxis(value.reshape(*before, peers, -1, *after), dim, 0)


def sum_at_owner(value, axis, dim):
    peers = lax.axis_size(axis)
    blocks = lax.all_to_all(in_blocks(value, dim, peers), axis, 0, 0, tiled=True)
    return jnp.sum(blocks.astype(jnp.float32), axis=0)


def summed_rows(value, axes, dim):
    far, near = axes
    own = sum_at_owner(in_blocks(value, dim, lax.axis_size(far)), near, dim + 1)
    return jnp.sum(
        lax.all_to_all(own.astype(jnp.bfloat16), far, 0, 0, tiled=True).astype(jnp.float32), axis=0
    )


def positions(span_order, span_rows):
    offsets = jnp.arange(span_rows, dtype=jnp.int32)
    return (span_order[:, None] * span_rows + offsets[None, :]).reshape(-1)


def block_scores(query_block, key_block, query_places, key_places, factor):
    scores = (
        jnp.einsum("qkgd,skd->kgqs", query_block, key_block, preferred_element_type=jnp.float32)
        * factor
    )
    visible = key_places[None, :] <= query_places[:, None]
    return jnp.where(visible, scores, -jnp.inf)


def local(queries, key_states, value_states, out_grad, o_weight, span_order):
    own_rows = queries.shape[0]
    kv_width = key_states.shape[1]
    kv_heads = kv_width // HEAD_DIM
    groups = HEADS // KV_HEADS
    factor = HEAD_DIM ** (-0.5)
    upstream = lax.dot_general(
        collect(out_grad, "vocab", 1),
        o_weight,
        (((1,), (1,)), ((), ())),
        preferred_element_type=jnp.float32,
    ).astype(jnp.bfloat16)
    places = positions(span_order, own_rows // 2)
    seq_len = places.shape[0]
    own_places = lax.dynamic_slice_in_dim(places, lax.axis_index(CP) * own_rows, own_rows, 0)
    query_heads = queries.reshape(own_rows, kv_heads, groups, HEAD_DIM)
    upstream_heads = upstream.reshape(own_rows, kv_heads, groups, HEAD_DIM)
    key_all, value_all = sent_together((key_states, value_states), (("cp_0", "cp_1"), "cp_2"), 0, 1)
    key_all = key_all.reshape(seq_len, kv_heads, HEAD_DIM)
    value_all = value_all.reshape(seq_len, kv_heads, HEAD_DIM)
    block_rows = own_rows * 8
    block_count = seq_len // block_rows
    block_ids = jnp.arange(block_count, dtype=jnp.int32)
    stat_shape = (kv_heads, groups, own_rows)

    def key_block(block_index):
        offset = block_index * block_rows
        return (
            lax.dynamic_slice_in_dim(key_all, offset, block_rows, 0),
            lax.dynamic_slice_in_dim(value_all, offset, block_rows, 0),
            lax.dynamic_slice_in_dim(places, offset, block_rows, 0),
        )

    def stats_step(carried, block_index):
        running, totals, delta_acc = carried
        keys_now, values_now, places_now = key_block(block_index)
        scores = block_scores(query_heads, keys_now, own_places, places_now, factor)
        newest = jnp.maximum(running, jnp.max(scores, axis=3))
        rescale = jnp.exp(running - newest)
        raised = jnp.exp(scores - newest[..., None])
        grad_probs = jnp.einsum(
            "qkgd,skd->kgqs", upstream_heads, values_now, preferred_element_type=jnp.float32
        )
        totals = totals * rescale + jnp.sum(raised, axis=3)
        delta_acc = delta_acc * rescale + jnp.sum(raised * grad_probs, axis=3)
        return ((newest, totals, delta_acc), None)

    start_stats = (
        jnp.full(stat_shape, -1e30, jnp.float32),
        jnp.zeros(stat_shape, jnp.float32),
        jnp.zeros(stat_shape, jnp.float32),
    )
    (running, totals, delta_acc), unused = lax.scan(stats_step, start_stats, block_ids)
    logsum = running + jnp.log(totals)
    deltas = delta_acc / totals

    def grad_pieces(block_index):
        keys_now, values_now, places_now = key_block(block_index)
        scores = block_scores(query_heads, keys_now, own_places, places_now, factor)
        weights = jnp.exp(scores - logsum[..., None])
        grad_probs = jnp.einsum(
            "qkgd,skd->kgqs", upstream_heads, values_now, preferred_element_type=jnp.float32
        )
        grad_scores = (weights * (grad_probs - deltas[..., None])).astype(jnp.bfloat16)
        return (keys_now, weights, grad_scores)

    query_zeros = jnp.zeros((own_rows, kv_heads, groups, HEAD_DIM), jnp.float32)

    def grad_step(carried, block_index):
        keys_now, weights, grad_scores = grad_pieces(block_index)
        carried = (
            carried
            + jnp.einsum(
                "kgqs,skd->qkgd", grad_scores, keys_now, preferred_element_type=jnp.float32
            )
            * factor
        )
        key_term = (
            jnp.einsum(
                "kgqs,qkgd->skd", grad_scores, query_heads, preferred_element_type=jnp.float32
            )
            * factor
        )
        value_term = jnp.einsum(
            "kgqs,qkgd->skd",
            weights.astype(jnp.bfloat16),
            upstream_heads,
            preferred_element_type=jnp.float32,
        )
        joined = jnp.concatenate(
            (key_term.reshape(block_rows, kv_width), value_term.reshape(block_rows, kv_width)),
            axis=1,
        )
        return (carried, joined)

    query_total, stacked = lax.scan(grad_step, query_zeros, block_ids)
    terms = stacked.reshape(seq_len, 2 * kv_width)
    mine = summed_rows(terms.astype(jnp.bfloat16), (("cp_0", "cp_1"), "cp_2"), 0)
    key_grad = mine[:, :kv_width]
    value_grad = mine[:, kv_width:]
    query_grad = query_total.reshape(own_rows, kv_heads * groups * HEAD_DIM)
    return (query_grad, key_grad, value_grad)


def solution(mesh):
    finer = Mesh(
        mesh.devices.reshape(2, 8, 2, mesh.shape["vocab"]), ("cp_0", "cp_1", "cp_2", "vocab")
    )
    return jax.shard_map(
        local,
        mesh=finer,
        in_specs=(
            P(CP, "vocab"),
            P(CP, "vocab"),
            P(CP, "vocab"),
            P(CP, "vocab"),
            P("vocab", None),
            P(),
        ),
        out_specs=(P(CP, "vocab"), P(CP, "vocab"), P(CP, "vocab")),
        check_vma=False,
    )
```

profile of v0, /device:TPU:2, one launch (start us, length us, event | category | flops | bytes accessed | tf_op | source)
XLA Modules:
  0.0 161.3 jit_solution(5398240033900326470)
XLA Ops:
  0.7 1.0 copy.70
  1.7 1.1 broadcast_in_dim.59
  2.8 5.8 %all-to-all-start.2 = ((bf16[8,128,512]{1,2,0:T(8,128)(2,1)}), bf16[8,128,512]{1,2,0:T(8,128)(2,1)S(1)}, u32[]{:S(2)}, u32[]{:S(2)}) async-start(bf16[8,128,512]{1,2,0:T(8,128)(2,1)} %broadcast_in_dim.59), calls=%async_computation.2 | async-start | bytes 2097152 | tf_op jit(solution)/shard_map/all_to_all | solution.py:21
  8.7 14.5 %all-to-all-done.2 = bf16[8,128,512]{1,2,0:T(8,128)(2,1)S(1)} async-done(((bf16[8,128,512]{1,2,0:T(8,128)(2,1)}), bf16[8,128,512]{1,2,0:T(8,128)(2,1)S(1)}, u32[]{:S(2)}, u32[]{:S(2)}) %all-to-all-start.2) | async-done | bytes 1048608 | tf_op jit(solution)/shard_map/all_to_all | solution.py:21
  23.2 1.1 broadcast_in_dim.56
  24.3 11.0 %all-to-all-start = ((bf16[16,128,256]{2,1,0:T(8,128)(2,1)}), bf16[16,128,256]{2,1,0:T(8,128)(2,1)}, u32[]{:S(2)}, u32[]{:S(2)}) async-start(bf16[16,128,256]{2,1,0:T(8,128)(2,1)} %broadcast_in_dim.56), calls=%async_computation | async-start | bytes 2097152 | tf_op jit(solution)/shard_map/all_to_all | solution.py:21
  35.5 0.8 copy.69
  36.2 1.0 copy.71
  37.8 3.7 %convolution_convert_fusion = bf16[128,512]{1,0:T(8,128)(2,1)S(1)} fusion(bf16[128,4096]{0,1:T(8,128)(2,1)S(1)} %bitcast.177, bf16[512,4096]{1,0:T(8,128)(2,1)} %param.14), kind=kOutput, calls=%fused_computation.52 | convolution fusion | flops 536936448 | bytes 5373952 | tf_op jit(solution)/shard_map/dot_general | solution.py:85
  41.8 20.8 %all-to-all-done = bf16[16,128,256]{2,1,0:T(8,128)(2,1)} async-done(((bf16[16,128,256]{2,1,0:T(8,128)(2,1)}), bf16[16,128,256]{2,1,0:T(8,128)(2,1)}, u32[]{:S(2)}, u32[]{:S(2)}) %all-to-all-start) | async-done | bytes 1048608 | tf_op jit(solution)/shard_map/all_to_all | solution.py:21
  62.6 1.5 broadcast_in_dim.57
  64.0 5.4 %all_to_all.25 = bf16[2,16,128,256]{3,2,1,0:T(8,128)(2,1)S(1)} all-to-all(bf16[2,16,128,256]{3,2,1,0:T(8,128)(2,1)S(1)} %broadcast_in_dim.57), channel_id=1, replica_groups=mesh['cp_0'=2,'cp_1'=8,'cp_2'=2,'vocab'=8] {'cp_2'}, dimensions={0} | all-to-all | bytes 4194304 | tf_op jit(solution)/shard_map/all_to_all | solution.py:21
  69.8 13.4 %while.28 = (s32[]{:T(128)}, f32[1,4,128]{2,1,0:T(4,128)S(1)}, f32[1,4,128]{2,1,0:T(4,128)S(1)}, f32[1,4,128]{2,1,0:T(4,128)S(1)}, s32[4]{0:T(128)S(1)}, /*index...) while((s32[]{:T(128)}, f32[1,4,128]{2,1,0:T(4,128)S(1)}, ...), condition=%wide.region_4.5_spmd.clone, body=%wide.region_0.4_spmd.clone.sunk | while | flops 272764416 | bytes 7389926 | solution.py:131
  71.1 0.8 broadcast_compare_fusion.4
  74.4 0.8 broadcast_compare_fusion.4
  77.8 0.8 broadcast_compare_fusion.4
  81.2 0.8 broadcast_compare_fusion.4
  84.3 34.3 %while.29 = (s32[]{:T(128)}, f32[128,1,4,128]{0,3,2,1:T(8,128)S(1)}, bf16[4,1024,256]{2,1,0:T(8,128)(2,1)}, s32[4]{0:T(128)}, bf16[4096,1,128]{2,0,1:T(8,128)(2,...) while((s32[]{:T(128)}, ...), condition=%wide.region_6.7_spmd.clone, body=%wide.region_5.6_spmd.clone.sunk | while | flops 676397056 | bytes 15221493 | solution.py:174
  84.3 1.2 dynamic_slice.75
  86.2 0.8 broadcast_compare_fusion.5
  87.0 1.5 fusion.74
  88.9 1.1 fusion.75
  90.4 1.4 fusion.77
  92.0 0.8 constant_dynamic-update-slice_fusion.2
  92.9 1.2 dynamic_slice.75
  94.7 0.8 broadcast_compare_fusion.5
  95.5 1.4 fusion.74
  97.5 1.1 fusion.75
  99.0 1.4 fusion.77
  100.6 0.8 constant_dynamic-update-slice_fusion.2
  101.4 1.2 dynamic_slice.75
  103.3 0.8 broadcast_compare_fusion.5
  104.1 1.5 fusion.74
  106.0 1.1 fusion.75
  107.5 1.4 fusion.77
  109.2 0.8 constant_dynamic-update-slice_fusion.2
  110.0 1.2 dynamic_slice.75
  111.9 0.8 broadcast_compare_fusion.5
  112.7 1.5 fusion.74
  114.6 1.1 fusion.75
  116.1 1.4 fusion.77
  117.8 0.8 constant_dynamic-update-slice_fusion.2
  118.6 1.7 %copy.76 = bf16[2,16,128,256]{3,2,1,0:T(8,128)(2,1)S(1)} copy(bf16[2,16,128,256]{3,2,0,1:T(8,128)(2,1)} %bitcast.178) | data formatting | bytes 4194304 | tf_op jit(solution)/shard_map/transpose | solution.py:48
  120.3 5.4 %all_to_all.26 = bf16[2,16,128,256]{3,2,1,0:T(8,128)(2,1)S(1)} all-to-all(bf16[2,16,128,256]{3,2,1,0:T(8,128)(2,1)S(1)} %copy.76), channel_id=1, replica_groups=mesh['cp_0'=2,'cp_1'=8,'cp_2'=2,'vocab'=8] {'cp_2'}, dimensions={0} | all-to-all | bytes 4194304 | tf_op jit(solution)/shard_map/all_to_all | solution.py:53
  125.7 1.6 %reduce_sum.43 = bf16[16,128,256]{2,1,0:T(8,128)(2,1)} reduce(bf16[2,16,128,256]{3,2,1,0:T(8,128)(2,1)S(1)} %all_to_all.26, bf16[]{:T(256)} %constant.70.clone.1), dimensions={0}, to_apply=%region_7.8 | reduce | flops 524288 | bytes 3145730 | tf_op jit(solution)/shard_map/reduce_sum | solution.py:54
  127.4 4.2 %all-to-all-start.4 = ((bf16[16,128,256]{2,1,0:T(8,128)(2,1)}), bf16[16,128,256]{2,1,0:T(8,128)(2,1)S(1)}, u32[]{:S(2)}, u32[]{:S(2)}) async-start(bf16[16,128,256]{2,1,0:T(8,128)(2,1)} %reduce_sum.43), calls=%async_computation.4 | async-start | bytes 2097152 | tf_op jit(solution)/shard_map/all_to_all | solution.py:61
  131.6 0.8 copy.83
  132.5 28.1 %all-to-all-done.4 = bf16[16,128,256]{2,1,0:T(8,128)(2,1)S(1)} async-done(((bf16[16,128,256]{2,1,0:T(8,128)(2,1)}), bf16[16,128,256]{2,1,0:T(8,128)(2,1)S(1)}, u32[]{:S(2)}, u32[]{:S(2)}) %all-to-all-start.4) | async-done | bytes 1048608 | tf_op jit(solution)/shard_map/all_to_all | solution.py:61
  (80 shorter events, 15.0 us)
Async XLA Ops:
  0.6 8.0 %copy-start.1 = (bf16[128,128]{1,0:T(8,128)(2,1)S(1)}, bf16[128,128]{1,0:T(8,128)(2,1)}, u32[]{:S(2)}) copy-start(bf16[128,128]{1,0:T(8,128)(2,1)} %param.12) | copy-start | bytes 98308
  0.6 8.0 %copy-start.2 = (bf16[128,128]{1,0:T(8,128)(2,1)S(1)}, bf16[128,128]{1,0:T(8,128)(2,1)}, u32[]{:S(2)}) copy-start(bf16[128,128]{1,0:T(8,128)(2,1)} %param.11) | copy-start | bytes 98308
  2.8 20.4 %all-to-all-start.2 = ((bf16[8,128,512]{1,2,0:T(8,128)(2,1)}), bf16[8,128,512]{1,2,0:T(8,128)(2,1)S(1)}, u32[]{:S(2)}, u32[]{:S(2)}) async-start(bf16[8,128,512]{1,2,0:T(8,128)(2,1)} %broadcast_in_dim.59), calls=%async_computation.2 | async-start | bytes 2097152 | tf_op jit(solution)/shard_map/all_to_all | solution.py:21
  8.7 26.6 %copy-start.3 = (s32[64]{0:T(128)S(1)}, s32[64]{0:T(128)}, u32[]{:S(2)}) copy-start(s32[64]{0:T(128)} %param.15) | copy-start | bytes 772
  8.7 26.8 %copy-start = (bf16[128,512]{1,0:T(8,128)(2,1)S(1)}, bf16[128,512]{1,0:T(8,128)(2,1)}, u32[]{:S(2)}) copy-start(bf16[128,512]{1,0:T(8,128)(2,1)} %param.10) | copy-start | bytes 393220
  24.3 38.3 %all-to-all-start = ((bf16[16,128,256]{2,1,0:T(8,128)(2,1)}), bf16[16,128,256]{2,1,0:T(8,128)(2,1)}, u32[]{:S(2)}, u32[]{:S(2)}) async-start(bf16[16,128,256]{2,1,0:T(8,128)(2,1)} %broadcast_in_dim.56), calls=%async_computation | async-start | bytes 2097152 | tf_op jit(solution)/shard_map/all_to_all | solution.py:21
  127.4 33.1 %all-to-all-start.4 = ((bf16[16,128,256]{2,1,0:T(8,128)(2,1)}), bf16[16,128,256]{2,1,0:T(8,128)(2,1)S(1)}, u32[]{:S(2)}, u32[]{:S(2)}) async-start(bf16[16,128,256]{2,1,0:T(8,128)(2,1)} %reduce_sum.43), calls=%async_computation.4 | async-start | bytes 2097152 | tf_op jit(solution)/shard_map/all_to_all | solution.py:61
where the time goes:
time: 163 us; the launch traced here: 161 us
  waiting for transfers between devices  63.4 us (39%)
  matrix products  26.5 us (16%)
  local copies, waits for them, and re-layouts  22.8 us (14%)
  starting transfers between devices  21 us (13%)
  blocking collectives  10.8 us (7%)
  other arithmetic  10.3 us (6%)
  loops' own time  5.65 us (3%)
    all_to_all x2, waiting for transfers between devices, from_everyone(): lax.all_to_all(jnp.broadcast_to(value[None], (peers, *value.shape)), axis...  35.3 us
    all_to_all x1, waiting for transfers between devices, summed_rows(): lax.all_to_all(own.astype(jnp.bfloat16), far, 0, 0, tiled=True)  28.1 us
    all_to_all x2, starting transfers between devices, from_everyone(): lax.all_to_all(jnp.broadcast_to(value[None], (peers, *value.shape)), axis...  16.8 us
    dot_general x8, matrix products, block_scores(): jnp.einsum('qkgd,skd->kgqs', query_block, key_block, preferred_element_ty...  7.61 us
    dynamic_slice x8, local copies, waits for them, and re-layouts, local(): lax.scan(stats_step, start_stats, block_ids)  7.19 us
    le x8, other arithmetic, block_scores(): visible = key_places[None, :] <= query_places[:, None]  6.37 us
    dot_general x4, matrix products, grad_step(): jnp.einsum('kgqs,qkgd->skd', grad_scores, query_heads, preferred_element_...  5.51 us
    all_to_all x1, blocking collectives, sum_at_owner(): lax.all_to_all(in_blocks(value, dim, peers), axis, 0, 0, tiled=True)  5.42 us
  transfers between devices with their start and end apart: 3, of which 3 were waited for; matrix products, arithmetic and copies ran while one was open for 5% of the time, Pallas kernels for 0%

commit v1 on v0

v1 whole, which is shorter than its diff:
```python
import math

import jax
import jax.numpy as jnp
from jax import lax
from jax.experimental import pallas as pl
from jax.experimental.pallas import tpu as pltpu
from jax.sharding import Mesh
from jax.sharding import PartitionSpec as P

HEADS = 32
KV_HEADS = 8
HEAD_DIM = 128
GROUPS = HEADS // KV_HEADS
SPAN = 64
CP = ("yh", "z", "c")
VOCAB = ("yl", "x")
FACTOR = HEAD_DIM**-0.5
SCALE2 = FACTOR * math.log2(math.e)
MASKED = -1e30
CHUNK = 256
VMEM_LIMIT = 48 * 1024 * 1024
NT = (((1,), (1,)), ((), ()))
NN = (((1,), (0,)), ((), ()))


def mm(a, b, dims):
    return lax.dot_general(a, b, dims, preferred_element_type=jnp.float32)


def shift_by(value, axes, steps):
    sizes = [lax.axis_size(a) for a in axes]
    total = math.prod(sizes)
    pairs = []
    for src in range(total):
        rest, at = src, []
        for n in reversed(sizes):
            at.insert(0, rest % n)
            rest //= n
        dst = 0
        for n, i, s in zip(sizes, at, steps):
            dst = dst * n + (i + s) % n
        pairs.append((src, dst))
    return lax.ppermute(value, axes, pairs)


def joined(refs):
    return jnp.concatenate([r[...] for r in refs], axis=0)


def fill_bias(kpos_ref, qpos_ref, bias_ref):
    @pl.when(pl.program_id(0) == 0)
    def _():
        for at in range(0, bias_ref.shape[0], CHUNK):
            rows = pl.ds(at, CHUNK)
            visible = kpos_ref[rows, :] <= qpos_ref[...]
            bias_ref[rows, :] = jnp.where(visible, 0.0, MASKED)


def stats_kernel(kpos, qpos, q0, q1, q2, q3, k, lse_ref, bias, s_scr):
    fill_bias(kpos, qpos, bias)
    q = joined((q0, q1, q2, q3))
    keys = k.shape[0]
    peak = jnp.full((1, q.shape[0]), MASKED, jnp.float32)
    for at in range(0, keys, CHUNK):
        rows = pl.ds(at, CHUNK)
        s = mm(k[rows, :], q, NT) * SCALE2 + bias[rows, :]
        s_scr[rows, :] = s
        peak = jnp.maximum(peak, jnp.max(s, axis=0, keepdims=True))
    total = jnp.zeros_like(peak)
    for at in range(0, keys, CHUNK):
        total = total + jnp.sum(jnp.exp2(s_scr[pl.ds(at, CHUNK), :] - peak), axis=0, keepdims=True)
    lse_ref[0] = peak + jnp.log2(total)


def aligned(own, far, core, both):
    n = own.shape[1] // 4

    def pick(a, order):
        return jnp.concatenate([a[:, g * n : (g + 1) * n] for g in order], axis=1)

    return own, pick(far, (1, 0, 3, 2)), pick(core, (2, 3, 0, 1)), pick(both, (3, 2, 1, 0))


def delta_kernel(
    kpos, qpos, q0, q1, q2, q3, u0, u1, u2, u3, k, v, l0, l1, l2, l3, lse_ref, delta_ref, bias
):
    fill_bias(kpos, qpos, bias)
    q, u = joined((q0, q1, q2, q3)), joined((u0, u1, u2, u3))
    parts = aligned(l0[0], l1[0], l2[0], l3[0])
    peak = jnp.maximum(jnp.maximum(parts[0], parts[1]), jnp.maximum(parts[2], parts[3]))
    lse = peak + jnp.log2(sum(jnp.exp2(p - peak) for p in parts))
    lse_ref[0] = lse
    total = jnp.zeros_like(lse)
    for at in range(0, k.shape[0], CHUNK):
        rows = pl.ds(at, CHUNK)
        w = jnp.exp2(mm(k[rows, :], q, NT) * SCALE2 + bias[rows, :] - lse)
        total = total + jnp.sum(w * mm(v[rows, :], u, NT), axis=0, keepdims=True)
    delta_ref[0] = total


def grad_kernel(
    kpos, qpos, q0, q1, q2, q3, u0, u1, u2, u3, k, v, kt, lse_in, d0, d1, d2, d3,
    own_ref, far_ref, core_ref, both_ref, terms_ref, bias, dk, dv,
):
    fill_bias(kpos, qpos, bias)
    head = pl.program_id(0)
    q, u = joined((q0, q1, q2, q3)), joined((u0, u1, u2, u3))
    lse = lse_in[0]
    delta = sum(aligned(d0[0], d1[0], d2[0], d3[0]))

    @pl.when(head == 0)
    def _():
        dk[...] = jnp.zeros_like(dk)
        dv[...] = jnp.zeros_like(dv)

    dq = jnp.zeros((HEAD_DIM, q.shape[0]), jnp.float32)
    for at in range(0, k.shape[0], CHUNK):
        rows = pl.ds(at, CHUNK)
        w = jnp.exp2(mm(k[rows, :], q, NT) * SCALE2 + bias[rows, :] - lse)
        ds = (w * (mm(v[rows, :], u, NT) - delta)).astype(jnp.bfloat16)
        dv[rows, :] += mm(w.astype(jnp.bfloat16), u, NN)
        dk[rows, :] += mm(ds, q, NN)
        dq = dq + mm(kt[:, at : at + CHUNK], ds, NN)
    dq = (dq * FACTOR).T
    n = own_ref.shape[0]
    own_ref[...] = dq[:n]
    far_ref[...] = dq[n : 2 * n]
    core_ref[...] = dq[2 * n : 3 * n].astype(jnp.bfloat16)
    both_ref[...] = dq[3 * n :].astype(jnp.bfloat16)

    @pl.when(head == pl.num_programs(0) - 1)
    def _():
        terms_ref[:, :HEAD_DIM] = (dk[...] * FACTOR).astype(jnp.bfloat16)
        terms_ref[:, HEAD_DIM:] = dv[...].astype(jnp.bfloat16)


def upstream_kernel(order, *refs):
    parts, w, out, acc = refs[:-3], refs[-3], refs[-2], refs[-1]
    step = pl.program_id(0)
    for i, part in enumerate(parts):

        @pl.when(step == i)
        def _(i=i, part=part):
            term = mm(part[...], w[...], NT)
            if i == 0:
                acc[...] = term
            elif i == len(parts) - 1:
                out[...] = (acc[...] + term).astype(out.dtype)
            else:
                acc[...] += term


def whole(shape):
    return pl.BlockSpec(shape, lambda h: (0,) * len(shape))


def upstream_of(parts, order, o_weight):
    rows, width = parts[0].shape
    cols = o_weight.shape[0]

    def const(shape):
        return pl.BlockSpec(shape, lambda i, o: (0, 0))

    return pl.pallas_call(
        upstream_kernel,
        out_shape=jax.ShapeDtypeStruct((rows, cols), jnp.bfloat16),
        grid_spec=pltpu.PrefetchScalarGridSpec(
            num_scalar_prefetch=1,
            grid=(len(parts),),
            in_specs=[const((rows, width))] * len(parts)
            + [pl.BlockSpec((cols, width), lambda i, o: (0, o[i]))],
            out_specs=const((rows, cols)),
            scratch_shapes=[pltpu.VMEM((rows, cols), jnp.float32)],
        ),
        compiler_params=pltpu.CompilerParams(vmem_limit_bytes=VMEM_LIMIT),
        name="upstream",
    )(order, *parts, o_weight)


def local(queries, key_states, value_states, out_grad, o_weight, span_order):
    rows = queries.shape[0]
    nz = lax.axis_size("z")
    nx = lax.axis_size("x")
    keys = nz * rows
    many = 4 * rows
    f32, bf16 = jnp.float32, jnp.bfloat16
    yh, z, c = lax.axis_index("yh"), lax.axis_index("z"), lax.axis_index("c")
    yl, x = lax.axis_index("yl"), lax.axis_index("x")

    both = jnp.concatenate((key_states, value_states), axis=1)
    kv = lax.all_to_all(
        jnp.broadcast_to(both[None], (nz, *both.shape)), "z", 0, 0, tiled=True
    ).reshape(keys, 2 * HEAD_DIM)
    k_all, v_all = kv[:, :HEAD_DIM], kv[:, HEAD_DIM:]
    kt_all = k_all.T

    parts, sources = [out_grad], [yl * nx + x]
    for steps in ((0, 1), (0, 3), (1, 0), (0, 2), (1, 1), (1, 3), (1, 2)):
        parts.append(shift_by(out_grad, VOCAB, steps))
        sources.append((yl - steps[0]) % 2 * nx + (x - steps[1]) % nx)
    order = jnp.stack(sources).astype(jnp.int32)

    def shared(own):
        far = shift_by(own, ("yh",), (1,))
        return own, far, shift_by(own, ("c",), (1,)), shift_by(far, ("c",), (1,))

    def everyone(own):
        return (
            own,
            shift_by(own, ("yh",), (1,)),
            shift_by(own, ("c",), (1,)),
            shift_by(own, ("yh", "c"), (1, 1)),
        )

    spans = span_order.reshape(2, nz, 2, 2)
    offsets = jnp.arange(SPAN, dtype=jnp.int32)
    key_spans = lax.dynamic_slice(spans, (yh, 0, c, 0), (1, nz, 1, 2)).reshape(2 * nz, 1)
    kpos = (key_spans * SPAN + offsets[None, :]).reshape(keys, 1)
    groups = [(yh, c), (1 - yh, c), (yh, 1 - c), (1 - yh, 1 - c)]
    query_spans = jnp.concatenate(
        [lax.dynamic_slice(spans, (a, z, b, 0), (1, 1, 1, 2)).reshape(2, 1) for a, b in groups]
    )
    qpos = (query_spans * SPAN + offsets[None, :]).reshape(1, many)

    head_block = pl.BlockSpec((rows, HEAD_DIM), lambda h: (0, h))
    row_block = pl.BlockSpec((1, 1, many), lambda h: (h, 0, 0))
    row_shape = jax.ShapeDtypeStruct((GROUPS, 1, many), f32)
    places = [whole((keys, 1)), whole((1, many))]
    key_block = whole((keys, HEAD_DIM))
    bias = pltpu.VMEM((keys, many), f32)
    params = pltpu.CompilerParams(vmem_limit_bytes=VMEM_LIMIT)

    q = shared(queries)
    lse = pl.pallas_call(
        stats_kernel,
        grid=(GROUPS,),
        out_shape=row_shape,
        in_specs=places + [head_block] * 4 + [key_block],
        out_specs=row_block,
        scratch_shapes=[bias, bias],
        compiler_params=params,
        name="row_stats",
    )(kpos, qpos, *q, k_all)
    lse_parts = everyone(lse)

    upstream = upstream_of(parts, order, o_weight)
    u = shared(upstream)
    lse_all, delta = pl.pallas_call(
        delta_kernel,
        grid=(GROUPS,),
        out_shape=(row_shape, row_shape),
        in_specs=places + [head_block] * 8 + [key_block] * 2 + [row_block] * 4,
        out_specs=(row_block, row_block),
        scratch_shapes=[bias],
        compiler_params=params,
        name="row_delta",
    )(kpos, qpos, *q, *u, k_all, v_all, *lse_parts)
    delta_parts = everyone(delta)

    wide = (rows, GROUPS * HEAD_DIM)
    own, far, core, across, terms = pl.pallas_call(
        grad_kernel,
        grid=(GROUPS,),
        out_shape=(
            jax.ShapeDtypeStruct(wide, f32),
            jax.ShapeDtypeStruct(wide, f32),
            jax.ShapeDtypeStruct(wide, bf16),
            jax.ShapeDtypeStruct(wide, bf16),
            jax.ShapeDtypeStruct((keys, 2 * HEAD_DIM), bf16),
        ),
        in_specs=places
        + [head_block] * 8
        + [key_block] * 2
        + [whole((HEAD_DIM, keys))]
        + [row_block] * 5,
        out_specs=(head_block,) * 4 + (whole((keys, 2 * HEAD_DIM)),),
        scratch_shapes=[bias, pltpu.VMEM((keys, HEAD_DIM), f32), pltpu.VMEM((keys, HEAD_DIM), f32)],
        compiler_params=params,
        name="gradients",
    )(kpos, qpos, *q, *u, k_all, v_all, kt_all, lse_all, *delta_parts)

    summed = lax.all_to_all(terms.reshape(nz, rows, 2 * HEAD_DIM), "z", 0, 0, tiled=True)
    summed = jnp.sum(summed.astype(f32), axis=0)
    own = own + shift_by(core, ("c",), (1,)).astype(f32)
    far = far + shift_by(across, ("c",), (1,)).astype(f32)
    query_grad = own + shift_by(far.astype(bf16), ("yh",), (1,)).astype(f32)
    return query_grad, summed[:, :HEAD_DIM], summed[:, HEAD_DIM:]


def solution(mesh):
    finer = Mesh(mesh.devices.reshape(2, 8, 2, 2, 4), CP + VOCAB)
    return jax.shard_map(
        local,
        mesh=finer,
        in_specs=(P(CP, VOCAB), P(CP, VOCAB), P(CP, VOCAB), P(CP, VOCAB), P(VOCAB, None), P()),
        out_specs=(P(CP, VOCAB), P(CP, VOCAB), P(CP, VOCAB)),
        check_vma=False,
    )
```

time: 163 us -> 98.9 us (0.61)
  waiting for transfers between devices: 63.4 us -> 23.7 us
  matrix products: 26.5 us -> 0 us
  starting transfers between devices: 21 us -> 45.1 us
  Pallas kernels: 0 us -> 18.8 us
  local copies, waits for them, and re-layouts: 22.8 us -> 6.72 us
  blocking collectives: 10.8 us -> 0 us
  other arithmetic: 10.3 us -> 1.87 us
  loops' own time: 5.65 us -> 0 us
    all_to_all x3 -> x2, waiting for transfers between devices: 63.4 us -> 7.26 us  [the longest x1 7.25 us: local(): lax.all_to_all(terms.reshape(nz, rows, 2 * HEAD_DIM), 'z', 0, 0, tiled=True)]
    ppermute x0 -> x22, starting transfers between devices: none -> 29.5 us  [shift_by(): return lax.ppermute(value, axes, pairs)]
    dot_general x29 -> x0, matrix products: 26.5 us -> none  [the longest x8 7.61 us: block_scores(): jnp.einsum('qkgd,skd->kgqs', query_block, key_block, preferred_element_ty...]
    pallas_call x0 -> x4, Pallas kernels: none -> 18.8 us  [the longest x1 8.05 us: local(): pl.pallas_call(grad_kernel, grid=(GROUPS,), out_shape=(jax.ShapeDtypeStru...]
    ppermute x0 -> x22, waiting for transfers between devices: none -> 16.4 us  [shift_by(): return lax.ppermute(value, axes, pairs)]
    all_to_all x2 -> x0, blocking collectives: 10.8 us -> none  [the longest x1 5.42 us: sum_at_owner(): lax.all_to_all(in_blocks(value, dim, peers), axis, 0, 0, tiled=True)]
    dynamic_slice x17 -> x0, local copies, waits for them, and re-layouts: 7.84 us -> none  [the longest x8 7.19 us: local(): lax.scan(stats_step, start_stats, block_ids)]
    le x8 -> x0, other arithmetic: 6.37 us -> none  [block_scores(): visible = key_places[None, :] <= query_places[:, None]]
  transfers between devices with their start and end apart: 3 -> 24, of which waited for: 3 -> 9; matrix products, arithmetic and copies ran while one was open for 5% -> 3% of each run, Pallas kernels for 0% -> 7%
where the time goes in v1:
time: 98.9 us; the launch traced here: 97.1 us
  starting transfers between devices  45.1 us (46%)
  waiting for transfers between devices  23.7 us (24%)
  Pallas kernels  18.8 us (19%)
  local copies, waits for them, and re-layouts  6.72 us (7%)
  other arithmetic  1.87 us (2%)
    ppermute x22, starting transfers between devices, shift_by(): return lax.ppermute(value, axes, pairs)  29.5 us
    ppermute x22, waiting for transfers between devices, shift_by(): return lax.ppermute(value, axes, pairs)  16.4 us
    all_to_all x1, starting transfers between devices, local(): lax.all_to_all(jnp.broadcast_to(both[None], (nz, *both.shape)), 'z', 0, 0...  8.47 us
    pallas_call x1, Pallas kernels, local(): pl.pallas_call(grad_kernel, grid=(GROUPS,), out_shape=(jax.ShapeDtypeStru...  8.05 us
    all_to_all x1, waiting for transfers between devices, local(): lax.all_to_all(terms.reshape(nz, rows, 2 * HEAD_DIM), 'z', 0, 0, tiled=True)  7.25 us
    all_to_all x1, starting transfers between devices, local(): lax.all_to_all(terms.reshape(nz, rows, 2 * HEAD_DIM), 'z', 0, 0, tiled=True)  7.22 us
    pallas_call x1, Pallas kernels, upstream_of(): pl.pallas_call(upstream_kernel, out_shape=jax.ShapeDtypeStruct((rows, col...  3.7 us
    pallas_call x1, Pallas kernels, local(): pl.pallas_call(stats_kernel, grid=(GROUPS,), out_shape=row_shape, in_spec...  3.54 us
  transfers between devices with their start and end apart: 24, of which 9 were waited for; matrix products, arithmetic and copies ran while one was open for 3% of the time, Pallas kernels for 7%

profile of v1, /device:TPU:2, one launch (start us, length us, event | category | flops | bytes accessed | tf_op | source)
XLA Modules:
  0.0 97.1 jit_solution(4166507406740592093)
XLA Ops:
  0.6 0.8 pad_maximum_fusion
  1.4 0.1 copy.24
  1.5 0.9 broadcast_in_dim.2
  2.4 8.5 %all-to-all-start = ((bf16[8,128,256]{1,2,0:T(8,128)(2,1)}), bf16[8,128,256]{1,2,0:T(8,128)(2,1)S(1)}, u32[]{:S(2)}, u32[]{:S(2)}) async-start(bf16[8,128,256]{1,2,0:T(8,128)(2,1)} %broadcast_in_dim.2), calls=%async_computation | async-start | bytes 1048576 | tf_op jit(solution)/shard_map/all_to_all | solution.py:192
  10.9 1.5 %collective-permute-start.8 = (bf16[128,512]{1,0:T(8,128)(2,1)}, bf16[128,512]{1,0:T(8,128)(2,1)S(1)}, u32[]{:S(2)}, u32[]{:S(2)}) collective-permute-start(bf16[128,512]{1,0:T(8,128)(2,1)} %refs_0_.1), channel_id=1, source_target_pairs={{0,7},{1,4},{2,5},{3,6},{4,3},{5,0},{6,1},{7,2},{8,15},{9,12},{10,... | collective-permute-start | bytes 393224 | tf_op jit(solution)/shard_map/ppermute | solution.py:44
  12.4 1.4 %collective-permute-start.7 = (bf16[128,512]{1,0:T(8,128)(2,1)}, bf16[128,512]{1,0:T(8,128)(2,1)S(1)}, u32[]{:S(2)}, u32[]{:S(2)}) collective-permute-start(bf16[128,512]{1,0:T(8,128)(2,1)} %refs_0_.1), channel_id=1, source_target_pairs={{0,5},{1,6},{2,7},{3,4},{4,1},{5,2},{6,3},{7,0},{8,13},{9,14},{10,... | collective-permute-start | bytes 393224 | tf_op jit(solution)/shard_map/ppermute | solution.py:44
  13.8 3.3 %collective-permute-start.6 = (bf16[128,512]{1,0:T(8,128)(2,1)}, bf16[128,512]{1,0:T(8,128)(2,1)S(1)}, u32[]{:S(2)}, u32[]{:S(2)}) collective-permute-start(bf16[128,512]{1,0:T(8,128)(2,1)} %refs_0_.1), channel_id=1, source_target_pairs={{0,2},{1,3},{2,0},{3,1},{4,6},{5,7},{6,4},{7,5},{8,10},{9,11},{10,... | collective-permute-start | bytes 393224 | tf_op jit(solution)/shard_map/ppermute | solution.py:44
  17.1 1.6 %collective-permute-start.5 = (bf16[128,512]{1,0:T(8,128)(2,1)}, bf16[128,512]{1,0:T(8,128)(2,1)S(1)}, u32[]{:S(2)}, u32[]{:S(2)}) collective-permute-start(bf16[128,512]{1,0:T(8,128)(2,1)} %refs_0_.1), channel_id=1, source_target_pairs={{0,4},{1,5},{2,6},{3,7},{4,0},{5,1},{6,2},{7,3},{8,12},{9,13},{10,... | collective-permute-start | bytes 393224 | tf_op jit(solution)/shard_map/ppermute | solution.py:44
  18.7 0.2 collective-permute-start.4
  18.9 0.8 reshape.118
  19.9 0.1 mul.34
  20.0 1.8 %collective-permute-start.3 = (bf16[128,512]{1,0:T(8,128)(2,1)}, bf16[128,512]{1,0:T(8,128)(2,1)S(1)}, u32[]{:S(2)}, u32[]{:S(2)}) collective-permute-start(bf16[128,512]{1,0:T(8,128)(2,1)} %refs_0_.1), channel_id=1, source_target_pairs={{0,1},{1,2},{2,3},{3,0},{4,5},{5,6},{6,7},{7,4},{8,9},{9,10},{10,1... | collective-permute-start | bytes 393224 | tf_op jit(solution)/shard_map/ppermute | solution.py:44
  21.9 1.6 %collective-permute-start.9 = (bf16[128,512]{1,0:T(8,128)(2,1)}, bf16[128,512]{1,0:T(8,128)(2,1)S(1)}, u32[]{:S(2)}, u32[]{:S(2)}) collective-permute-start(bf16[128,512]{1,0:T(8,128)(2,1)} %refs_0_.1), channel_id=1, source_target_pairs={{0,6},{1,7},{2,4},{3,5},{4,2},{5,3},{6,0},{7,1},{8,14},{9,15},{10,... | collective-permute-start | bytes 393224 | tf_op jit(solution)/shard_map/ppermute | solution.py:44
  23.5 0.1 add.148.qpos
  23.6 0.1 stack.35.order
  23.7 0.1 collective-permute-start.1
  23.8 3.3 %collective-permute-start = (bf16[128,512]{1,0:T(8,128)(2,1)}, bf16[128,512]{1,0:T(8,128)(2,1)S(1)}, u32[]{:S(2)}, u32[]{:S(2)}) collective-permute-start(bf16[128,512]{1,0:T(8,128)(2,1)} %q0.5), channel_id=1, source_target_pairs={{0,128},{128,0},{1,129},{129,1},{2,130},{130,2},{3,131},{131,3},{4... | collective-permute-start | bytes 393224 | tf_op jit(solution)/shard_map/ppermute | solution.py:44
  27.1 2.4 %collective-permute-done.9.refs_7_ = bf16[128,512]{1,0:T(8,128)(2,1)S(1)} collective-permute-done((bf16[128,512]{1,0:T(8,128)(2,1)}, bf16[128,512]{1,0:T(8,128)(2,1)S(1)}, u32[]{:S(2)}, u32[]{:S(2)}) %collective-permute-start.9) | collective-permute-done | bytes 131104 | tf_op jit(solution)/shard_map/ppermute | solution.py:44
  29.5 2.2 %copy-done = bf16[512,4096]{1,0:T(8,128)(2,1)S(1)} copy-done((bf16[512,4096]{1,0:T(8,128)(2,1)S(1)}, bf16[512,4096]{1,0:T(8,128)(2,1)}, u32[]{:S(2)}) %copy-start) | copy-done | bytes 4194328
  31.7 0.9 copy-done.2
  32.6 3.7 %upstream.1.u0 = bf16[128,512]{1,0:T(8,128)(2,1)S(1)} custom-call(s32[8]{0:T(128)S(1)} %stack.35.order, bf16[128,512]{1,0:T(8,128)(2,1)S(1)} %copy-done.2, bf16[128,512]{1,0:T(8,128)(2,1)S(1)} %collective-permute-done.3.refs_1_, bf16[128,512]{1,0:T(8,128)(2,1)S(1)} %collective-permute-done.4.refs_2_, bf16[128,512]{1,0:T(8,128)(2,1)S(1)} %collective-permute-done.5.refs_3_, ...), custom_call_target="tpu_custom_call" | custom-call | tf_op jit(solution)/shard_map/upstream/pallas_call | solution.py:165
  36.3 3.0 %collective-permute-start.10 = (bf16[128,512]{1,0:T(8,128)(2,1)S(1)}, bf16[128,512]{1,0:T(8,128)(2,1)S(1)}, u32[]{:S(2)}, u32[]{:S(2)}) collective-permute-start(bf16[128,512]{1,0:T(8,128)(2,1)S(1)} %upstream.1.u0), channel_id=1, source_target_pairs={{0,128},{128,0},{1,129},{129,1},{2,130},{130,2},{3,131},{131,3},{4... | collective-permute-start | bytes 393224 | tf_op jit(solution)/shard_map/ppermute | solution.py:44
  39.4 0.5 add.166.kpos
  39.9 0.1 collective-permute-start.11
  40.0 0.5 collective-permute-start.2
  40.5 2.4 %collective-permute-done.10.u1 = bf16[128,512]{1,0:T(8,128)(2,1)S(1)} collective-permute-done((bf16[128,512]{1,0:T(8,128)(2,1)S(1)}, bf16[128,512]{1,0:T(8,128)(2,1)S(1)}, u32[]{:S(2)}, u32[]{:S(2)}) %collective-permute-start.10) | collective-permute-done | bytes 131104 | tf_op jit(solution)/shard_map/ppermute | solution.py:44
  43.0 0.2 copy.32.k
  43.2 3.5 %row_stats.1.l0 = f32[4,1,512]{2,1,0:T(1,128)S(1)} custom-call(s32[1024,1]{1,0:T(8,128)S(1)} %add.166.kpos, s32[1,512]{1,0:T(1,128)S(1)} %add.148.qpos, bf16[128,512]{1,0:T(8,128)(2,1)S(1)} %copy-done.1, bf16[128,512]{1,0:T(8,128)(2,1)S(1)} %collective-permute-done.q1, bf16[128,512]{1,0:T(8,128)(2,1)S(1)} %collective-permute-done.1.q2, ...), custom_call_target="tpu_custom_call" | custom-call | tf_op jit(solution)/shard_map/row_stats/pallas_call | solution.py:235
  46.8 3.1 %collective-permute-start.15 = (f32[4,1,512]{2,1,0:T(1,128)S(1)}, f32[4,1,512]{2,1,0:T(1,128)S(1)}, u32[]{:S(2)}, u32[]{:S(2)}) collective-permute-start(f32[4,1,512]{2,1,0:T(1,128)S(1)} %row_stats.1.l0), channel_id=1, source_target_pairs={{0,136},{8,128},{128,8},{136,0},{1,137},{9,129},{129,9},{137,1},{2... | collective-permute-start | bytes 24584 | tf_op jit(solution)/shard_map/ppermute | solution.py:44
  49.9 0.7 collective-permute-start.13
  50.6 0.2 copy.33.v
  50.8 0.7 collective-permute-done.15.l3
  51.4 3.6 %collective-permute-done.13.l1 = f32[4,1,512]{2,1,0:T(1,128)S(1)} collective-permute-done((f32[4,1,512]{2,1,0:T(1,128)S(1)}, f32[4,1,512]{2,1,0:T(1,128)S(1)}, u32[]{:S(2)}, u32[]{:S(2)}) %collective-permute-start.13) | collective-permute-done | bytes 8224 | tf_op jit(solution)/shard_map/ppermute | solution.py:44
  55.1 3.5 %row_delta.1 = (f32[4,1,512]{2,1,0:T(1,128)S(1)}, f32[4,1,512]{2,1,0:T(1,128)S(1)}) custom-call(s32[1024,1]{1,0:T(8,128)S(1)} %add.166.kpos, s32[1,512]{1,0:T(1,128)S(1)} %add.148.qpos, bf16[128,512]{1,0:T(8,128)(2,1)S(1)} %copy-done.1, bf16[128,512]{1,0:T(8,128)(2,1)S(1)} %collective-permute-done.q1, bf16[128,512]{1,0:T(8,128)(2,1)S(1)} %collective-permute-done.1.q2, ...), custom_call_target="tpu_custom_call" | custom-call | tf_op jit(solution)/shard_map/row_delta/pallas_call | solution.py:249
  58.6 0.1 collective-permute-start.18
  58.7 0.8 collective-permute-start.17
  59.5 2.9 %collective-permute-start.16 = (f32[4,1,512]{2,1,0:T(1,128)S(1)}, f32[4,1,512]{2,1,0:T(1,128)S(1)}, u32[]{:S(2)}, u32[]{:S(2)}) collective-permute-start(f32[4,1,512]{2,1,0:T(1,128)S(1)} %get-tuple-element.11.d0), channel_id=1, source_target_pairs={{0,128},{128,0},{1,129},{129,1},{2,130},{130,2},{3,131},{131,3},{4... | collective-permute-start | bytes 24584 | tf_op jit(solution)/shard_map/ppermute | solution.py:44
  62.3 0.9 collective-permute-done.18.d3
  63.3 1.4 %collective-permute-done.16.d1 = f32[4,1,512]{2,1,0:T(1,128)S(1)} collective-permute-done((f32[4,1,512]{2,1,0:T(1,128)S(1)}, f32[4,1,512]{2,1,0:T(1,128)S(1)}, u32[]{:S(2)}, u32[]{:S(2)}) %collective-permute-start.16) | collective-permute-done | bytes 8224 | tf_op jit(solution)/shard_map/ppermute | solution.py:44
  64.6 8.0 %gradients.1 = (f32[128,512]{1,0:T(8,128)S(1)}, f32[128,512]{1,0:T(8,128)S(1)}, bf16[128,512]{1,0:T(8,128)(2,1)S(1)}, bf16[128,512]{1,0:T(8,128)(2,1)S(1)}, bf16[1024,256]{1,0:T(8,128)(2,1)}) custom-call(s32[1024,1]{1,0:T(8,128)S(1)} %add.166.kpos, s32[1,512]{1,0:T(1,128)S(1)} %add.148.qpos, bf16[128,512]{1,0:T(8,128)(2,1)S(1)} %copy-done.1, ...), custom_call_target="tpu_custom_call" | custom-call | tf_op jit(solution)/shard_map/gradients/pallas_call | solution.py:262
  72.7 7.2 %all-to-all-start.1 = ((bf16[8,128,256]{2,1,0:T(8,128)(2,1)}), bf16[8,128,256]{2,1,0:T(8,128)(2,1)S(1)}, u32[]{:S(2)}, u32[]{:S(2)}) async-start(bf16[8,128,256]{2,1,0:T(8,128)(2,1)} %bitcast.13), calls=%async_computation.1 | async-start | bytes 1048576 | tf_op jit(solution)/shard_map/all_to_all | solution.py:283
  79.9 0.5 collective-permute-start.19
  80.4 0.8 collective-permute-done.20
  81.3 2.9 %collective-permute-start.21 = (bf16[128,512]{1,0:T(8,128)(2,1)S(1)}, bf16[128,512]{1,0:T(8,128)(2,1)S(1)}, u32[]{:S(2)}, u32[]{:S(2)}) collective-permute-start(bf16[128,512]{1,0:T(8,128)(2,1)S(1)} %add_convert_fusion), channel_id=1, source_target_pairs={{0,128},{128,0},{1,129},{129,1},{2,130},{130,2},{3,131},{131,3},{4... | collective-permute-start | bytes 393224 | tf_op jit(solution)/shard_map/ppermute | solution.py:44
  84.2 4.2 %collective-permute-done.21 = bf16[128,512]{1,0:T(8,128)(2,1)S(1)} collective-permute-done((bf16[128,512]{1,0:T(8,128)(2,1)S(1)}, bf16[128,512]{1,0:T(8,128)(2,1)S(1)}, u32[]{:S(2)}, u32[]{:S(2)}) %collective-permute-start.21) | collective-permute-done | bytes 131104 | tf_op jit(solution)/shard_map/ppermute | solution.py:44
  88.4 0.7 convert_add_fusion
  89.2 7.3 %all-to-all-done.1 = bf16[8,128,256]{2,1,0:T(8,128)(2,1)S(1)} async-done(((bf16[8,128,256]{2,1,0:T(8,128)(2,1)}), bf16[8,128,256]{2,1,0:T(8,128)(2,1)S(1)}, u32[]{:S(2)}, u32[]{:S(2)}) %all-to-all-start.1) | async-done | bytes 524320 | tf_op jit(solution)/shard_map/all_to_all | solution.py:283
  96.5 0.7 fusion.4
  (31 shorter events, 0.6 us)
Async XLA Ops:
  2.4 40.4 %all-to-all-start = ((bf16[8,128,256]{1,2,0:T(8,128)(2,1)}), bf16[8,128,256]{1,2,0:T(8,128)(2,1)S(1)}, u32[]{:S(2)}, u32[]{:S(2)}) async-start(bf16[8,128,256]{1,2,0:T(8,128)(2,1)} %broadcast_in_dim.2), calls=%async_computation | async-start | bytes 1048576 | tf_op jit(solution)/shard_map/all_to_all | solution.py:192
  10.9 9.1 %collective-permute-start.8 = (bf16[128,512]{1,0:T(8,128)(2,1)}, bf16[128,512]{1,0:T(8,128)(2,1)S(1)}, u32[]{:S(2)}, u32[]{:S(2)}) collective-permute-start(bf16[128,512]{1,0:T(8,128)(2,1)} %refs_0_.1), channel_id=1, source_target_pairs={{0,7},{1,4},{2,5},{3,6},{4,3},{5,0},{6,1},{7,2},{8,15},{9,12},{10,... | collective-permute-start | bytes 393224 | tf_op jit(solution)/shard_map/ppermute | solution.py:44
  12.4 9.4 %collective-permute-start.7 = (bf16[128,512]{1,0:T(8,128)(2,1)}, bf16[128,512]{1,0:T(8,128)(2,1)S(1)}, u32[]{:S(2)}, u32[]{:S(2)}) collective-permute-start(bf16[128,512]{1,0:T(8,128)(2,1)} %refs_0_.1), channel_id=1, source_target_pairs={{0,5},{1,6},{2,7},{3,4},{4,1},{5,2},{6,3},{7,0},{8,13},{9,14},{10,... | collective-permute-start | bytes 393224 | tf_op jit(solution)/shard_map/ppermute | solution.py:44
  13.8 9.9 %collective-permute-start.6 = (bf16[128,512]{1,0:T(8,128)(2,1)}, bf16[128,512]{1,0:T(8,128)(2,1)S(1)}, u32[]{:S(2)}, u32[]{:S(2)}) collective-permute-start(bf16[128,512]{1,0:T(8,128)(2,1)} %refs_0_.1), channel_id=1, source_target_pairs={{0,2},{1,3},{2,0},{3,1},{4,6},{5,7},{6,4},{7,5},{8,10},{9,11},{10,... | collective-permute-start | bytes 393224 | tf_op jit(solution)/shard_map/ppermute | solution.py:44
  17.1 6.6 %collective-permute-start.5 = (bf16[128,512]{1,0:T(8,128)(2,1)}, bf16[128,512]{1,0:T(8,128)(2,1)S(1)}, u32[]{:S(2)}, u32[]{:S(2)}) collective-permute-start(bf16[128,512]{1,0:T(8,128)(2,1)} %refs_0_.1), channel_id=1, source_target_pairs={{0,4},{1,5},{2,6},{3,7},{4,0},{5,1},{6,2},{7,3},{8,12},{9,13},{10,... | collective-permute-start | bytes 393224 | tf_op jit(solution)/shard_map/ppermute | solution.py:44
  18.7 8.4 %collective-permute-start.4 = (bf16[128,512]{1,0:T(8,128)(2,1)}, bf16[128,512]{1,0:T(8,128)(2,1)S(1)}, u32[]{:S(2)}, u32[]{:S(2)}) collective-permute-start(bf16[128,512]{1,0:T(8,128)(2,1)} %refs_0_.1), channel_id=1, source_target_pairs={{0,3},{1,0},{2,1},{3,2},{4,7},{5,4},{6,5},{7,6},{8,11},{9,8},{10,9... | collective-permute-start | bytes 393224 | tf_op jit(solution)/shard_map/ppermute | solution.py:44
  20.0 7.1 %collective-permute-start.3 = (bf16[128,512]{1,0:T(8,128)(2,1)}, bf16[128,512]{1,0:T(8,128)(2,1)S(1)}, u32[]{:S(2)}, u32[]{:S(2)}) collective-permute-start(bf16[128,512]{1,0:T(8,128)(2,1)} %refs_0_.1), channel_id=1, source_target_pairs={{0,1},{1,2},{2,3},{3,0},{4,5},{5,6},{6,7},{7,4},{8,9},{9,10},{10,1... | collective-permute-start | bytes 393224 | tf_op jit(solution)/shard_map/ppermute | solution.py:44
  21.9 7.6 %collective-permute-start.9 = (bf16[128,512]{1,0:T(8,128)(2,1)}, bf16[128,512]{1,0:T(8,128)(2,1)S(1)}, u32[]{:S(2)}, u32[]{:S(2)}) collective-permute-start(bf16[128,512]{1,0:T(8,128)(2,1)} %refs_0_.1), channel_id=1, source_target_pairs={{0,6},{1,7},{2,4},{3,5},{4,2},{5,3},{6,0},{7,1},{8,14},{9,15},{10,... | collective-permute-start | bytes 393224 | tf_op jit(solution)/shard_map/ppermute | solution.py:44
  23.7 19.5 %collective-permute-start.1 = (bf16[128,512]{1,0:T(8,128)(2,1)}, bf16[128,512]{1,0:T(8,128)(2,1)S(1)}, u32[]{:S(2)}, u32[]{:S(2)}) collective-permute-start(bf16[128,512]{1,0:T(8,128)(2,1)} %q0.5), channel_id=1, source_target_pairs={{0,8},{8,0},{1,9},{9,1},{2,10},{10,2},{3,11},{11,3},{4,12},{12,4},... | collective-permute-start | bytes 393224 | tf_op jit(solution)/shard_map/ppermute | solution.py:44
  23.8 16.2 %collective-permute-start = (bf16[128,512]{1,0:T(8,128)(2,1)}, bf16[128,512]{1,0:T(8,128)(2,1)S(1)}, u32[]{:S(2)}, u32[]{:S(2)}) collective-permute-start(bf16[128,512]{1,0:T(8,128)(2,1)} %q0.5), channel_id=1, source_target_pairs={{0,128},{128,0},{1,129},{129,1},{2,130},{130,2},{3,131},{131,3},{4... | collective-permute-start | bytes 393224 | tf_op jit(solution)/shard_map/ppermute | solution.py:44
  29.5 2.2 %copy-start = (bf16[512,4096]{1,0:T(8,128)(2,1)S(1)}, bf16[512,4096]{1,0:T(8,128)(2,1)}, u32[]{:S(2)}) copy-start(bf16[512,4096]{1,0:T(8,128)(2,1)} %refs_8_.1) | copy-start | bytes 12582916
  31.7 0.9 copy-start.2
  32.6 10.6 %copy-start.1 = (bf16[128,512]{1,0:T(8,128)(2,1)S(1)}, bf16[128,512]{1,0:T(8,128)(2,1)}, u32[]{:S(2)}) copy-start(bf16[128,512]{1,0:T(8,128)(2,1)} %q0.5) | copy-start | bytes 393220
  36.3 6.6 %collective-permute-start.10 = (bf16[128,512]{1,0:T(8,128)(2,1)S(1)}, bf16[128,512]{1,0:T(8,128)(2,1)S(1)}, u32[]{:S(2)}, u32[]{:S(2)}) collective-permute-start(bf16[128,512]{1,0:T(8,128)(2,1)S(1)} %upstream.1.u0), channel_id=1, source_target_pairs={{0,128},{128,0},{1,129},{129,1},{2,130},{130,2},{3,131},{131,3},{4... | collective-permute-start | bytes 393224 | tf_op jit(solution)/shard_map/ppermute | solution.py:44
  39.9 10.9 %collective-permute-start.11 = (bf16[128,512]{1,0:T(8,128)(2,1)S(1)}, bf16[128,512]{1,0:T(8,128)(2,1)S(1)}, u32[]{:S(2)}, u32[]{:S(2)}) collective-permute-start(bf16[128,512]{1,0:T(8,128)(2,1)S(1)} %upstream.1.u0), channel_id=1, source_target_pairs={{0,8},{8,0},{1,9},{9,1},{2,10},{10,2},{3,11},{11,3},{4,12},{12,4},... | collective-permute-start | bytes 393224 | tf_op jit(solution)/shard_map/ppermute | solution.py:44
  40.0 3.2 %collective-permute-start.2 = (bf16[128,512]{1,0:T(8,128)(2,1)S(1)}, bf16[128,512]{1,0:T(8,128)(2,1)S(1)}, u32[]{:S(2)}, u32[]{:S(2)}) collective-permute-start(bf16[128,512]{1,0:T(8,128)(2,1)S(1)} %collective-permute-done.q1), channel_id=1, source_target_pairs={{0,8},{8,0},{1,9},{9,1},{2,10},{10,2},{3,11},{11,3},{4,12},{12,4},... | collective-permute-start | bytes 393224 | tf_op jit(solution)/shard_map/ppermute | solution.py:44
  42.8 7.9 %collective-permute-start.12 = (bf16[128,512]{1,0:T(8,128)(2,1)S(1)}, bf16[128,512]{1,0:T(8,128)(2,1)S(1)}, u32[]{:S(2)}, u32[]{:S(2)}) collective-permute-start(bf16[128,512]{1,0:T(8,128)(2,1)S(1)} %collective-permute-done.10.u1), channel_id=1, source_target_pairs={{0,8},{8,0},{1,9},{9,1},{2,10},{10,2},{3,11},{11,3},{4,12},{12,4},... | collective-permute-start | bytes 393224 | tf_op jit(solution)/shard_map/ppermute | solution.py:44
  46.8 4.7 %collective-permute-start.15 = (f32[4,1,512]{2,1,0:T(1,128)S(1)}, f32[4,1,512]{2,1,0:T(1,128)S(1)}, u32[]{:S(2)}, u32[]{:S(2)}) collective-permute-start(f32[4,1,512]{2,1,0:T(1,128)S(1)} %row_stats.1.l0), channel_id=1, source_target_pairs={{0,136},{8,128},{128,8},{136,0},{1,137},{9,129},{129,9},{137,1},{2... | collective-permute-start | bytes 24584 | tf_op jit(solution)/shard_map/ppermute | solution.py:44
  49.9 1.5 %collective-permute-start.14 = (f32[4,1,512]{2,1,0:T(1,128)S(1)}, f32[4,1,512]{2,1,0:T(1,128)S(1)}, u32[]{:S(2)}, u32[]{:S(2)}) collective-permute-start(f32[4,1,512]{2,1,0:T(1,128)S(1)} %row_stats.1.l0), channel_id=1, source_target_pairs={{0,8},{8,0},{1,9},{9,1},{2,10},{10,2},{3,11},{11,3},{4,12},{12,4},... | collective-permute-start | bytes 24584 | tf_op jit(solution)/shard_map/ppermute | solution.py:44
  49.9 5.2 %collective-permute-start.13 = (f32[4,1,512]{2,1,0:T(1,128)S(1)}, f32[4,1,512]{2,1,0:T(1,128)S(1)}, u32[]{:S(2)}, u32[]{:S(2)}) collective-permute-start(f32[4,1,512]{2,1,0:T(1,128)S(1)} %row_stats.1.l0), channel_id=1, source_target_pairs={{0,128},{128,0},{1,129},{129,1},{2,130},{130,2},{3,131},{131,3},{4... | collective-permute-start | bytes 24584 | tf_op jit(solution)/shard_map/ppermute | solution.py:44
  58.6 4.7 %collective-permute-start.18 = (f32[4,1,512]{2,1,0:T(1,128)S(1)}, f32[4,1,512]{2,1,0:T(1,128)S(1)}, u32[]{:S(2)}, u32[]{:S(2)}) collective-permute-start(f32[4,1,512]{2,1,0:T(1,128)S(1)} %get-tuple-element.11.d0), channel_id=1, source_target_pairs={{0,136},{8,128},{128,8},{136,0},{1,137},{9,129},{129,9},{137,1},{2... | collective-permute-start | bytes 24584 | tf_op jit(solution)/shard_map/ppermute | solution.py:44
  58.7 4.6 %collective-permute-start.17 = (f32[4,1,512]{2,1,0:T(1,128)S(1)}, f32[4,1,512]{2,1,0:T(1,128)S(1)}, u32[]{:S(2)}, u32[]{:S(2)}) collective-permute-start(f32[4,1,512]{2,1,0:T(1,128)S(1)} %get-tuple-element.11.d0), channel_id=1, source_target_pairs={{0,8},{8,0},{1,9},{9,1},{2,10},{10,2},{3,11},{11,3},{4,12},{12,4},... | collective-permute-start | bytes 24584 | tf_op jit(solution)/shard_map/ppermute | solution.py:44
  59.5 5.2 %collective-permute-start.16 = (f32[4,1,512]{2,1,0:T(1,128)S(1)}, f32[4,1,512]{2,1,0:T(1,128)S(1)}, u32[]{:S(2)}, u32[]{:S(2)}) collective-permute-start(f32[4,1,512]{2,1,0:T(1,128)S(1)} %get-tuple-element.11.d0), channel_id=1, source_target_pairs={{0,128},{128,0},{1,129},{129,1},{2,130},{130,2},{3,131},{131,3},{4... | collective-permute-start | bytes 24584 | tf_op jit(solution)/shard_map/ppermute | solution.py:44
  72.7 23.7 %all-to-all-start.1 = ((bf16[8,128,256]{2,1,0:T(8,128)(2,1)}), bf16[8,128,256]{2,1,0:T(8,128)(2,1)S(1)}, u32[]{:S(2)}, u32[]{:S(2)}) async-start(bf16[8,128,256]{2,1,0:T(8,128)(2,1)} %bitcast.13), calls=%async_computation.1 | async-start | bytes 1048576 | tf_op jit(solution)/shard_map/all_to_all | solution.py:283
  79.9 1.3 %collective-permute-start.20 = (bf16[128,512]{1,0:T(8,128)(2,1)S(1)}, bf16[128,512]{1,0:T(8,128)(2,1)S(1)}, u32[]{:S(2)}, u32[]{:S(2)}) collective-permute-start(bf16[128,512]{1,0:T(8,128)(2,1)S(1)} %get-tuple-element.15), channel_id=1, source_target_pairs={{0,8},{8,0},{1,9},{9,1},{2,10},{10,2},{3,11},{11,3},{4,12},{12,4},... | collective-permute-start | bytes 393224 | tf_op jit(solution)/shard_map/ppermute | solution.py:44
  79.9 4.3 %collective-permute-start.19 = (bf16[128,512]{1,0:T(8,128)(2,1)S(1)}, bf16[128,512]{1,0:T(8,128)(2,1)S(1)}, u32[]{:S(2)}, u32[]{:S(2)}) collective-permute-start(bf16[128,512]{1,0:T(8,128)(2,1)S(1)} %get-tuple-element.13), channel_id=1, source_target_pairs={{0,8},{8,0},{1,9},{9,1},{2,10},{10,2},{3,11},{11,3},{4,12},{12,4},... | collective-permute-start | bytes 393224 | tf_op jit(solution)/shard_map/ppermute | solution.py:44
  81.3 7.1 %collective-permute-start.21 = (bf16[128,512]{1,0:T(8,128)(2,1)S(1)}, bf16[128,512]{1,0:T(8,128)(2,1)S(1)}, u32[]{:S(2)}, u32[]{:S(2)}) collective-permute-start(bf16[128,512]{1,0:T(8,128)(2,1)S(1)} %add_convert_fusion), channel_id=1, source_target_pairs={{0,128},{128,0},{1,129},{129,1},{2,130},{130,2},{3,131},{131,3},{4... | collective-permute-start | bytes 393224 | tf_op jit(solution)/shard_map/ppermute | solution.py:44

commit v2 on v1

--- a/solution.py
+++ b/solution.py
@@ -19,7 +19,8 @@
 SCALE2 = FACTOR * math.log2(math.e)
 MASKED = -1e30
 CHUNK = 256
-VMEM_LIMIT = 48 * 1024 * 1024
+EXTRA = 16
+VMEM_LIMIT = 32 * 1024 * 1024
 NT = (((1,), (1,)), ((), ()))
 NN = (((1,), (0,)), ((), ()))
 
@@ -82,12 +83,19 @@
     return own, pick(far, (1, 0, 3, 2)), pick(core, (2, 3, 0, 1)), pick(both, (3, 2, 1, 0))
 
 
+def whole_row(ref, head):
+    at = 3 * head
+    parts = ref[...].astype(jnp.float32)
+    row = lax.broadcasted_iota(jnp.int32, parts.shape, 0)
+    return jnp.sum(jnp.where((row >= at) & (row < at + 3), parts, 0.0), axis=0, keepdims=True)
+
+
 def delta_kernel(
     kpos, qpos, q0, q1, q2, q3, u0, u1, u2, u3, k, v, l0, l1, l2, l3, lse_ref, delta_ref, bias
 ):
     fill_bias(kpos, qpos, bias)
     q, u = joined((q0, q1, q2, q3)), joined((u0, u1, u2, u3))
-    parts = aligned(l0[0], l1[0], l2[0], l3[0])
+    parts = aligned(*(whole_row(r, pl.program_id(0)) for r in (l0, l1, l2, l3)))
     peak = jnp.maximum(jnp.maximum(parts[0], parts[1]), jnp.maximum(parts[2], parts[3]))
     lse = peak + jnp.log2(sum(jnp.exp2(p - peak) for p in parts))
     lse_ref[0] = lse
@@ -100,8 +108,8 @@
 
 
 def grad_kernel(
-    kpos, qpos, q0, q1, q2, q3, u0, u1, u2, u3, k, v, kt, lse_in, d0, d1, d2, d3,
-    own_ref, far_ref, core_ref, both_ref, terms_ref, bias, dk, dv,
+    kpos, qpos, q0, q1, q2, q3, u0, u1, u2, u3, k, v, lse_in, d0, d1, d2, d3,
+    own_ref, far_ref, core_ref, both_ref, terms_ref, bias, dk, dv, kt,
 ):
     fill_bias(kpos, qpos, bias)
     head = pl.program_id(0)
@@ -113,6 +121,7 @@
     def _():
         dk[...] = jnp.zeros_like(dk)
         dv[...] = jnp.zeros_like(dv)
+        kt[...] = k[...].T
 
     dq = jnp.zeros((HEAD_DIM, q.shape[0]), jnp.float32)
     for at in range(0, k.shape[0], CHUNK):
@@ -135,47 +144,60 @@
         terms_ref[:, HEAD_DIM:] = dv[...].astype(jnp.bfloat16)
 
 
+def split3(value):
+    high = value.astype(jnp.bfloat16)
+    rest = value - high.astype(jnp.float32)
+    mid = rest.astype(jnp.bfloat16)
+    low = (rest - mid.astype(jnp.float32)).astype(jnp.bfloat16)
+    return high, mid, low
+
+
 def upstream_kernel(order, *refs):
-    parts, w, out, acc = refs[:-3], refs[-3], refs[-2], refs[-1]
-    step = pl.program_id(0)
-    for i, part in enumerate(parts):
-
-        @pl.when(step == i)
-        def _(i=i, part=part):
-            term = mm(part[...], w[...], NT)
-            if i == 0:
-                acc[...] = term
-            elif i == len(parts) - 1:
-                out[...] = (acc[...] + term).astype(out.dtype)
-            else:
-                acc[...] += term
+    parts, lse, w_hbm, out, w, sems = refs[:-5], *refs[-5:]
+    width = parts[0].shape[1]
+    copies = []
+    for i in range(order.shape[0]):
+        at = pl.multiple_of(order[i] * width, width)
+        copies.append(pltpu.make_async_copy(w_hbm.at[:, pl.ds(at, width)], w.at[i], sems.at[i]))
+        copies[-1].start()
+    rows = out.shape[0] - EXTRA
+    pieces = [piece for h in range(GROUPS) for piece in split3(lse[h])]
+    pieces.append(jnp.zeros((EXTRA - len(pieces), out.shape[1]), jnp.bfloat16))
+    out[rows:, :] = jnp.concatenate(pieces, axis=0)
+    total, i = None, 0
+    for part in parts:
+        for at in range(0, part.shape[0], rows):
+            copies[i].wait()
+            term = mm(part[at : at + rows, :], w[i], NT)
+            total = term if total is None else total + term
+            i += 1
+    out[:rows, :] = total.astype(out.dtype)
 
 
 def whole(shape):
     return pl.BlockSpec(shape, lambda h: (0,) * len(shape))
 
 
-def upstream_of(parts, order, o_weight):
-    rows, width = parts[0].shape
+def upstream_of(parts, order, lse, o_weight):
+    width = parts[0].shape[1]
     cols = o_weight.shape[0]
-
-    def const(shape):
-        return pl.BlockSpec(shape, lambda i, o: (0, 0))
-
+    count = order.shape[0]
+    rows = sum(p.shape[0] for p in parts) // count
+    vmem = pl.BlockSpec(memory_space=pltpu.VMEM)
     return pl.pallas_call(
         upstream_kernel,
-        out_shape=jax.ShapeDtypeStruct((rows, cols), jnp.bfloat16),
-        grid_spec=pltpu.PrefetchScalarGridSpec(
-            num_scalar_prefetch=1,
-            grid=(len(parts),),
-            in_specs=[const((rows, width))] * len(parts)
-            + [pl.BlockSpec((cols, width), lambda i, o: (0, o[i]))],
-            out_specs=const((rows, cols)),
-            scratch_shapes=[pltpu.VMEM((rows, cols), jnp.float32)],
-        ),
+        out_shape=jax.ShapeDtypeStruct((rows + EXTRA, cols), jnp.bfloat16),
+        in_specs=[pl.BlockSpec(memory_space=pltpu.SMEM)]
+        + [vmem] * (len(parts) + 1)
+        + [pl.BlockSpec(memory_space=pltpu.HBM)],
+        out_specs=vmem,
+        scratch_shapes=[
+            pltpu.VMEM((count, cols, width), jnp.bfloat16),
+            pltpu.SemaphoreType.DMA((count,)),
+        ],
         compiler_params=pltpu.CompilerParams(vmem_limit_bytes=VMEM_LIMIT),
         name="upstream",
-    )(order, *parts, o_weight)
+    )(order, *parts, lse, pltpu.with_memory_space_constraint(o_weight, pltpu.HBM))
 
 
 def local(queries, key_states, value_states, out_grad, o_weight, span_order):
@@ -192,13 +214,13 @@
     kv = lax.all_to_all(
         jnp.broadcast_to(both[None], (nz, *both.shape)), "z", 0, 0, tiled=True
     ).reshape(keys, 2 * HEAD_DIM)
-    k_all, v_all = kv[:, :HEAD_DIM], kv[:, HEAD_DIM:]
-    kt_all = k_all.T
-
-    parts, sources = [out_grad], [yl * nx + x]
-    for steps in ((0, 1), (0, 3), (1, 0), (0, 2), (1, 1), (1, 3), (1, 2)):
-        parts.append(shift_by(out_grad, VOCAB, steps))
-        sources.append((yl - steps[0]) % 2 * nx + (x - steps[1]) % nx)
+
+    pair = jnp.concatenate((out_grad, shift_by(out_grad, ("yl",), (1,))), axis=0)
+    parts, sources = [], []
+    for step in (0, 1, 3, 2):
+        parts.append(shift_by(pair, ("x",), (step,)) if step else pair)
+        near = (x - step) % nx
+        sources += [yl * nx + near, (1 - yl) * nx + near]
     order = jnp.stack(sources).astype(jnp.int32)
 
     def shared(own):
@@ -227,7 +249,10 @@
     row_block = pl.BlockSpec((1, 1, many), lambda h: (h, 0, 0))
     row_shape = jax.ShapeDtypeStruct((GROUPS, 1, many), f32)
     places = [whole((keys, 1)), whole((1, many))]
-    key_block = whole((keys, HEAD_DIM))
+    key_block = pl.BlockSpec((keys, HEAD_DIM), lambda h: (0, 0))
+    value_block = pl.BlockSpec((keys, HEAD_DIM), lambda h: (0, 1))
+    extra_block = pl.BlockSpec((EXTRA, many), lambda h: (rows // EXTRA, 0))
+    term_sum = pltpu.VMEM((keys, HEAD_DIM), f32)
     bias = pltpu.VMEM((keys, many), f32)
     params = pltpu.CompilerParams(vmem_limit_bytes=VMEM_LIMIT)
 
@@ -241,21 +266,20 @@
         scratch_shapes=[bias, bias],
         compiler_params=params,
         name="row_stats",
-    )(kpos, qpos, *q, k_all)
-    lse_parts = everyone(lse)
-
-    upstream = upstream_of(parts, order, o_weight)
+    )(kpos, qpos, *q, kv)
+
+    upstream = upstream_of(parts, order, lse, o_weight)
     u = shared(upstream)
     lse_all, delta = pl.pallas_call(
         delta_kernel,
         grid=(GROUPS,),
         out_shape=(row_shape, row_shape),
-        in_specs=places + [head_block] * 8 + [key_block] * 2 + [row_block] * 4,
+        in_specs=places + [head_block] * 8 + [key_block, value_block] + [extra_block] * 4,
         out_specs=(row_block, row_block),
         scratch_shapes=[bias],
         compiler_params=params,
         name="row_delta",
-    )(kpos, qpos, *q, *u, k_all, v_all, *lse_parts)
+    )(kpos, qpos, *q, *u, kv, kv, *u)
     delta_parts = everyone(delta)
 
     wide = (rows, GROUPS * HEAD_DIM)
@@ -271,14 +295,13 @@
         ),
         in_specs=places
         + [head_block] * 8
-        + [key_block] * 2
-        + [whole((HEAD_DIM, keys))]
+        + [key_block, value_block]
         + [row_block] * 5,
         out_specs=(head_block,) * 4 + (whole((keys, 2 * HEAD_DIM)),),
-        scratch_shapes=[bias, pltpu.VMEM((keys, HEAD_DIM), f32), pltpu.VMEM((keys, HEAD_DIM), f32)],
+        scratch_shapes=[bias, term_sum, term_sum, pltpu.VMEM((HEAD_DIM, keys), bf16)],
         compiler_params=params,
         name="gradients",
-    )(kpos, qpos, *q, *u, k_all, v_all, kt_all, lse_all, *delta_parts)
+    )(kpos, qpos, *q, *u, kv, kv, lse_all, *delta_parts)
 
     summed = lax.all_to_all(terms.reshape(nz, rows, 2 * HEAD_DIM), "z", 0, 0, tiled=True)
     summed = jnp.sum(summed.astype(f32), axis=0)

time: 98.9 us -> 92.9 us (0.939); the launches traced: 97.1 us -> 92.5 us
  starting transfers between devices: 45.1 us -> 31.8 us
  waiting for transfers between devices: 23.7 us -> 34.2 us
  local copies, waits for them, and re-layouts: 6.72 us -> 4.82 us
    ppermute x22 -> x16, starting transfers between devices: 29.5 us -> 16.3 us  [shift_by(): return lax.ppermute(value, axes, pairs)]
    ppermute x22 -> x16, waiting for transfers between devices: 16.4 us -> 26.1 us  [shift_by(): return lax.ppermute(value, axes, pairs)]
    unnamed x6 -> x5, local copies, waits for them, and re-layouts: 3.1 us -> 1.82 us
  transfers between devices with their start and end apart: 24 -> 18, of which waited for: 9 -> 12; matrix products, arithmetic and copies ran while one was open for 3% -> 4% of each run, Pallas kernels for 7% -> 4%
where the time goes in v2:
time: 92.9 us; the launch traced here: 92.5 us
  waiting for transfers between devices  34.2 us (37%)
  starting transfers between devices  31.8 us (34%)
  Pallas kernels  19 us (20%)
  local copies, waits for them, and re-layouts  4.82 us (5%)
  other arithmetic  1.87 us (2%)
    ppermute x16, waiting for transfers between devices, shift_by(): return lax.ppermute(value, axes, pairs)  26.1 us
    ppermute x16, starting transfers between devices, shift_by(): return lax.ppermute(value, axes, pairs)  16.3 us
    all_to_all x1, starting transfers between devices, local(): lax.all_to_all(jnp.broadcast_to(both[None], (nz, *both.shape)), 'z', 0, 0...  8.47 us
    pallas_call x1, Pallas kernels, local(): pl.pallas_call(grad_kernel, grid=(GROUPS,), out_shape=(jax.ShapeDtypeStru...  8.25 us
    all_to_all x1, waiting for transfers between devices, local(): lax.all_to_all(terms.reshape(nz, rows, 2 * HEAD_DIM), 'z', 0, 0, tiled=True)  7.4 us
    all_to_all x1, starting transfers between devices, local(): lax.all_to_all(terms.reshape(nz, rows, 2 * HEAD_DIM), 'z', 0, 0, tiled=True)  7.11 us
    pallas_call x1, Pallas kernels, local(): pl.pallas_call(delta_kernel, grid=(GROUPS,), out_shape=(row_shape, row_sh...  3.67 us
    pallas_call x1, Pallas kernels, local(): pl.pallas_call(stats_kernel, grid=(GROUPS,), out_shape=row_shape, in_spec...  3.6 us
  transfers between devices with their start and end apart: 18, of which 12 were waited for; matrix products, arithmetic and copies ran while one was open for 4% of the time, Pallas kernels for 4%

profile of v2, /device:TPU:2, one launch (start us, length us, event | category | flops | bytes accessed | tf_op | source)
XLA Modules:
  0.0 92.5 jit_solution(15671026271297111267)
XLA Ops:
  0.6 0.8 pad_maximum_fusion
  1.4 0.8 broadcast_in_dim.2
  2.2 8.5 %all-to-all-start = ((bf16[8,128,256]{2,1,0:T(8,128)(2,1)}), bf16[8,128,256]{2,1,0:T(8,128)(2,1)S(1)}, u32[]{:S(2)}, u32[]{:S(2)}) async-start(bf16[8,128,256]{2,1,0:T(8,128)(2,1)} %broadcast_in_dim.2), calls=%async_computation | async-start | bytes 1048576 | tf_op jit(solution)/shard_map/all_to_all | solution.py:214
  10.7 0.1 collective-permute-start.1
  10.8 3.3 %collective-permute-start = (bf16[128,512]{1,0:T(8,128)(2,1)}, bf16[128,512]{1,0:T(8,128)(2,1)S(1)}, u32[]{:S(2)}, u32[]{:S(2)}) collective-permute-start(bf16[128,512]{1,0:T(8,128)(2,1)} %q0.5), channel_id=1, source_target_pairs={{0,128},{128,0},{1,129},{129,1},{2,130},{130,2},{3,131},{131,3},{4... | collective-permute-start | bytes 393224 | tf_op jit(solution)/shard_map/ppermute | solution.py:45
  14.1 0.7 collective-permute-start.3
  14.8 0.8 reshape.118
  15.6 0.1 add_multiply_fusion
  15.7 0.9 constant_dynamic-update-slice_fusion.1
  16.6 5.0 %collective-permute-done.3 = bf16[128,512]{1,0:T(8,128)(2,1)S(1)} collective-permute-done((bf16[128,512]{1,0:T(8,128)(2,1)}, bf16[128,512]{1,0:T(8,128)(2,1)S(1)}, u32[]{:S(2)}, u32[]{:S(2)}) %collective-permute-start.3) | collective-permute-done | bytes 131104 | tf_op jit(solution)/shard_map/ppermute | solution.py:45
  21.6 2.2 %collective-permute-start.6 = (bf16[256,512]{1,0:T(8,128)(2,1)S(1)}, bf16[256,512]{1,0:T(8,128)(2,1)S(1)}, u32[]{:S(2)}, u32[]{:S(2)}) collective-permute-start(bf16[256,512]{1,0:T(8,128)(2,1)S(1)} %constant_dynamic-update-slice_fusion.refs_0_), channel_id=1, source_target_pairs={{0,2},{1,3},{2,0},{3,1},{4,6},{5,7},{6,4},{7,5},{8,10},{9,11},{10,... | collective-permute-start | bytes 786440 | tf_op jit(solution)/shard_map/ppermute | solution.py:45
  23.8 1.4 %collective-permute-start.5 = (bf16[256,512]{1,0:T(8,128)(2,1)S(1)}, bf16[256,512]{1,0:T(8,128)(2,1)S(1)}, u32[]{:S(2)}, u32[]{:S(2)}) collective-permute-start(bf16[256,512]{1,0:T(8,128)(2,1)S(1)} %constant_dynamic-update-slice_fusion.refs_0_), channel_id=1, source_target_pairs={{0,3},{1,0},{2,1},{3,2},{4,7},{5,4},{6,5},{7,6},{8,11},{9,8},{10,9... | collective-permute-start | bytes 786440 | tf_op jit(solution)/shard_map/ppermute | solution.py:45
  25.3 0.6 collective-permute-start.4
  25.8 0.1 iota_add_fusion.1
  25.9 0.1 mul.32
  26.0 0.1 add.133.qpos
  26.1 0.0 collective-permute-start.2
  26.1 0.1 iota_add_fusion
  26.2 0.5 add.149.kpos
  26.7 0.1 stack.35.order
  26.8 0.0 collective-permute-done.1.q2
  26.8 0.7 collective-permute-done.2.q3
  27.5 0.7 all-to-all-done
  28.2 0.9 copy-done
  29.1 3.6 %row_stats.1.refs_4_ = f32[4,1,512]{2,1,0:T(1,128)S(1)} custom-call(s32[1024,1]{1,0:T(8,128)S(1)} %add.149.kpos, s32[1,512]{1,0:T(1,128)S(1)} %add.133.qpos, bf16[128,512]{1,0:T(8,128)(2,1)S(1)} %copy-done, bf16[128,512]{1,0:T(8,128)(2,1)S(1)} %collective-permute-done.q1, bf16[128,512]{1,0:T(8,128)(2,1)S(1)} %collective-permute-done.1.q2, ...), custom_call_target="tpu_custom_call" | custom-call | tf_op jit(solution)/shard_map/row_stats/pallas_call | solution.py:260
  32.7 3.9 %collective-permute-done.5.refs_2_ = bf16[256,512]{1,0:T(8,128)(2,1)S(1)} collective-permute-done((bf16[256,512]{1,0:T(8,128)(2,1)S(1)}, bf16[256,512]{1,0:T(8,128)(2,1)S(1)}, u32[]{:S(2)}, u32[]{:S(2)}) %collective-permute-start.5) | collective-permute-done | bytes 262176 | tf_op jit(solution)/shard_map/ppermute | solution.py:45
  36.7 0.1 collective-permute-done.4.refs_1_
  36.7 3.5 %upstream.1.u0.l0 = bf16[144,512]{1,0:T(8,128)(2,1)S(1)} custom-call(s32[8]{0:T(128)S(1)} %stack.35.order, bf16[256,512]{1,0:T(8,128)(2,1)S(1)} %constant_dynamic-update-slice_fusion.refs_0_, bf16[256,512]{1,0:T(8,128)(2,1)S(1)} %collective-permute-done.4.refs_1_, bf16[256,512]{1,0:T(8,128)(2,1)S(1)} %collective-permute-done.5.refs_2_, ...), custom_call_target="tpu_custom_call" | custom-call | tf_op jit(solution)/shard_map/upstream/pallas_call | solution.py:187
  40.3 1.9 %collective-permute-start.7 = (bf16[144,512]{1,0:T(8,128)(2,1)S(1)}, bf16[144,512]{1,0:T(8,128)(2,1)S(1)}, u32[]{:S(2)}, u32[]{:S(2)}) collective-permute-start(bf16[144,512]{1,0:T(8,128)(2,1)S(1)} %upstream.1.u0.l0), channel_id=1, source_target_pairs={{0,128},{128,0},{1,129},{129,1},{2,130},{130,2},{3,131},{131,3},{4... | collective-permute-start | bytes 442376 | tf_op jit(solution)/shard_map/ppermute | solution.py:45
  42.2 0.0 collective-permute-start.8
  42.2 5.4 %collective-permute-done.7.u1.l1 = bf16[144,512]{1,0:T(8,128)(2,1)S(1)} collective-permute-done((bf16[144,512]{1,0:T(8,128)(2,1)S(1)}, bf16[144,512]{1,0:T(8,128)(2,1)S(1)}, u32[]{:S(2)}, u32[]{:S(2)}) %collective-permute-start.7) | collective-permute-done | bytes 147488 | tf_op jit(solution)/shard_map/ppermute | solution.py:45
  47.6 1.4 %collective-permute-done.9.u3.l3 = bf16[144,512]{1,0:T(8,128)(2,1)S(1)} collective-permute-done((bf16[144,512]{1,0:T(8,128)(2,1)S(1)}, bf16[144,512]{1,0:T(8,128)(2,1)S(1)}, u32[]{:S(2)}, u32[]{:S(2)}) %collective-permute-start.9) | collective-permute-done | bytes 147488 | tf_op jit(solution)/shard_map/ppermute | solution.py:45
  48.9 3.7 %row_delta.1 = (f32[4,1,512]{2,1,0:T(1,128)S(1)}, f32[4,1,512]{2,1,0:T(1,128)S(1)}) custom-call(s32[1024,1]{1,0:T(8,128)S(1)} %add.149.kpos, s32[1,512]{1,0:T(1,128)S(1)} %add.133.qpos, bf16[128,512]{1,0:T(8,128)(2,1)S(1)} %copy-done.1, bf16[128,512]{1,0:T(8,128)(2,1)S(1)} %collective-permute-done.q1, bf16[128,512]{1,0:T(8,128)(2,1)S(1)} %collective-permute-done.1.q2, ...), custom_call_target="tpu_custom_call" | custom-call | tf_op jit(solution)/shard_map/row_delta/pallas_call | solution.py:273
  52.6 1.7 %collective-permute-start.12 = (f32[4,1,512]{2,1,0:T(1,128)S(1)}, f32[4,1,512]{2,1,0:T(1,128)S(1)}, u32[]{:S(2)}, u32[]{:S(2)}) collective-permute-start(f32[4,1,512]{2,1,0:T(1,128)S(1)} %get-tuple-element.11.d0), channel_id=1, source_target_pairs={{0,136},{8,128},{128,8},{136,0},{1,137},{9,129},{129,9},{137,1},{2... | collective-permute-start | bytes 24584 | tf_op jit(solution)/shard_map/ppermute | solution.py:45
  54.3 0.4 collective-permute-start.11
  54.6 1.7 %collective-permute-start.10 = (f32[4,1,512]{2,1,0:T(1,128)S(1)}, f32[4,1,512]{2,1,0:T(1,128)S(1)}, u32[]{:S(2)}, u32[]{:S(2)}) collective-permute-start(f32[4,1,512]{2,1,0:T(1,128)S(1)} %get-tuple-element.11.d0), channel_id=1, source_target_pairs={{0,128},{128,0},{1,129},{129,1},{2,130},{130,2},{3,131},{131,3},{4... | collective-permute-start | bytes 24584 | tf_op jit(solution)/shard_map/ppermute | solution.py:45
  56.3 0.9 %collective-permute-done.12.d3 = f32[4,1,512]{2,1,0:T(1,128)S(1)} collective-permute-done((f32[4,1,512]{2,1,0:T(1,128)S(1)}, f32[4,1,512]{2,1,0:T(1,128)S(1)}, u32[]{:S(2)}, u32[]{:S(2)}) %collective-permute-start.12) | collective-permute-done | bytes 8224 | tf_op jit(solution)/shard_map/ppermute | solution.py:45
  57.3 2.5 %collective-permute-done.10.d1 = f32[4,1,512]{2,1,0:T(1,128)S(1)} collective-permute-done((f32[4,1,512]{2,1,0:T(1,128)S(1)}, f32[4,1,512]{2,1,0:T(1,128)S(1)}, u32[]{:S(2)}, u32[]{:S(2)}) %collective-permute-start.10) | collective-permute-done | bytes 8224 | tf_op jit(solution)/shard_map/ppermute | solution.py:45
  59.8 8.2 %gradients.1 = (f32[128,512]{1,0:T(8,128)S(1)}, f32[128,512]{1,0:T(8,128)S(1)}, bf16[128,512]{1,0:T(8,128)(2,1)S(1)}, bf16[128,512]{1,0:T(8,128)(2,1)S(1)}, bf16[1024,256]{1,0:T(8,128)(2,1)}) custom-call(s32[1024,1]{1,0:T(8,128)S(1)} %add.149.kpos, s32[1,512]{1,0:T(1,128)S(1)} %add.133.qpos, bf16[128,512]{1,0:T(8,128)(2,1)S(1)} %copy-done.1, ...), custom_call_target="tpu_custom_call" | custom-call | tf_op jit(solution)/shard_map/gradients/pallas_call | solution.py:286
  68.0 7.1 %all-to-all-start.1 = ((bf16[8,128,256]{2,1,0:T(8,128)(2,1)}), bf16[8,128,256]{2,1,0:T(8,128)(2,1)S(1)}, u32[]{:S(2)}, u32[]{:S(2)}) async-start(bf16[8,128,256]{2,1,0:T(8,128)(2,1)} %bitcast.13), calls=%async_computation.1 | async-start | bytes 1048576 | tf_op jit(solution)/shard_map/all_to_all | solution.py:306
  75.2 0.5 collective-permute-start.13
  75.7 0.8 collective-permute-done.14
  76.5 1.8 %collective-permute-start.15 = (bf16[128,512]{1,0:T(8,128)(2,1)S(1)}, bf16[128,512]{1,0:T(8,128)(2,1)S(1)}, u32[]{:S(2)}, u32[]{:S(2)}) collective-permute-start(bf16[128,512]{1,0:T(8,128)(2,1)S(1)} %add_convert_fusion), channel_id=1, source_target_pairs={{0,128},{128,0},{1,129},{129,1},{2,130},{130,2},{3,131},{131,3},{4... | collective-permute-start | bytes 393224 | tf_op jit(solution)/shard_map/ppermute | solution.py:45
  78.3 5.4 %collective-permute-done.15 = bf16[128,512]{1,0:T(8,128)(2,1)S(1)} collective-permute-done((bf16[128,512]{1,0:T(8,128)(2,1)S(1)}, bf16[128,512]{1,0:T(8,128)(2,1)S(1)}, u32[]{:S(2)}, u32[]{:S(2)}) %collective-permute-start.15) | collective-permute-done | bytes 131104 | tf_op jit(solution)/shard_map/ppermute | solution.py:45
  83.7 0.7 convert_add_fusion
  84.4 7.4 %all-to-all-done.1 = bf16[8,128,256]{2,1,0:T(8,128)(2,1)S(1)} async-done(((bf16[8,128,256]{2,1,0:T(8,128)(2,1)}), bf16[8,128,256]{2,1,0:T(8,128)(2,1)S(1)}, u32[]{:S(2)}, u32[]{:S(2)}) %all-to-all-start.1) | async-done | bytes 524320 | tf_op jit(solution)/shard_map/all_to_all | solution.py:306
  91.8 0.1 convert_reduce_fusion
  91.9 0.7 fusion.4
  (14 shorter events, 0.1 us)
Async XLA Ops:
  2.2 26.0 %all-to-all-start = ((bf16[8,128,256]{2,1,0:T(8,128)(2,1)}), bf16[8,128,256]{2,1,0:T(8,128)(2,1)S(1)}, u32[]{:S(2)}, u32[]{:S(2)}) async-start(bf16[8,128,256]{2,1,0:T(8,128)(2,1)} %broadcast_in_dim.2), calls=%async_computation | async-start | bytes 1048576 | tf_op jit(solution)/shard_map/all_to_all | solution.py:214
  10.7 38.2 %copy-start.1 = (bf16[128,512]{1,0:T(8,128)(2,1)S(1)}, bf16[128,512]{1,0:T(8,128)(2,1)}, u32[]{:S(2)}) copy-start(bf16[128,512]{1,0:T(8,128)(2,1)} %q0.5) | copy-start | bytes 393220
  10.7 16.1 %collective-permute-start.1 = (bf16[128,512]{1,0:T(8,128)(2,1)}, bf16[128,512]{1,0:T(8,128)(2,1)S(1)}, u32[]{:S(2)}, u32[]{:S(2)}) collective-permute-start(bf16[128,512]{1,0:T(8,128)(2,1)} %q0.5), channel_id=1, source_target_pairs={{0,8},{8,0},{1,9},{9,1},{2,10},{10,2},{3,11},{11,3},{4,12},{12,4},... | collective-permute-start | bytes 393224 | tf_op jit(solution)/shard_map/ppermute | solution.py:45
  10.8 15.3 %collective-permute-start = (bf16[128,512]{1,0:T(8,128)(2,1)}, bf16[128,512]{1,0:T(8,128)(2,1)S(1)}, u32[]{:S(2)}, u32[]{:S(2)}) collective-permute-start(bf16[128,512]{1,0:T(8,128)(2,1)} %q0.5), channel_id=1, source_target_pairs={{0,128},{128,0},{1,129},{129,1},{2,130},{130,2},{3,131},{131,3},{4... | collective-permute-start | bytes 393224 | tf_op jit(solution)/shard_map/ppermute | solution.py:45
  14.1 7.5 %collective-permute-start.3 = (bf16[128,512]{1,0:T(8,128)(2,1)}, bf16[128,512]{1,0:T(8,128)(2,1)S(1)}, u32[]{:S(2)}, u32[]{:S(2)}) collective-permute-start(bf16[128,512]{1,0:T(8,128)(2,1)} %param.9), channel_id=1, source_target_pairs={{0,4},{4,0},{1,5},{5,1},{2,6},{6,2},{3,7},{7,3},{8,12},{12,8},{9,1... | collective-permute-start | bytes 393224 | tf_op jit(solution)/shard_map/ppermute | solution.py:45
  21.6 11.1 %collective-permute-start.6 = (bf16[256,512]{1,0:T(8,128)(2,1)S(1)}, bf16[256,512]{1,0:T(8,128)(2,1)S(1)}, u32[]{:S(2)}, u32[]{:S(2)}) collective-permute-start(bf16[256,512]{1,0:T(8,128)(2,1)S(1)} %constant_dynamic-update-slice_fusion.refs_0_), channel_id=1, source_target_pairs={{0,2},{1,3},{2,0},{3,1},{4,6},{5,7},{6,4},{7,5},{8,10},{9,11},{10,... | collective-permute-start | bytes 786440 | tf_op jit(solution)/shard_map/ppermute | solution.py:45
  23.8 12.8 %collective-permute-start.5 = (bf16[256,512]{1,0:T(8,128)(2,1)S(1)}, bf16[256,512]{1,0:T(8,128)(2,1)S(1)}, u32[]{:S(2)}, u32[]{:S(2)}) collective-permute-start(bf16[256,512]{1,0:T(8,128)(2,1)S(1)} %constant_dynamic-update-slice_fusion.refs_0_), channel_id=1, source_target_pairs={{0,3},{1,0},{2,1},{3,2},{4,7},{5,4},{6,5},{7,6},{8,11},{9,8},{10,9... | collective-permute-start | bytes 786440 | tf_op jit(solution)/shard_map/ppermute | solution.py:45
  25.3 11.5 %collective-permute-start.4 = (bf16[256,512]{1,0:T(8,128)(2,1)S(1)}, bf16[256,512]{1,0:T(8,128)(2,1)S(1)}, u32[]{:S(2)}, u32[]{:S(2)}) collective-permute-start(bf16[256,512]{1,0:T(8,128)(2,1)S(1)} %constant_dynamic-update-slice_fusion.refs_0_), channel_id=1, source_target_pairs={{0,1},{1,2},{2,3},{3,0},{4,5},{5,6},{6,7},{7,4},{8,9},{9,10},{10,1... | collective-permute-start | bytes 786440 | tf_op jit(solution)/shard_map/ppermute | solution.py:45
  26.1 1.4 %collective-permute-start.2 = (bf16[128,512]{1,0:T(8,128)(2,1)S(1)}, bf16[128,512]{1,0:T(8,128)(2,1)S(1)}, u32[]{:S(2)}, u32[]{:S(2)}) collective-permute-start(bf16[128,512]{1,0:T(8,128)(2,1)S(1)} %collective-permute-done.q1), channel_id=1, source_target_pairs={{0,8},{8,0},{1,9},{9,1},{2,10},{10,2},{3,11},{11,3},{4,12},{12,4},... | collective-permute-start | bytes 393224 | tf_op jit(solution)/shard_map/ppermute | solution.py:45
  28.2 0.9 copy-start
  40.3 7.3 %collective-permute-start.7 = (bf16[144,512]{1,0:T(8,128)(2,1)S(1)}, bf16[144,512]{1,0:T(8,128)(2,1)S(1)}, u32[]{:S(2)}, u32[]{:S(2)}) collective-permute-start(bf16[144,512]{1,0:T(8,128)(2,1)S(1)} %upstream.1.u0.l0), channel_id=1, source_target_pairs={{0,128},{128,0},{1,129},{129,1},{2,130},{130,2},{3,131},{131,3},{4... | collective-permute-start | bytes 442376 | tf_op jit(solution)/shard_map/ppermute | solution.py:45
  42.2 5.4 %collective-permute-start.8 = (bf16[144,512]{1,0:T(8,128)(2,1)S(1)}, bf16[144,512]{1,0:T(8,128)(2,1)S(1)}, u32[]{:S(2)}, u32[]{:S(2)}) collective-permute-start(bf16[144,512]{1,0:T(8,128)(2,1)S(1)} %upstream.1.u0.l0), channel_id=1, source_target_pairs={{0,8},{8,0},{1,9},{9,1},{2,10},{10,2},{3,11},{11,3},{4,12},{12,4},... | collective-permute-start | bytes 442376 | tf_op jit(solution)/shard_map/ppermute | solution.py:45
  47.5 1.4 %collective-permute-start.9 = (bf16[144,512]{1,0:T(8,128)(2,1)S(1)}, bf16[144,512]{1,0:T(8,128)(2,1)S(1)}, u32[]{:S(2)}, u32[]{:S(2)}) collective-permute-start(bf16[144,512]{1,0:T(8,128)(2,1)S(1)} %collective-permute-done.7.u1.l1), channel_id=1, source_target_pairs={{0,8},{8,0},{1,9},{9,1},{2,10},{10,2},{3,11},{11,3},{4,12},{12,4},... | collective-permute-start | bytes 442376 | tf_op jit(solution)/shard_map/ppermute | solution.py:45
  52.6 4.7 %collective-permute-start.12 = (f32[4,1,512]{2,1,0:T(1,128)S(1)}, f32[4,1,512]{2,1,0:T(1,128)S(1)}, u32[]{:S(2)}, u32[]{:S(2)}) collective-permute-start(f32[4,1,512]{2,1,0:T(1,128)S(1)} %get-tuple-element.11.d0), channel_id=1, source_target_pairs={{0,136},{8,128},{128,8},{136,0},{1,137},{9,129},{129,9},{137,1},{2... | collective-permute-start | bytes 24584 | tf_op jit(solution)/shard_map/ppermute | solution.py:45
  54.3 3.0 %collective-permute-start.11 = (f32[4,1,512]{2,1,0:T(1,128)S(1)}, f32[4,1,512]{2,1,0:T(1,128)S(1)}, u32[]{:S(2)}, u32[]{:S(2)}) collective-permute-start(f32[4,1,512]{2,1,0:T(1,128)S(1)} %get-tuple-element.11.d0), channel_id=1, source_target_pairs={{0,8},{8,0},{1,9},{9,1},{2,10},{10,2},{3,11},{11,3},{4,12},{12,4},... | collective-permute-start | bytes 24584 | tf_op jit(solution)/shard_map/ppermute | solution.py:45
  54.6 5.2 %collective-permute-start.10 = (f32[4,1,512]{2,1,0:T(1,128)S(1)}, f32[4,1,512]{2,1,0:T(1,128)S(1)}, u32[]{:S(2)}, u32[]{:S(2)}) collective-permute-start(f32[4,1,512]{2,1,0:T(1,128)S(1)} %get-tuple-element.11.d0), channel_id=1, source_target_pairs={{0,128},{128,0},{1,129},{129,1},{2,130},{130,2},{3,131},{131,3},{4... | collective-permute-start | bytes 24584 | tf_op jit(solution)/shard_map/ppermute | solution.py:45
  68.0 23.8 %all-to-all-start.1 = ((bf16[8,128,256]{2,1,0:T(8,128)(2,1)}), bf16[8,128,256]{2,1,0:T(8,128)(2,1)S(1)}, u32[]{:S(2)}, u32[]{:S(2)}) async-start(bf16[8,128,256]{2,1,0:T(8,128)(2,1)} %bitcast.13), calls=%async_computation.1 | async-start | bytes 1048576 | tf_op jit(solution)/shard_map/all_to_all | solution.py:306
  75.1 1.3 %collective-permute-start.14 = (bf16[128,512]{1,0:T(8,128)(2,1)S(1)}, bf16[128,512]{1,0:T(8,128)(2,1)S(1)}, u32[]{:S(2)}, u32[]{:S(2)}) collective-permute-start(bf16[128,512]{1,0:T(8,128)(2,1)S(1)} %get-tuple-element.15), channel_id=1, source_target_pairs={{0,8},{8,0},{1,9},{9,1},{2,10},{10,2},{3,11},{11,3},{4,12},{12,4},... | collective-permute-start | bytes 393224 | tf_op jit(solution)/shard_map/ppermute | solution.py:45
  75.2 3.1 %collective-permute-start.13 = (bf16[128,512]{1,0:T(8,128)(2,1)S(1)}, bf16[128,512]{1,0:T(8,128)(2,1)S(1)}, u32[]{:S(2)}, u32[]{:S(2)}) collective-permute-start(bf16[128,512]{1,0:T(8,128)(2,1)S(1)} %get-tuple-element.13), channel_id=1, source_target_pairs={{0,8},{8,0},{1,9},{9,1},{2,10},{10,2},{3,11},{11,3},{4,12},{12,4},... | collective-permute-start | bytes 393224 | tf_op jit(solution)/shard_map/ppermute | solution.py:45
  76.5 7.1 %collective-permute-start.15 = (bf16[128,512]{1,0:T(8,128)(2,1)S(1)}, bf16[128,512]{1,0:T(8,128)(2,1)S(1)}, u32[]{:S(2)}, u32[]{:S(2)}) collective-permute-start(bf16[128,512]{1,0:T(8,128)(2,1)S(1)} %add_convert_fusion), channel_id=1, source_target_pairs={{0,128},{128,0},{1,129},{129,1},{2,130},{130,2},{3,131},{131,3},{4... | collective-permute-start | bytes 393224 | tf_op jit(solution)/shard_map/ppermute | solution.py:45

commit v3 on v2

--- a/solution.py
+++ b/solution.py
@@ -19,7 +19,6 @@
 SCALE2 = FACTOR * math.log2(math.e)
 MASKED = -1e30
 CHUNK = 256
-EXTRA = 16
 VMEM_LIMIT = 32 * 1024 * 1024
 NT = (((1,), (1,)), ((), ()))
 NN = (((1,), (0,)), ((), ()))
@@ -83,39 +82,36 @@
     return own, pick(far, (1, 0, 3, 2)), pick(core, (2, 3, 0, 1)), pick(both, (3, 2, 1, 0))
 
 
-def whole_row(ref, head):
-    at = 3 * head
-    parts = ref[...].astype(jnp.float32)
-    row = lax.broadcasted_iota(jnp.int32, parts.shape, 0)
-    return jnp.sum(jnp.where((row >= at) & (row < at + 3), parts, 0.0), axis=0, keepdims=True)
-
-
 def delta_kernel(
-    kpos, qpos, q0, q1, q2, q3, u0, u1, u2, u3, k, v, l0, l1, l2, l3, lse_ref, delta_ref, bias
+    kpos, qpos, q0, q1, q2, q3, u0, u1, u2, u3, k, v, lse_ref, stats_ref, bias
 ):
     fill_bias(kpos, qpos, bias)
     q, u = joined((q0, q1, q2, q3)), joined((u0, u1, u2, u3))
-    parts = aligned(*(whole_row(r, pl.program_id(0)) for r in (l0, l1, l2, l3)))
-    peak = jnp.maximum(jnp.maximum(parts[0], parts[1]), jnp.maximum(parts[2], parts[3]))
-    lse = peak + jnp.log2(sum(jnp.exp2(p - peak) for p in parts))
-    lse_ref[0] = lse
+    lse = lse_ref[0]
     total = jnp.zeros_like(lse)
     for at in range(0, k.shape[0], CHUNK):
         rows = pl.ds(at, CHUNK)
         w = jnp.exp2(mm(k[rows, :], q, NT) * SCALE2 + bias[rows, :] - lse)
         total = total + jnp.sum(w * mm(v[rows, :], u, NT), axis=0, keepdims=True)
-    delta_ref[0] = total
+    stats_ref[0, 0:1, :] = lse
+    stats_ref[0, 1:2, :] = total
 
 
 def grad_kernel(
-    kpos, qpos, q0, q1, q2, q3, u0, u1, u2, u3, k, v, lse_in, d0, d1, d2, d3,
+    kpos, qpos, q0, q1, q2, q3, u0, u1, u2, u3, k, v, s0, s1, s2, s3,
     own_ref, far_ref, core_ref, both_ref, terms_ref, bias, dk, dv, kt,
 ):
     fill_bias(kpos, qpos, bias)
     head = pl.program_id(0)
     q, u = joined((q0, q1, q2, q3)), joined((u0, u1, u2, u3))
-    lse = lse_in[0]
-    delta = sum(aligned(d0[0], d1[0], d2[0], d3[0]))
+    parts = aligned(s0[0], s1[0], s2[0], s3[0])
+    peak = jnp.maximum(
+        jnp.maximum(parts[0][:1], parts[1][:1]), jnp.maximum(parts[2][:1], parts[3][:1])
+    )
+    shares = [jnp.exp2(p[:1] - peak) for p in parts]
+    whole_share = sum(shares)
+    lse = peak + jnp.log2(whole_share)
+    delta = sum(p[1:] * share for p, share in zip(parts, shares)) / whole_share
 
     @pl.when(head == 0)
     def _():
@@ -144,26 +140,14 @@
         terms_ref[:, HEAD_DIM:] = dv[...].astype(jnp.bfloat16)
 
 
-def split3(value):
-    high = value.astype(jnp.bfloat16)
-    rest = value - high.astype(jnp.float32)
-    mid = rest.astype(jnp.bfloat16)
-    low = (rest - mid.astype(jnp.float32)).astype(jnp.bfloat16)
-    return high, mid, low
-
-
 def upstream_kernel(order, *refs):
-    parts, lse, w_hbm, out, w, sems = refs[:-5], *refs[-5:]
-    width = parts[0].shape[1]
+    parts, w_hbm, out, w, sems = refs[:-4], *refs[-4:]
+    rows, width = out.shape[0], parts[0].shape[1]
     copies = []
     for i in range(order.shape[0]):
         at = pl.multiple_of(order[i] * width, width)
         copies.append(pltpu.make_async_copy(w_hbm.at[:, pl.ds(at, width)], w.at[i], sems.at[i]))
         copies[-1].start()
-    rows = out.shape[0] - EXTRA
-    pieces = [piece for h in range(GROUPS) for piece in split3(lse[h])]
-    pieces.append(jnp.zeros((EXTRA - len(pieces), out.shape[1]), jnp.bfloat16))
-    out[rows:, :] = jnp.concatenate(pieces, axis=0)
     total, i = None, 0
     for part in parts:
         for at in range(0, part.shape[0], rows):
@@ -171,14 +155,10 @@
             term = mm(part[at : at + rows, :], w[i], NT)
             total = term if total is None else total + term
             i += 1
-    out[:rows, :] = total.astype(out.dtype)
-
-
-def whole(shape):
-    return pl.BlockSpec(shape, lambda h: (0,) * len(shape))
-
-
-def upstream_of(parts, order, lse, o_weight):
+    out[...] = total.astype(out.dtype)
+
+
+def upstream_of(parts, order, o_weight):
     width = parts[0].shape[1]
     cols = o_weight.shape[0]
     count = order.shape[0]
@@ -186,9 +166,9 @@
     vmem = pl.BlockSpec(memory_space=pltpu.VMEM)
     return pl.pallas_call(
         upstream_kernel,
-        out_shape=jax.ShapeDtypeStruct((rows + EXTRA, cols), jnp.bfloat16),
+        out_shape=jax.ShapeDtypeStruct((rows, cols), jnp.bfloat16),
         in_specs=[pl.BlockSpec(memory_space=pltpu.SMEM)]
-        + [vmem] * (len(parts) + 1)
+        + [vmem] * len(parts)
         + [pl.BlockSpec(memory_space=pltpu.HBM)],
         out_specs=vmem,
         scratch_shapes=[
@@ -197,7 +177,11 @@
         ],
         compiler_params=pltpu.CompilerParams(vmem_limit_bytes=VMEM_LIMIT),
         name="upstream",
-    )(order, *parts, lse, pltpu.with_memory_space_constraint(o_weight, pltpu.HBM))
+    )(order, *parts, pltpu.with_memory_space_constraint(o_weight, pltpu.HBM))
+
+
+def whole(shape):
+    return pl.BlockSpec(shape, lambda h: (0,) * len(shape))
 
 
 def local(queries, key_states, value_states, out_grad, o_weight, span_order):
@@ -251,12 +235,13 @@
     places = [whole((keys, 1)), whole((1, many))]
     key_block = pl.BlockSpec((keys, HEAD_DIM), lambda h: (0, 0))
     value_block = pl.BlockSpec((keys, HEAD_DIM), lambda h: (0, 1))
-    extra_block = pl.BlockSpec((EXTRA, many), lambda h: (rows // EXTRA, 0))
+    stats_block = pl.BlockSpec((1, 2, many), lambda h: (h, 0, 0))
     term_sum = pltpu.VMEM((keys, HEAD_DIM), f32)
     bias = pltpu.VMEM((keys, many), f32)
     params = pltpu.CompilerParams(vmem_limit_bytes=VMEM_LIMIT)
 
-    q = shared(queries)
+    held, pair = lax.optimization_barrier((queries, pair))
+    q = shared(held)
     lse = pl.pallas_call(
         stats_kernel,
         grid=(GROUPS,),
@@ -268,19 +253,21 @@
         name="row_stats",
     )(kpos, qpos, *q, kv)
 
-    upstream = upstream_of(parts, order, lse, o_weight)
-    u = shared(upstream)
-    lse_all, delta = pl.pallas_call(
+    upstream = upstream_of(parts, order, o_weight)
+    far = shift_by(upstream, ("yh",), (1,))
+    far, lse = lax.optimization_barrier((far, lse))
+    u = upstream, far, shift_by(upstream, ("c",), (1,)), shift_by(far, ("c",), (1,))
+    stats = pl.pallas_call(
         delta_kernel,
         grid=(GROUPS,),
-        out_shape=(row_shape, row_shape),
-        in_specs=places + [head_block] * 8 + [key_block, value_block] + [extra_block] * 4,
-        out_specs=(row_block, row_block),
+        out_shape=jax.ShapeDtypeStruct((GROUPS, 2, many), f32),
+        in_specs=places + [head_block] * 8 + [key_block, value_block, row_block],
+        out_specs=stats_block,
         scratch_shapes=[bias],
         compiler_params=params,
         name="row_delta",
-    )(kpos, qpos, *q, *u, kv, kv, *u)
-    delta_parts = everyone(delta)
+    )(kpos, qpos, *q, *u, kv, kv, lse)
+    stats_parts = everyone(stats)
 
     wide = (rows, GROUPS * HEAD_DIM)
     own, far, core, across, terms = pl.pallas_call(
@@ -296,12 +283,12 @@
         in_specs=places
         + [head_block] * 8
         + [key_block, value_block]
-        + [row_block] * 5,
+        + [stats_block] * 4,
         out_specs=(head_block,) * 4 + (whole((keys, 2 * HEAD_DIM)),),
         scratch_shapes=[bias, term_sum, term_sum, pltpu.VMEM((HEAD_DIM, keys), bf16)],
         compiler_params=params,
         name="gradients",
-    )(kpos, qpos, *q, *u, kv, kv, lse_all, *delta_parts)
+    )(kpos, qpos, *q, *u, kv, kv, *stats_parts)
 
     summed = lax.all_to_all(terms.reshape(nz, rows, 2 * HEAD_DIM), "z", 0, 0, tiled=True)
     summed = jnp.sum(summed.astype(f32), axis=0)

time: 92.9 us -> 87.2 us (0.939)
  waiting for transfers between devices: 34.2 us -> 26.9 us
  starting transfers between devices: 31.8 us -> 34.3 us
    ppermute x16, waiting for transfers between devices: 26.1 us -> 19.5 us  [shift_by(): return lax.ppermute(value, axes, pairs)]
    ppermute x16, starting transfers between devices: 16.3 us -> 18.6 us  [shift_by(): return lax.ppermute(value, axes, pairs)]
  transfers between devices with their start and end apart: 18 -> 18, of which waited for: 12 -> 10; matrix products, arithmetic and copies ran while one was open for 4% -> 4% of each run, Pallas kernels for 4% -> 8%
where the time goes in v3:
time: 87.2 us; the launch traced here: 86.8 us
  starting transfers between devices  34.3 us (39%)
  waiting for transfers between devices  26.9 us (31%)
  Pallas kernels  19.1 us (22%)
  local copies, waits for them, and re-layouts  3.93 us (5%)
  other arithmetic  1.87 us (2%)
    ppermute x16, waiting for transfers between devices, shift_by(): return lax.ppermute(value, axes, pairs)  19.5 us
    ppermute x16, starting transfers between devices, shift_by(): return lax.ppermute(value, axes, pairs)  18.6 us
    all_to_all x1, starting transfers between devices, local(): lax.all_to_all(jnp.broadcast_to(both[None], (nz, *both.shape)), 'z', 0, 0...  8.47 us
    pallas_call x1, Pallas kernels, local(): pl.pallas_call(grad_kernel, grid=(GROUPS,), out_shape=(jax.ShapeDtypeStru...  8.32 us
    all_to_all x1, waiting for transfers between devices, local(): lax.all_to_all(terms.reshape(nz, rows, 2 * HEAD_DIM), 'z', 0, 0, tiled=True)  7.4 us
    all_to_all x1, starting transfers between devices, local(): lax.all_to_all(terms.reshape(nz, rows, 2 * HEAD_DIM), 'z', 0, 0, tiled=True)  7.22 us
    pallas_call x1, Pallas kernels, local(): pl.pallas_call(stats_kernel, grid=(GROUPS,), out_shape=row_shape, in_spec...  3.63 us
    pallas_call x1, Pallas kernels, local(): pl.pallas_call(delta_kernel, grid=(GROUPS,), out_shape=jax.ShapeDtypeStru...  3.62 us
  transfers between devices with their start and end apart: 18, of which 10 were waited for; matrix products, arithmetic and copies ran while one was open for 4% of the time, Pallas kernels for 8%

profile of v3, /device:TPU:2, one launch (start us, length us, event | category | flops | bytes accessed | tf_op | source)
XLA Modules:
  0.0 86.8 jit_solution(2169226359276806138)
XLA Ops:
  0.6 0.8 pad_maximum_fusion
  1.4 0.8 broadcast_in_dim.2
  2.3 8.5 %all-to-all-start = ((bf16[8,128,256]{2,1,0:T(8,128)(2,1)}), bf16[8,128,256]{2,1,0:T(8,128)(2,1)S(1)}, u32[]{:S(2)}, u32[]{:S(2)}) async-start(bf16[8,128,256]{2,1,0:T(8,128)(2,1)} %broadcast_in_dim.2), calls=%async_computation | async-start | bytes 1048576 | tf_op jit(solution)/shard_map/all_to_all | solution.py:198
  10.7 1.6 %collective-permute-start = (bf16[128,512]{1,0:T(8,128)(2,1)}, bf16[128,512]{1,0:T(8,128)(2,1)S(1)}, u32[]{:S(2)}, u32[]{:S(2)}) collective-permute-start(bf16[128,512]{1,0:T(8,128)(2,1)} %param.9), channel_id=1, source_target_pairs={{0,4},{4,0},{1,5},{5,1},{2,6},{6,2},{3,7},{7,3},{8,12},{12,8},{9,1... | collective-permute-start | bytes 393224 | tf_op jit(solution)/shard_map/ppermute | solution.py:44
  12.3 0.8 reshape.118
  13.1 0.9 %constant_dynamic-update-slice_fusion.1 = bf16[256,512]{1,0:T(8,128)(2,1)S(1)} fusion(bf16[128,512]{1,0:T(8,128)(2,1)} %param.9), kind=kLoop, calls=%fused_computation.6 | loop fusion | bytes 262144
  14.0 1.9 %collective-permute-done = bf16[128,512]{1,0:T(8,128)(2,1)S(1)} collective-permute-done((bf16[128,512]{1,0:T(8,128)(2,1)}, bf16[128,512]{1,0:T(8,128)(2,1)S(1)}, u32[]{:S(2)}, u32[]{:S(2)}) %collective-permute-start) | collective-permute-done | bytes 131104 | tf_op jit(solution)/shard_map/ppermute | solution.py:44
  15.9 2.2 %collective-permute-start.6 = (bf16[256,512]{1,0:T(8,128)(2,1)S(1)}, bf16[256,512]{1,0:T(8,128)(2,1)S(1)}, u32[]{:S(2)}, u32[]{:S(2)}) collective-permute-start(bf16[256,512]{1,0:T(8,128)(2,1)S(1)} %constant_dynamic-update-slice_fusion.refs_0_), channel_id=1, source_target_pairs={{0,2},{1,3},{2,0},{3,1},{4,6},{5,7},{6,4},{7,5},{8,10},{9,11},{10,... | collective-permute-start | bytes 786440 | tf_op jit(solution)/shard_map/ppermute | solution.py:44
  18.1 1.4 %collective-permute-start.5 = (bf16[256,512]{1,0:T(8,128)(2,1)S(1)}, bf16[256,512]{1,0:T(8,128)(2,1)S(1)}, u32[]{:S(2)}, u32[]{:S(2)}) collective-permute-start(bf16[256,512]{1,0:T(8,128)(2,1)S(1)} %constant_dynamic-update-slice_fusion.refs_0_), channel_id=1, source_target_pairs={{0,3},{1,0},{2,1},{3,2},{4,7},{5,4},{6,5},{7,6},{8,11},{9,8},{10,9... | collective-permute-start | bytes 786440 | tf_op jit(solution)/shard_map/ppermute | solution.py:44
  19.6 0.6 collective-permute-start.4
  20.2 0.1 add_multiply_fusion
  20.3 0.1 mul.32
  20.3 3.2 %collective-permute-start.1 = (bf16[128,512]{1,0:T(8,128)(2,1)}, bf16[128,512]{1,0:T(8,128)(2,1)S(1)}, u32[]{:S(2)}, u32[]{:S(2)}) collective-permute-start(bf16[128,512]{1,0:T(8,128)(2,1)} %q0.2), channel_id=1, source_target_pairs={{0,128},{128,0},{1,129},{129,1},{2,130},{130,2},{3,131},{131,3},{4... | collective-permute-start | bytes 393224 | tf_op jit(solution)/shard_map/ppermute | solution.py:44
  23.6 0.1 iota_add_fusion.1
  23.6 0.1 add.133.qpos
  23.7 0.1 stack.35.order
  23.8 0.0 collective-permute-start.2
  23.8 3.2 %collective-permute-done.1.q1 = bf16[128,512]{1,0:T(8,128)(2,1)S(1)} collective-permute-done((bf16[128,512]{1,0:T(8,128)(2,1)}, bf16[128,512]{1,0:T(8,128)(2,1)S(1)}, u32[]{:S(2)}, u32[]{:S(2)}) %collective-permute-start.1) | collective-permute-done | bytes 131104 | tf_op jit(solution)/shard_map/ppermute | solution.py:44
  27.1 0.0 collective-permute-start.3
  27.1 0.0 collective-permute-done.6.refs_3_
  27.1 2.7 %collective-permute-done.5.refs_2_ = bf16[256,512]{1,0:T(8,128)(2,1)S(1)} collective-permute-done((bf16[256,512]{1,0:T(8,128)(2,1)S(1)}, bf16[256,512]{1,0:T(8,128)(2,1)S(1)}, u32[]{:S(2)}, u32[]{:S(2)}) %collective-permute-start.5) | collective-permute-done | bytes 262176 | tf_op jit(solution)/shard_map/ppermute | solution.py:44
  29.7 0.1 collective-permute-done.4.refs_1_
  29.8 3.5 %upstream.1.u0 = bf16[128,512]{1,0:T(8,128)(2,1)S(1)} custom-call(s32[8]{0:T(128)S(1)} %stack.35.order, bf16[256,512]{1,0:T(8,128)(2,1)S(1)} %constant_dynamic-update-slice_fusion.refs_0_, bf16[256,512]{1,0:T(8,128)(2,1)S(1)} %collective-permute-done.4.refs_1_, bf16[256,512]{1,0:T(8,128)(2,1)S(1)} %collective-permute-done.5.refs_2_, ...), custom_call_target="tpu_custom_call" | custom-call | tf_op jit(solution)/shard_map/upstream/pallas_call | solution.py:167
  33.3 3.3 %collective-permute-start.7 = (bf16[128,512]{1,0:T(8,128)(2,1)S(1)}, bf16[128,512]{1,0:T(8,128)(2,1)S(1)}, u32[]{:S(2)}, u32[]{:S(2)}) collective-permute-start(bf16[128,512]{1,0:T(8,128)(2,1)S(1)} %upstream.1.u0), channel_id=1, source_target_pairs={{0,128},{128,0},{1,129},{129,1},{2,130},{130,2},{3,131},{131,3},{4... | collective-permute-start | bytes 393224 | tf_op jit(solution)/shard_map/ppermute | solution.py:44
  36.6 0.1 iota_add_fusion
  36.7 0.5 add.149.kpos
  37.2 0.1 collective-permute-start.8
  37.3 0.0 collective-permute-done.2.q2
  37.3 0.0 all-to-all-done
  37.3 3.6 %row_stats.1.lse_ref = f32[4,1,512]{2,1,0:T(1,128)S(1)} custom-call(s32[1024,1]{1,0:T(8,128)S(1)} %add.149.kpos, s32[1,512]{1,0:T(1,128)S(1)} %add.133.qpos, bf16[128,512]{1,0:T(8,128)(2,1)S(1)} %copy-done, bf16[128,512]{1,0:T(8,128)(2,1)S(1)} %collective-permute-done.1.q1, bf16[128,512]{1,0:T(8,128)(2,1)S(1)} %collective-permute-done.2.q2, ...), custom_call_target="tpu_custom_call" | custom-call | tf_op jit(solution)/shard_map/row_stats/pallas_call | solution.py:245
  40.9 0.6 collective-permute-start.9
  41.5 1.0 %collective-permute-done.9.u3 = bf16[128,512]{1,0:T(8,128)(2,1)S(1)} collective-permute-done((bf16[128,512]{1,0:T(8,128)(2,1)S(1)}, bf16[128,512]{1,0:T(8,128)(2,1)S(1)}, u32[]{:S(2)}, u32[]{:S(2)}) %collective-permute-start.9) | collective-permute-done | bytes 131104 | tf_op jit(solution)/shard_map/ppermute | solution.py:44
  42.5 3.6 %row_delta.1.s0 = f32[4,2,512]{2,1,0:T(2,128)S(1)} custom-call(s32[1024,1]{1,0:T(8,128)S(1)} %add.149.kpos, s32[1,512]{1,0:T(1,128)S(1)} %add.133.qpos, bf16[128,512]{1,0:T(8,128)(2,1)S(1)} %copy-done, bf16[128,512]{1,0:T(8,128)(2,1)S(1)} %collective-permute-done.1.q1, bf16[128,512]{1,0:T(8,128)(2,1)S(1)} %collective-permute-done.2.q2, ...), custom_call_target="tpu_custom_call" | custom-call | tf_op jit(solution)/shard_map/row_delta/pallas_call | solution.py:260
  46.1 2.2 %collective-permute-start.12 = (f32[4,2,512]{2,1,0:T(2,128)S(1)}, f32[4,2,512]{2,1,0:T(2,128)S(1)}, u32[]{:S(2)}, u32[]{:S(2)}) collective-permute-start(f32[4,2,512]{2,1,0:T(2,128)S(1)} %row_delta.1.s0), channel_id=1, source_target_pairs={{0,136},{8,128},{128,8},{136,0},{1,137},{9,129},{129,9},{137,1},{2... | collective-permute-start | bytes 49160 | tf_op jit(solution)/shard_map/ppermute | solution.py:44
  48.3 0.4 collective-permute-start.11
  48.6 1.2 %collective-permute-start.10 = (f32[4,2,512]{2,1,0:T(2,128)S(1)}, f32[4,2,512]{2,1,0:T(2,128)S(1)}, u32[]{:S(2)}, u32[]{:S(2)}) collective-permute-start(f32[4,2,512]{2,1,0:T(2,128)S(1)} %row_delta.1.s0), channel_id=1, source_target_pairs={{0,128},{128,0},{1,129},{129,1},{2,130},{130,2},{3,131},{131,3},{4... | collective-permute-start | bytes 49160 | tf_op jit(solution)/shard_map/ppermute | solution.py:44
  49.9 1.0 %collective-permute-done.12.s3 = f32[4,2,512]{2,1,0:T(2,128)S(1)} collective-permute-done((f32[4,2,512]{2,1,0:T(2,128)S(1)}, f32[4,2,512]{2,1,0:T(2,128)S(1)}, u32[]{:S(2)}, u32[]{:S(2)}) %collective-permute-start.12) | collective-permute-done | bytes 16416 | tf_op jit(solution)/shard_map/ppermute | solution.py:44
  50.9 3.0 %collective-permute-done.10.s1 = f32[4,2,512]{2,1,0:T(2,128)S(1)} collective-permute-done((f32[4,2,512]{2,1,0:T(2,128)S(1)}, f32[4,2,512]{2,1,0:T(2,128)S(1)}, u32[]{:S(2)}, u32[]{:S(2)}) %collective-permute-start.10) | collective-permute-done | bytes 16416 | tf_op jit(solution)/shard_map/ppermute | solution.py:44
  53.9 8.3 %gradients.1 = (f32[128,512]{1,0:T(8,128)S(1)}, f32[128,512]{1,0:T(8,128)S(1)}, bf16[128,512]{1,0:T(8,128)(2,1)S(1)}, bf16[128,512]{1,0:T(8,128)(2,1)S(1)}, bf16[1024,256]{1,0:T(8,128)(2,1)}) custom-call(s32[1024,1]{1,0:T(8,128)S(1)} %add.149.kpos, s32[1,512]{1,0:T(1,128)S(1)} %add.133.qpos, bf16[128,512]{1,0:T(8,128)(2,1)S(1)} %copy-done, ...), custom_call_target="tpu_custom_call" | custom-call | tf_op jit(solution)/shard_map/gradients/pallas_call | solution.py:273
  62.2 7.2 %all-to-all-start.1 = ((bf16[8,128,256]{2,1,0:T(8,128)(2,1)}), bf16[8,128,256]{2,1,0:T(8,128)(2,1)S(1)}, u32[]{:S(2)}, u32[]{:S(2)}) async-start(bf16[8,128,256]{2,1,0:T(8,128)(2,1)} %bitcast.13), calls=%async_computation.1 | async-start | bytes 1048576 | tf_op jit(solution)/shard_map/all_to_all | solution.py:293
  69.4 0.5 collective-permute-start.13
  69.9 0.8 collective-permute-done.14
  70.8 1.3 %collective-permute-start.15 = (bf16[128,512]{1,0:T(8,128)(2,1)S(1)}, bf16[128,512]{1,0:T(8,128)(2,1)S(1)}, u32[]{:S(2)}, u32[]{:S(2)}) collective-permute-start(bf16[128,512]{1,0:T(8,128)(2,1)S(1)} %add_convert_fusion), channel_id=1, source_target_pairs={{0,128},{128,0},{1,129},{129,1},{2,130},{130,2},{3,131},{131,3},{4... | collective-permute-start | bytes 393224 | tf_op jit(solution)/shard_map/ppermute | solution.py:44
  72.1 5.8 %collective-permute-done.15 = bf16[128,512]{1,0:T(8,128)(2,1)S(1)} collective-permute-done((bf16[128,512]{1,0:T(8,128)(2,1)S(1)}, bf16[128,512]{1,0:T(8,128)(2,1)S(1)}, u32[]{:S(2)}, u32[]{:S(2)}) %collective-permute-start.15) | collective-permute-done | bytes 131104 | tf_op jit(solution)/shard_map/ppermute | solution.py:44
  78.0 0.7 convert_add_fusion
  78.7 7.4 %all-to-all-done.1 = bf16[8,128,256]{2,1,0:T(8,128)(2,1)S(1)} async-done(((bf16[8,128,256]{2,1,0:T(8,128)(2,1)}), bf16[8,128,256]{2,1,0:T(8,128)(2,1)S(1)}, u32[]{:S(2)}, u32[]{:S(2)}) %all-to-all-start.1) | async-done | bytes 524320 | tf_op jit(solution)/shard_map/all_to_all | solution.py:293
  86.1 0.1 convert_reduce_fusion
  86.2 0.7 fusion.4
  (12 shorter events, 0.1 us)
Async XLA Ops:
  1.4 35.9 %copy-start = (bf16[128,512]{1,0:T(8,128)(2,1)S(1)}, bf16[128,512]{1,0:T(8,128)(2,1)}, u32[]{:S(2)}) copy-start(bf16[128,512]{1,0:T(8,128)(2,1)} %q0.2) | copy-start | bytes 393220
  2.3 35.0 %all-to-all-start = ((bf16[8,128,256]{2,1,0:T(8,128)(2,1)}), bf16[8,128,256]{2,1,0:T(8,128)(2,1)S(1)}, u32[]{:S(2)}, u32[]{:S(2)}) async-start(bf16[8,128,256]{2,1,0:T(8,128)(2,1)} %broadcast_in_dim.2), calls=%async_computation | async-start | bytes 1048576 | tf_op jit(solution)/shard_map/all_to_all | solution.py:198
  10.7 5.2 %collective-permute-start = (bf16[128,512]{1,0:T(8,128)(2,1)}, bf16[128,512]{1,0:T(8,128)(2,1)S(1)}, u32[]{:S(2)}, u32[]{:S(2)}) collective-permute-start(bf16[128,512]{1,0:T(8,128)(2,1)} %param.9), channel_id=1, source_target_pairs={{0,4},{4,0},{1,5},{5,1},{2,6},{6,2},{3,7},{7,3},{8,12},{12,8},{9,1... | collective-permute-start | bytes 393224 | tf_op jit(solution)/shard_map/ppermute | solution.py:44
  15.9 11.1 %collective-permute-start.6 = (bf16[256,512]{1,0:T(8,128)(2,1)S(1)}, bf16[256,512]{1,0:T(8,128)(2,1)S(1)}, u32[]{:S(2)}, u32[]{:S(2)}) collective-permute-start(bf16[256,512]{1,0:T(8,128)(2,1)S(1)} %constant_dynamic-update-slice_fusion.refs_0_), channel_id=1, source_target_pairs={{0,2},{1,3},{2,0},{3,1},{4,6},{5,7},{6,4},{7,5},{8,10},{9,11},{10,... | collective-permute-start | bytes 786440 | tf_op jit(solution)/shard_map/ppermute | solution.py:44
  18.1 11.6 %collective-permute-start.5 = (bf16[256,512]{1,0:T(8,128)(2,1)S(1)}, bf16[256,512]{1,0:T(8,128)(2,1)S(1)}, u32[]{:S(2)}, u32[]{:S(2)}) collective-permute-start(bf16[256,512]{1,0:T(8,128)(2,1)S(1)} %constant_dynamic-update-slice_fusion.refs_0_), channel_id=1, source_target_pairs={{0,3},{1,0},{2,1},{3,2},{4,7},{5,4},{6,5},{7,6},{8,11},{9,8},{10,9... | collective-permute-start | bytes 786440 | tf_op jit(solution)/shard_map/ppermute | solution.py:44
  19.6 10.3 %collective-permute-start.4 = (bf16[256,512]{1,0:T(8,128)(2,1)S(1)}, bf16[256,512]{1,0:T(8,128)(2,1)S(1)}, u32[]{:S(2)}, u32[]{:S(2)}) collective-permute-start(bf16[256,512]{1,0:T(8,128)(2,1)S(1)} %constant_dynamic-update-slice_fusion.refs_0_), channel_id=1, source_target_pairs={{0,1},{1,2},{2,3},{3,0},{4,5},{5,6},{6,7},{7,4},{8,9},{9,10},{10,1... | collective-permute-start | bytes 786440 | tf_op jit(solution)/shard_map/ppermute | solution.py:44
  20.3 6.7 %collective-permute-start.1 = (bf16[128,512]{1,0:T(8,128)(2,1)}, bf16[128,512]{1,0:T(8,128)(2,1)S(1)}, u32[]{:S(2)}, u32[]{:S(2)}) collective-permute-start(bf16[128,512]{1,0:T(8,128)(2,1)} %q0.2), channel_id=1, source_target_pairs={{0,128},{128,0},{1,129},{129,1},{2,130},{130,2},{3,131},{131,3},{4... | collective-permute-start | bytes 393224 | tf_op jit(solution)/shard_map/ppermute | solution.py:44
  23.8 13.5 %collective-permute-start.2 = (bf16[128,512]{1,0:T(8,128)(2,1)}, bf16[128,512]{1,0:T(8,128)(2,1)S(1)}, u32[]{:S(2)}, u32[]{:S(2)}) collective-permute-start(bf16[128,512]{1,0:T(8,128)(2,1)} %q0.2), channel_id=1, source_target_pairs={{0,8},{8,0},{1,9},{9,1},{2,10},{10,2},{3,11},{11,3},{4,12},{12,4},... | collective-permute-start | bytes 393224 | tf_op jit(solution)/shard_map/ppermute | solution.py:44
  27.1 10.2 %collective-permute-start.3 = (bf16[128,512]{1,0:T(8,128)(2,1)S(1)}, bf16[128,512]{1,0:T(8,128)(2,1)S(1)}, u32[]{:S(2)}, u32[]{:S(2)}) collective-permute-start(bf16[128,512]{1,0:T(8,128)(2,1)S(1)} %collective-permute-done.1.q1), channel_id=1, source_target_pairs={{0,8},{8,0},{1,9},{9,1},{2,10},{10,2},{3,11},{11,3},{4,12},{12,4},... | collective-permute-start | bytes 393224 | tf_op jit(solution)/shard_map/ppermute | solution.py:44
  33.3 7.6 %collective-permute-start.7 = (bf16[128,512]{1,0:T(8,128)(2,1)S(1)}, bf16[128,512]{1,0:T(8,128)(2,1)S(1)}, u32[]{:S(2)}, u32[]{:S(2)}) collective-permute-start(bf16[128,512]{1,0:T(8,128)(2,1)S(1)} %upstream.1.u0), channel_id=1, source_target_pairs={{0,128},{128,0},{1,129},{129,1},{2,130},{130,2},{3,131},{131,3},{4... | collective-permute-start | bytes 393224 | tf_op jit(solution)/shard_map/ppermute | solution.py:44
  37.2 4.4 %collective-permute-start.8 = (bf16[128,512]{1,0:T(8,128)(2,1)S(1)}, bf16[128,512]{1,0:T(8,128)(2,1)S(1)}, u32[]{:S(2)}, u32[]{:S(2)}) collective-permute-start(bf16[128,512]{1,0:T(8,128)(2,1)S(1)} %upstream.1.u0), channel_id=1, source_target_pairs={{0,8},{8,0},{1,9},{9,1},{2,10},{10,2},{3,11},{11,3},{4,12},{12,4},... | collective-permute-start | bytes 393224 | tf_op jit(solution)/shard_map/ppermute | solution.py:44
  40.9 1.6 %collective-permute-start.9 = (bf16[128,512]{1,0:T(8,128)(2,1)S(1)}, bf16[128,512]{1,0:T(8,128)(2,1)S(1)}, u32[]{:S(2)}, u32[]{:S(2)}) collective-permute-start(bf16[128,512]{1,0:T(8,128)(2,1)S(1)} %collective-permute-done.7.u1), channel_id=1, source_target_pairs={{0,8},{8,0},{1,9},{9,1},{2,10},{10,2},{3,11},{11,3},{4,12},{12,4},... | collective-permute-start | bytes 393224 | tf_op jit(solution)/shard_map/ppermute | solution.py:44
  46.1 4.8 %collective-permute-start.12 = (f32[4,2,512]{2,1,0:T(2,128)S(1)}, f32[4,2,512]{2,1,0:T(2,128)S(1)}, u32[]{:S(2)}, u32[]{:S(2)}) collective-permute-start(f32[4,2,512]{2,1,0:T(2,128)S(1)} %row_delta.1.s0), channel_id=1, source_target_pairs={{0,136},{8,128},{128,8},{136,0},{1,137},{9,129},{129,9},{137,1},{2... | collective-permute-start | bytes 49160 | tf_op jit(solution)/shard_map/ppermute | solution.py:44
  48.3 2.6 %collective-permute-start.11 = (f32[4,2,512]{2,1,0:T(2,128)S(1)}, f32[4,2,512]{2,1,0:T(2,128)S(1)}, u32[]{:S(2)}, u32[]{:S(2)}) collective-permute-start(f32[4,2,512]{2,1,0:T(2,128)S(1)} %row_delta.1.s0), channel_id=1, source_target_pairs={{0,8},{8,0},{1,9},{9,1},{2,10},{10,2},{3,11},{11,3},{4,12},{12,4},... | collective-permute-start | bytes 49160 | tf_op jit(solution)/shard_map/ppermute | solution.py:44
  48.6 5.2 %collective-permute-start.10 = (f32[4,2,512]{2,1,0:T(2,128)S(1)}, f32[4,2,512]{2,1,0:T(2,128)S(1)}, u32[]{:S(2)}, u32[]{:S(2)}) collective-permute-start(f32[4,2,512]{2,1,0:T(2,128)S(1)} %row_delta.1.s0), channel_id=1, source_target_pairs={{0,128},{128,0},{1,129},{129,1},{2,130},{130,2},{3,131},{131,3},{4... | collective-permute-start | bytes 49160 | tf_op jit(solution)/shard_map/ppermute | solution.py:44
  62.2 23.9 %all-to-all-start.1 = ((bf16[8,128,256]{2,1,0:T(8,128)(2,1)}), bf16[8,128,256]{2,1,0:T(8,128)(2,1)S(1)}, u32[]{:S(2)}, u32[]{:S(2)}) async-start(bf16[8,128,256]{2,1,0:T(8,128)(2,1)} %bitcast.13), calls=%async_computation.1 | async-start | bytes 1048576 | tf_op jit(solution)/shard_map/all_to_all | solution.py:293
  69.4 1.3 %collective-permute-start.14 = (bf16[128,512]{1,0:T(8,128)(2,1)S(1)}, bf16[128,512]{1,0:T(8,128)(2,1)S(1)}, u32[]{:S(2)}, u32[]{:S(2)}) collective-permute-start(bf16[128,512]{1,0:T(8,128)(2,1)S(1)} %get-tuple-element.17), channel_id=1, source_target_pairs={{0,8},{8,0},{1,9},{9,1},{2,10},{10,2},{3,11},{11,3},{4,12},{12,4},... | collective-permute-start | bytes 393224 | tf_op jit(solution)/shard_map/ppermute | solution.py:44
  69.4 2.7 %collective-permute-start.13 = (bf16[128,512]{1,0:T(8,128)(2,1)S(1)}, bf16[128,512]{1,0:T(8,128)(2,1)S(1)}, u32[]{:S(2)}, u32[]{:S(2)}) collective-permute-start(bf16[128,512]{1,0:T(8,128)(2,1)S(1)} %get-tuple-element.15), channel_id=1, source_target_pairs={{0,8},{8,0},{1,9},{9,1},{2,10},{10,2},{3,11},{11,3},{4,12},{12,4},... | collective-permute-start | bytes 393224 | tf_op jit(solution)/shard_map/ppermute | solution.py:44
  70.8 7.1 %collective-permute-start.15 = (bf16[128,512]{1,0:T(8,128)(2,1)S(1)}, bf16[128,512]{1,0:T(8,128)(2,1)S(1)}, u32[]{:S(2)}, u32[]{:S(2)}) collective-permute-start(bf16[128,512]{1,0:T(8,128)(2,1)S(1)} %add_convert_fusion), channel_id=1, source_target_pairs={{0,128},{128,0},{1,129},{129,1},{2,130},{130,2},{3,131},{131,3},{4... | collective-permute-start | bytes 393224 | tf_op jit(solution)/shard_map/ppermute | solution.py:44

commit v4 on v3

--- a/solution.py
+++ b/solution.py
@@ -18,7 +18,7 @@
 FACTOR = HEAD_DIM**-0.5
 SCALE2 = FACTOR * math.log2(math.e)
 MASKED = -1e30
-CHUNK = 256
+CHUNK = 512
 VMEM_LIMIT = 32 * 1024 * 1024
 NT = (((1,), (1,)), ((), ()))
 NN = (((1,), (0,)), ((), ()))
@@ -44,67 +44,67 @@
     return lax.ppermute(value, axes, pairs)
 
 
-def joined(refs):
-    return jnp.concatenate([r[...] for r in refs], axis=0)
-
-
-def fill_bias(kpos_ref, qpos_ref, bias_ref):
-    @pl.when(pl.program_id(0) == 0)
-    def _():
-        for at in range(0, bias_ref.shape[0], CHUNK):
-            rows = pl.ds(at, CHUNK)
-            visible = kpos_ref[rows, :] <= qpos_ref[...]
-            bias_ref[rows, :] = jnp.where(visible, 0.0, MASKED)
-
-
-def stats_kernel(kpos, qpos, q0, q1, q2, q3, k, lse_ref, bias, s_scr):
-    fill_bias(kpos, qpos, bias)
-    q = joined((q0, q1, q2, q3))
-    keys = k.shape[0]
-    peak = jnp.full((1, q.shape[0]), MASKED, jnp.float32)
+def by_heads(refs):
+    return jnp.concatenate(
+        [r[:, h * HEAD_DIM : (h + 1) * HEAD_DIM] for h in range(GROUPS) for r in refs], axis=0
+    )
+
+
+def chunk_scores(k, kpos, qpos, q, at):
+    rows = pl.ds(at, CHUNK)
+    bias = jnp.where(kpos[rows, :] <= qpos[...], 0.0, MASKED)
+    bias = jnp.concatenate([bias] * GROUPS, axis=1)
+    return mm(k[rows, :HEAD_DIM], q, NT) * SCALE2 + bias
+
+
+def stats_kernel(kpos, qpos, q0, q1, q2, q3, kv, lse_ref, q_scr, s_scr):
+    q_scr[...] = by_heads((q0, q1, q2, q3))
+    keys = kv.shape[0]
+    peak = jnp.full((1, q_scr.shape[0]), MASKED, jnp.float32)
     for at in range(0, keys, CHUNK):
-        rows = pl.ds(at, CHUNK)
-        s = mm(k[rows, :], q, NT) * SCALE2 + bias[rows, :]
-        s_scr[rows, :] = s
+        s = chunk_scores(kv, kpos, qpos, q_scr[...], at)
+        s_scr[pl.ds(at, CHUNK), :] = s
         peak = jnp.maximum(peak, jnp.max(s, axis=0, keepdims=True))
     total = jnp.zeros_like(peak)
     for at in range(0, keys, CHUNK):
         total = total + jnp.sum(jnp.exp2(s_scr[pl.ds(at, CHUNK), :] - peak), axis=0, keepdims=True)
-    lse_ref[0] = peak + jnp.log2(total)
+    lse_ref[...] = peak + jnp.log2(total)
 
 
 def aligned(own, far, core, both):
-    n = own.shape[1] // 4
+    n = own.shape[1] // (4 * GROUPS)
 
     def pick(a, order):
-        return jnp.concatenate([a[:, g * n : (g + 1) * n] for g in order], axis=1)
+        return jnp.concatenate(
+            [a[:, (4 * h + g) * n : (4 * h + g + 1) * n] for h in range(GROUPS) for g in order],
+            axis=1,
+        )
 
     return own, pick(far, (1, 0, 3, 2)), pick(core, (2, 3, 0, 1)), pick(both, (3, 2, 1, 0))
 
 
 def delta_kernel(
-    kpos, qpos, q0, q1, q2, q3, u0, u1, u2, u3, k, v, lse_ref, stats_ref, bias
+    kpos, qpos, q0, q1, q2, q3, u0, u1, u2, u3, kv, lse_ref, stats_ref, q_scr, u_scr
 ):
-    fill_bias(kpos, qpos, bias)
-    q, u = joined((q0, q1, q2, q3)), joined((u0, u1, u2, u3))
-    lse = lse_ref[0]
+    q_scr[...] = by_heads((q0, q1, q2, q3))
+    u_scr[...] = by_heads((u0, u1, u2, u3))
+    lse = lse_ref[...]
     total = jnp.zeros_like(lse)
-    for at in range(0, k.shape[0], CHUNK):
-        rows = pl.ds(at, CHUNK)
-        w = jnp.exp2(mm(k[rows, :], q, NT) * SCALE2 + bias[rows, :] - lse)
-        total = total + jnp.sum(w * mm(v[rows, :], u, NT), axis=0, keepdims=True)
-    stats_ref[0, 0:1, :] = lse
-    stats_ref[0, 1:2, :] = total
+    for at in range(0, kv.shape[0], CHUNK):
+        w = jnp.exp2(chunk_scores(kv, kpos, qpos, q_scr[...], at) - lse)
+        dp = mm(kv[pl.ds(at, CHUNK), HEAD_DIM:], u_scr[...], NT)
+        total = total + jnp.sum(w * dp, axis=0, keepdims=True)
+    stats_ref[0:1, :] = lse
+    stats_ref[1:2, :] = total
 
 
 def grad_kernel(
-    kpos, qpos, q0, q1, q2, q3, u0, u1, u2, u3, k, v, s0, s1, s2, s3,
-    own_ref, far_ref, core_ref, both_ref, terms_ref, bias, dk, dv, kt,
+    kpos, qpos, q0, q1, q2, q3, u0, u1, u2, u3, kv, s0, s1, s2, s3,
+    own_ref, far_ref, core_ref, both_ref, terms_ref, q_scr, u_scr, dq_scr,
 ):
-    fill_bias(kpos, qpos, bias)
-    head = pl.program_id(0)
-    q, u = joined((q0, q1, q2, q3)), joined((u0, u1, u2, u3))
-    parts = aligned(s0[0], s1[0], s2[0], s3[0])
+    q_scr[...] = by_heads((q0, q1, q2, q3))
+    u_scr[...] = by_heads((u0, u1, u2, u3))
+    parts = aligned(s0[...], s1[...], s2[...], s3[...])
     peak = jnp.maximum(
         jnp.maximum(parts[0][:1], parts[1][:1]), jnp.maximum(parts[2][:1], parts[3][:1])
     )
@@ -113,31 +113,21 @@
     lse = peak + jnp.log2(whole_share)
     delta = sum(p[1:] * share for p, share in zip(parts, shares)) / whole_share
 
-    @pl.when(head == 0)
-    def _():
-        dk[...] = jnp.zeros_like(dk)
-        dv[...] = jnp.zeros_like(dv)
-        kt[...] = k[...].T
-
-    dq = jnp.zeros((HEAD_DIM, q.shape[0]), jnp.float32)
-    for at in range(0, k.shape[0], CHUNK):
+    for at in range(0, kv.shape[0], CHUNK):
         rows = pl.ds(at, CHUNK)
-        w = jnp.exp2(mm(k[rows, :], q, NT) * SCALE2 + bias[rows, :] - lse)
-        ds = (w * (mm(v[rows, :], u, NT) - delta)).astype(jnp.bfloat16)
-        dv[rows, :] += mm(w.astype(jnp.bfloat16), u, NN)
-        dk[rows, :] += mm(ds, q, NN)
-        dq = dq + mm(kt[:, at : at + CHUNK], ds, NN)
-    dq = (dq * FACTOR).T
+        w = jnp.exp2(chunk_scores(kv, kpos, qpos, q_scr[...], at) - lse)
+        dp = mm(kv[rows, HEAD_DIM:], u_scr[...], NT)
+        ds = (w * (dp - delta)).astype(jnp.bfloat16)
+        terms_ref[rows, HEAD_DIM:] = mm(w.astype(jnp.bfloat16), u_scr[...], NN).astype(jnp.bfloat16)
+        terms_ref[rows, :HEAD_DIM] = (mm(ds, q_scr[...], NN) * FACTOR).astype(jnp.bfloat16)
+        dq = mm(kv[rows, :HEAD_DIM].T, ds, NN)
+        dq_scr[...] = dq if at == 0 else dq_scr[...] + dq
     n = own_ref.shape[0]
-    own_ref[...] = dq[:n]
-    far_ref[...] = dq[n : 2 * n]
-    core_ref[...] = dq[2 * n : 3 * n].astype(jnp.bfloat16)
-    both_ref[...] = dq[3 * n :].astype(jnp.bfloat16)
-
-    @pl.when(head == pl.num_programs(0) - 1)
-    def _():
-        terms_ref[:, :HEAD_DIM] = (dk[...] * FACTOR).astype(jnp.bfloat16)
-        terms_ref[:, HEAD_DIM:] = dv[...].astype(jnp.bfloat16)
+    for h in range(GROUPS):
+        for g, ref in enumerate((own_ref, far_ref, core_ref, both_ref)):
+            at = (4 * h + g) * n
+            part = (dq_scr[:, at : at + n] * FACTOR).T
+            ref[:, h * HEAD_DIM : (h + 1) * HEAD_DIM] = part.astype(ref.dtype)
 
 
 def upstream_kernel(order, *refs):
@@ -180,10 +170,6 @@
     )(order, *parts, pltpu.with_memory_space_constraint(o_weight, pltpu.HBM))
 
 
-def whole(shape):
-    return pl.BlockSpec(shape, lambda h: (0,) * len(shape))
-
-
 def local(queries, key_states, value_states, out_grad, o_weight, span_order):
     rows = queries.shape[0]
     nz = lax.axis_size("z")
@@ -229,26 +215,18 @@
     )
     qpos = (query_spans * SPAN + offsets[None, :]).reshape(1, many)
 
-    head_block = pl.BlockSpec((rows, HEAD_DIM), lambda h: (0, h))
-    row_block = pl.BlockSpec((1, 1, many), lambda h: (h, 0, 0))
-    row_shape = jax.ShapeDtypeStruct((GROUPS, 1, many), f32)
-    places = [whole((keys, 1)), whole((1, many))]
-    key_block = pl.BlockSpec((keys, HEAD_DIM), lambda h: (0, 0))
-    value_block = pl.BlockSpec((keys, HEAD_DIM), lambda h: (0, 1))
-    stats_block = pl.BlockSpec((1, 2, many), lambda h: (h, 0, 0))
-    term_sum = pltpu.VMEM((keys, HEAD_DIM), f32)
-    bias = pltpu.VMEM((keys, many), f32)
+    vmem = pl.BlockSpec(memory_space=pltpu.VMEM)
+    wide = pltpu.VMEM((GROUPS * many, HEAD_DIM), bf16)
     params = pltpu.CompilerParams(vmem_limit_bytes=VMEM_LIMIT)
 
     held, pair = lax.optimization_barrier((queries, pair))
     q = shared(held)
     lse = pl.pallas_call(
         stats_kernel,
-        grid=(GROUPS,),
-        out_shape=row_shape,
-        in_specs=places + [head_block] * 4 + [key_block],
-        out_specs=row_block,
-        scratch_shapes=[bias, bias],
+        out_shape=jax.ShapeDtypeStruct((1, GROUPS * many), f32),
+        in_specs=[vmem] * 7,
+        out_specs=vmem,
+        scratch_shapes=[wide, pltpu.VMEM((keys, GROUPS * many), f32)],
         compiler_params=params,
         name="row_stats",
     )(kpos, qpos, *q, kv)
@@ -259,36 +237,31 @@
     u = upstream, far, shift_by(upstream, ("c",), (1,)), shift_by(far, ("c",), (1,))
     stats = pl.pallas_call(
         delta_kernel,
-        grid=(GROUPS,),
-        out_shape=jax.ShapeDtypeStruct((GROUPS, 2, many), f32),
-        in_specs=places + [head_block] * 8 + [key_block, value_block, row_block],
-        out_specs=stats_block,
-        scratch_shapes=[bias],
+        out_shape=jax.ShapeDtypeStruct((2, GROUPS * many), f32),
+        in_specs=[vmem] * 12,
+        out_specs=vmem,
+        scratch_shapes=[wide, wide],
         compiler_params=params,
         name="row_delta",
-    )(kpos, qpos, *q, *u, kv, kv, lse)
+    )(kpos, qpos, *q, *u, kv, lse)
     stats_parts = everyone(stats)
 
-    wide = (rows, GROUPS * HEAD_DIM)
+    shape = (rows, GROUPS * HEAD_DIM)
     own, far, core, across, terms = pl.pallas_call(
         grad_kernel,
-        grid=(GROUPS,),
         out_shape=(
-            jax.ShapeDtypeStruct(wide, f32),
-            jax.ShapeDtypeStruct(wide, f32),
-            jax.ShapeDtypeStruct(wide, bf16),
-            jax.ShapeDtypeStruct(wide, bf16),
+            jax.ShapeDtypeStruct(shape, f32),
+            jax.ShapeDtypeStruct(shape, f32),
+            jax.ShapeDtypeStruct(shape, bf16),
+            jax.ShapeDtypeStruct(shape, bf16),
             jax.ShapeDtypeStruct((keys, 2 * HEAD_DIM), bf16),
         ),
-        in_specs=places
-        + [head_block] * 8
-        + [key_block, value_block]
-        + [stats_block] * 4,
-        out_specs=(head_block,) * 4 + (whole((keys, 2 * HEAD_DIM)),),
-        scratch_shapes=[bias, term_sum, term_sum, pltpu.VMEM((HEAD_DIM, keys), bf16)],
+        in_specs=[vmem] * 15,
+        out_specs=(vmem,) * 5,
+        scratch_shapes=[wide, wide, pltpu.VMEM((HEAD_DIM, GROUPS * many), f32)],
         compiler_params=params,
         name="gradients",
-    )(kpos, qpos, *q, *u, kv, kv, *stats_parts)
+    )(kpos, qpos, *q, *u, kv, *stats_parts)
 
     summed = lax.all_to_all(terms.reshape(nz, rows, 2 * HEAD_DIM), "z", 0, 0, tiled=True)
     summed = jnp.sum(summed.astype(f32), axis=0)

time: 87.2 us -> 84 us (0.963)
  Pallas kernels: 19.1 us -> 15 us
  waiting for transfers between devices: 26.9 us -> 28.5 us
    pallas_call x3, Pallas kernels: 15.6 us -> 11.5 us  [the longest x1 5.99 us: local(): pl.pallas_call(grad_kernel, out_shape=(jax.ShapeDtypeStruct(shape, f32),...]
    ppermute x16, waiting for transfers between devices: 19.5 us -> 21.1 us  [shift_by(): return lax.ppermute(value, axes, pairs)]
  transfers between devices with their start and end apart: 18 -> 18, of which waited for: 10 -> 11; matrix products, arithmetic and copies ran while one was open for 4% -> 4% of each run, Pallas kernels for 8% -> 8%
where the time goes in v4:
time: 84 us; the launch traced here: 83.6 us
  starting transfers between devices  33.6 us (40%)
  waiting for transfers between devices  28.5 us (34%)
  Pallas kernels  15 us (18%)
  local copies, waits for them, and re-layouts  3.93 us (5%)
  other arithmetic  1.87 us (2%)
    ppermute x16, waiting for transfers between devices, shift_by(): return lax.ppermute(value, axes, pairs)  21.1 us
    ppermute x16, starting transfers between devices, shift_by(): return lax.ppermute(value, axes, pairs)  17.9 us
    all_to_all x1, starting transfers between devices, local(): lax.all_to_all(jnp.broadcast_to(both[None], (nz, *both.shape)), 'z', 0, 0...  8.47 us
    all_to_all x1, waiting for transfers between devices, local(): lax.all_to_all(terms.reshape(nz, rows, 2 * HEAD_DIM), 'z', 0, 0, tiled=True)  7.39 us
    all_to_all x1, starting transfers between devices, local(): lax.all_to_all(terms.reshape(nz, rows, 2 * HEAD_DIM), 'z', 0, 0, tiled=True)  7.22 us
    pallas_call x1, Pallas kernels, local(): pl.pallas_call(grad_kernel, out_shape=(jax.ShapeDtypeStruct(shape, f32),...  5.99 us
    pallas_call x1, Pallas kernels, upstream_of(): pl.pallas_call(upstream_kernel, out_shape=jax.ShapeDtypeStruct((rows, col...  3.51 us
    pallas_call x1, Pallas kernels, local(): pl.pallas_call(stats_kernel, out_shape=jax.ShapeDtypeStruct((1, GROUPS *...  2.76 us
  transfers between devices with their start and end apart: 18, of which 11 were waited for; matrix products, arithmetic and copies ran while one was open for 4% of the time, Pallas kernels for 8%

profile of v4, /device:TPU:2, one launch (start us, length us, event | category | flops | bytes accessed | tf_op | source)
XLA Modules:
  0.0 83.6 jit_solution(8628049239353175955)
XLA Ops:
  0.6 0.8 pad_maximum_fusion
  1.4 0.8 %broadcast_in_dim.2 = bf16[8,128,256]{2,1,0:T(8,128)(2,1)} broadcast(bf16[128,256]{1,0:T(8,128)(2,1)S(1)} %pad_maximum_fusion), dimensions={1,2} | broadcast | bytes 589824 | tf_op jit(solution)/shard_map/broadcast_in_dim | solution.py:185
  2.3 8.5 %all-to-all-start = ((bf16[8,128,256]{2,1,0:T(8,128)(2,1)}), bf16[8,128,256]{2,1,0:T(8,128)(2,1)S(1)}, u32[]{:S(2)}, u32[]{:S(2)}) async-start(bf16[8,128,256]{2,1,0:T(8,128)(2,1)} %broadcast_in_dim.2), calls=%async_computation | async-start | bytes 1048576 | tf_op jit(solution)/shard_map/all_to_all | solution.py:184
  10.7 1.6 %collective-permute-start = (bf16[128,512]{1,0:T(8,128)(2,1)}, bf16[128,512]{1,0:T(8,128)(2,1)S(1)}, u32[]{:S(2)}, u32[]{:S(2)}) collective-permute-start(bf16[128,512]{1,0:T(8,128)(2,1)} %param.9), channel_id=1, source_target_pairs={{0,4},{4,0},{1,5},{5,1},{2,6},{6,2},{3,7},{7,3},{8,12},{12,8},{9,1... | collective-permute-start | bytes 393224 | tf_op jit(solution)/shard_map/ppermute | solution.py:44
  12.3 0.8 reshape.118
  13.1 0.9 %constant_dynamic-update-slice_fusion.1 = bf16[256,512]{1,0:T(8,128)(2,1)S(1)} fusion(bf16[128,512]{1,0:T(8,128)(2,1)} %param.9), kind=kLoop, calls=%fused_computation.6 | loop fusion | bytes 262144
  14.0 1.9 %collective-permute-done = bf16[128,512]{1,0:T(8,128)(2,1)S(1)} collective-permute-done((bf16[128,512]{1,0:T(8,128)(2,1)}, bf16[128,512]{1,0:T(8,128)(2,1)S(1)}, u32[]{:S(2)}, u32[]{:S(2)}) %collective-permute-start) | collective-permute-done | bytes 131104 | tf_op jit(solution)/shard_map/ppermute | solution.py:44
  15.9 2.2 %collective-permute-start.6 = (bf16[256,512]{1,0:T(8,128)(2,1)S(1)}, bf16[256,512]{1,0:T(8,128)(2,1)S(1)}, u32[]{:S(2)}, u32[]{:S(2)}) collective-permute-start(bf16[256,512]{1,0:T(8,128)(2,1)S(1)} %constant_dynamic-update-slice_fusion.refs_0_), channel_id=1, source_target_pairs={{0,2},{1,3},{2,0},{3,1},{4,6},{5,7},{6,4},{7,5},{8,10},{9,11},{10,... | collective-permute-start | bytes 786440 | tf_op jit(solution)/shard_map/ppermute | solution.py:44
  18.1 1.4 %collective-permute-start.5 = (bf16[256,512]{1,0:T(8,128)(2,1)S(1)}, bf16[256,512]{1,0:T(8,128)(2,1)S(1)}, u32[]{:S(2)}, u32[]{:S(2)}) collective-permute-start(bf16[256,512]{1,0:T(8,128)(2,1)S(1)} %constant_dynamic-update-slice_fusion.refs_0_), channel_id=1, source_target_pairs={{0,3},{1,0},{2,1},{3,2},{4,7},{5,4},{6,5},{7,6},{8,11},{9,8},{10,9... | collective-permute-start | bytes 786440 | tf_op jit(solution)/shard_map/ppermute | solution.py:44
  19.6 0.6 collective-permute-start.4
  20.2 0.1 add_multiply_fusion
  20.3 0.1 mul.32
  20.3 3.2 %collective-permute-start.1 = (bf16[128,512]{1,0:T(8,128)(2,1)}, bf16[128,512]{1,0:T(8,128)(2,1)S(1)}, u32[]{:S(2)}, u32[]{:S(2)}) collective-permute-start(bf16[128,512]{1,0:T(8,128)(2,1)} %q0.2), channel_id=1, source_target_pairs={{0,128},{128,0},{1,129},{129,1},{2,130},{130,2},{3,131},{131,3},{4... | collective-permute-start | bytes 393224 | tf_op jit(solution)/shard_map/ppermute | solution.py:44
  23.6 0.1 iota_add_fusion.1
  23.6 0.1 add.133.qpos
  23.7 0.1 stack.35.order
  23.8 0.0 collective-permute-start.2
  23.8 3.2 %collective-permute-done.1.q1 = bf16[128,512]{1,0:T(8,128)(2,1)S(1)} collective-permute-done((bf16[128,512]{1,0:T(8,128)(2,1)}, bf16[128,512]{1,0:T(8,128)(2,1)S(1)}, u32[]{:S(2)}, u32[]{:S(2)}) %collective-permute-start.1) | collective-permute-done | bytes 131104 | tf_op jit(solution)/shard_map/ppermute | solution.py:44
  27.1 0.0 collective-permute-start.3
  27.1 0.0 collective-permute-done.6.refs_3_
  27.1 2.7 %collective-permute-done.5.refs_2_ = bf16[256,512]{1,0:T(8,128)(2,1)S(1)} collective-permute-done((bf16[256,512]{1,0:T(8,128)(2,1)S(1)}, bf16[256,512]{1,0:T(8,128)(2,1)S(1)}, u32[]{:S(2)}, u32[]{:S(2)}) %collective-permute-start.5) | collective-permute-done | bytes 262176 | tf_op jit(solution)/shard_map/ppermute | solution.py:44
  29.7 0.1 collective-permute-done.4.refs_1_
  29.8 3.5 %upstream.1.u0 = bf16[128,512]{1,0:T(8,128)(2,1)S(1)} custom-call(s32[8]{0:T(128)S(1)} %stack.35.order, bf16[256,512]{1,0:T(8,128)(2,1)S(1)} %constant_dynamic-update-slice_fusion.refs_0_, bf16[256,512]{1,0:T(8,128)(2,1)S(1)} %collective-permute-done.4.refs_1_, bf16[256,512]{1,0:T(8,128)(2,1)S(1)} %collective-permute-done.5.refs_2_, ...), custom_call_target="tpu_custom_call" | custom-call | tf_op jit(solution)/shard_map/upstream/pallas_call | solution.py:157
  33.3 3.3 %collective-permute-start.7 = (bf16[128,512]{1,0:T(8,128)(2,1)S(1)}, bf16[128,512]{1,0:T(8,128)(2,1)S(1)}, u32[]{:S(2)}, u32[]{:S(2)}) collective-permute-start(bf16[128,512]{1,0:T(8,128)(2,1)S(1)} %upstream.1.u0), channel_id=1, source_target_pairs={{0,128},{128,0},{1,129},{129,1},{2,130},{130,2},{3,131},{131,3},{4... | collective-permute-start | bytes 393224 | tf_op jit(solution)/shard_map/ppermute | solution.py:44
  36.6 0.1 iota_add_fusion
  36.7 0.5 add.149.kpos
  37.2 0.1 collective-permute-start.8
  37.3 0.0 collective-permute-done.2.q2
  37.3 2.8 %row_stats.1.lse_ref = f32[1,2048]{1,0:T(1,128)S(1)} custom-call(s32[1024,1]{1,0:T(8,128)S(1)} %add.149.kpos, s32[1,512]{1,0:T(1,128)S(1)} %add.133.qpos, bf16[128,512]{1,0:T(8,128)(2,1)S(1)} %copy-done, bf16[128,512]{1,0:T(8,128)(2,1)S(1)} %collective-permute-done.1.q1, bf16[128,512]{1,0:T(8,128)(2,1)S(1)} %collective-permute-done.2.q2, ...), custom_call_target="tpu_custom_call" | custom-call | tf_op jit(solution)/shard_map/row_stats/pallas_call | solution.py:224
  40.1 0.2 collective-permute-done.7.u1
  40.3 0.6 collective-permute-start.9
  40.8 1.0 %collective-permute-done.9.u3 = bf16[128,512]{1,0:T(8,128)(2,1)S(1)} collective-permute-done((bf16[128,512]{1,0:T(8,128)(2,1)S(1)}, bf16[128,512]{1,0:T(8,128)(2,1)S(1)}, u32[]{:S(2)}, u32[]{:S(2)}) %collective-permute-start.9) | collective-permute-done | bytes 131104 | tf_op jit(solution)/shard_map/ppermute | solution.py:44
  41.8 2.8 %row_delta.1.s0 = f32[2,2048]{1,0:T(2,128)S(1)} custom-call(s32[1024,1]{1,0:T(8,128)S(1)} %add.149.kpos, s32[1,512]{1,0:T(1,128)S(1)} %add.133.qpos, bf16[128,512]{1,0:T(8,128)(2,1)S(1)} %copy-done, bf16[128,512]{1,0:T(8,128)(2,1)S(1)} %collective-permute-done.1.q1, bf16[128,512]{1,0:T(8,128)(2,1)S(1)} %collective-permute-done.2.q2, ...), custom_call_target="tpu_custom_call" | custom-call | tf_op jit(solution)/shard_map/row_delta/pallas_call | solution.py:238
  44.6 2.8 %collective-permute-start.12 = (f32[2,2048]{1,0:T(2,128)S(1)}, f32[2,2048]{1,0:T(2,128)S(1)}, u32[]{:S(2)}, u32[]{:S(2)}) collective-permute-start(f32[2,2048]{1,0:T(2,128)S(1)} %row_delta.1.s0), channel_id=1, source_target_pairs={{0,136},{8,128},{128,8},{136,0},{1,137},{9,129},{129,9},{137,1},{2... | collective-permute-start | bytes 49160 | tf_op jit(solution)/shard_map/ppermute | solution.py:44
  47.4 0.4 collective-permute-start.11
  47.8 0.5 collective-permute-start.10
  48.3 1.0 %collective-permute-done.12.s3 = f32[2,2048]{1,0:T(2,128)S(1)} collective-permute-done((f32[2,2048]{1,0:T(2,128)S(1)}, f32[2,2048]{1,0:T(2,128)S(1)}, u32[]{:S(2)}, u32[]{:S(2)}) %collective-permute-start.12) | collective-permute-done | bytes 16416 | tf_op jit(solution)/shard_map/ppermute | solution.py:44
  49.3 3.7 %collective-permute-done.10.s1 = f32[2,2048]{1,0:T(2,128)S(1)} collective-permute-done((f32[2,2048]{1,0:T(2,128)S(1)}, f32[2,2048]{1,0:T(2,128)S(1)}, u32[]{:S(2)}, u32[]{:S(2)}) %collective-permute-start.10) | collective-permute-done | bytes 16416 | tf_op jit(solution)/shard_map/ppermute | solution.py:44
  53.0 6.0 %gradients.1 = (f32[128,512]{1,0:T(8,128)S(1)}, f32[128,512]{1,0:T(8,128)S(1)}, bf16[128,512]{1,0:T(8,128)(2,1)S(1)}, bf16[128,512]{1,0:T(8,128)(2,1)S(1)}, bf16[1024,256]{1,0:T(8,128)(2,1)}) custom-call(s32[1024,1]{1,0:T(8,128)S(1)} %add.149.kpos, s32[1,512]{1,0:T(1,128)S(1)} %add.133.qpos, bf16[128,512]{1,0:T(8,128)(2,1)S(1)} %copy-done, ...), custom_call_target="tpu_custom_call" | custom-call | tf_op jit(solution)/shard_map/gradients/pallas_call | solution.py:250
  59.0 7.2 %all-to-all-start.1 = ((bf16[8,128,256]{2,1,0:T(8,128)(2,1)}), bf16[8,128,256]{2,1,0:T(8,128)(2,1)S(1)}, u32[]{:S(2)}, u32[]{:S(2)}) async-start(bf16[8,128,256]{2,1,0:T(8,128)(2,1)} %bitcast.13), calls=%async_computation.1 | async-start | bytes 1048576 | tf_op jit(solution)/shard_map/all_to_all | solution.py:266
  66.2 0.5 collective-permute-start.13
  66.7 0.8 %collective-permute-done.14 = bf16[128,512]{1,0:T(8,128)(2,1)S(1)} collective-permute-done((bf16[128,512]{1,0:T(8,128)(2,1)S(1)}, bf16[128,512]{1,0:T(8,128)(2,1)S(1)}, u32[]{:S(2)}, u32[]{:S(2)}) %collective-permute-start.14) | collective-permute-done | bytes 131104 | tf_op jit(solution)/shard_map/ppermute | solution.py:44
  67.6 0.6 collective-permute-start.15
  68.2 6.5 %collective-permute-done.15 = bf16[128,512]{1,0:T(8,128)(2,1)S(1)} collective-permute-done((bf16[128,512]{1,0:T(8,128)(2,1)S(1)}, bf16[128,512]{1,0:T(8,128)(2,1)S(1)}, u32[]{:S(2)}, u32[]{:S(2)}) %collective-permute-start.15) | collective-permute-done | bytes 131104 | tf_op jit(solution)/shard_map/ppermute | solution.py:44
  74.7 0.7 convert_add_fusion
  75.5 7.4 %all-to-all-done.1 = bf16[8,128,256]{2,1,0:T(8,128)(2,1)S(1)} async-done(((bf16[8,128,256]{2,1,0:T(8,128)(2,1)}), bf16[8,128,256]{2,1,0:T(8,128)(2,1)S(1)}, u32[]{:S(2)}, u32[]{:S(2)}) %all-to-all-start.1) | async-done | bytes 524320 | tf_op jit(solution)/shard_map/all_to_all | solution.py:266
  82.9 0.1 convert_reduce_fusion
  83.0 0.7 fusion.4
  (12 shorter events, 0.1 us)
Async XLA Ops:
  1.4 35.9 %copy-start = (bf16[128,512]{1,0:T(8,128)(2,1)S(1)}, bf16[128,512]{1,0:T(8,128)(2,1)}, u32[]{:S(2)}) copy-start(bf16[128,512]{1,0:T(8,128)(2,1)} %q0.2) | copy-start | bytes 393220
  2.3 35.0 %all-to-all-start = ((bf16[8,128,256]{2,1,0:T(8,128)(2,1)}), bf16[8,128,256]{2,1,0:T(8,128)(2,1)S(1)}, u32[]{:S(2)}, u32[]{:S(2)}) async-start(bf16[8,128,256]{2,1,0:T(8,128)(2,1)} %broadcast_in_dim.2), calls=%async_computation | async-start | bytes 1048576 | tf_op jit(solution)/shard_map/all_to_all | solution.py:184
  10.7 5.2 %collective-permute-start = (bf16[128,512]{1,0:T(8,128)(2,1)}, bf16[128,512]{1,0:T(8,128)(2,1)S(1)}, u32[]{:S(2)}, u32[]{:S(2)}) collective-permute-start(bf16[128,512]{1,0:T(8,128)(2,1)} %param.9), channel_id=1, source_target_pairs={{0,4},{4,0},{1,5},{5,1},{2,6},{6,2},{3,7},{7,3},{8,12},{12,8},{9,1... | collective-permute-start | bytes 393224 | tf_op jit(solution)/shard_map/ppermute | solution.py:44
  15.9 11.1 %collective-permute-start.6 = (bf16[256,512]{1,0:T(8,128)(2,1)S(1)}, bf16[256,512]{1,0:T(8,128)(2,1)S(1)}, u32[]{:S(2)}, u32[]{:S(2)}) collective-permute-start(bf16[256,512]{1,0:T(8,128)(2,1)S(1)} %constant_dynamic-update-slice_fusion.refs_0_), channel_id=1, source_target_pairs={{0,2},{1,3},{2,0},{3,1},{4,6},{5,7},{6,4},{7,5},{8,10},{9,11},{10,... | collective-permute-start | bytes 786440 | tf_op jit(solution)/shard_map/ppermute | solution.py:44
  18.1 11.6 %collective-permute-start.5 = (bf16[256,512]{1,0:T(8,128)(2,1)S(1)}, bf16[256,512]{1,0:T(8,128)(2,1)S(1)}, u32[]{:S(2)}, u32[]{:S(2)}) collective-permute-start(bf16[256,512]{1,0:T(8,128)(2,1)S(1)} %constant_dynamic-update-slice_fusion.refs_0_), channel_id=1, source_target_pairs={{0,3},{1,0},{2,1},{3,2},{4,7},{5,4},{6,5},{7,6},{8,11},{9,8},{10,9... | collective-permute-start | bytes 786440 | tf_op jit(solution)/shard_map/ppermute | solution.py:44
  19.6 10.3 %collective-permute-start.4 = (bf16[256,512]{1,0:T(8,128)(2,1)S(1)}, bf16[256,512]{1,0:T(8,128)(2,1)S(1)}, u32[]{:S(2)}, u32[]{:S(2)}) collective-permute-start(bf16[256,512]{1,0:T(8,128)(2,1)S(1)} %constant_dynamic-update-slice_fusion.refs_0_), channel_id=1, source_target_pairs={{0,1},{1,2},{2,3},{3,0},{4,5},{5,6},{6,7},{7,4},{8,9},{9,10},{10,1... | collective-permute-start | bytes 786440 | tf_op jit(solution)/shard_map/ppermute | solution.py:44
  20.3 6.7 %collective-permute-start.1 = (bf16[128,512]{1,0:T(8,128)(2,1)}, bf16[128,512]{1,0:T(8,128)(2,1)S(1)}, u32[]{:S(2)}, u32[]{:S(2)}) collective-permute-start(bf16[128,512]{1,0:T(8,128)(2,1)} %q0.2), channel_id=1, source_target_pairs={{0,128},{128,0},{1,129},{129,1},{2,130},{130,2},{3,131},{131,3},{4... | collective-permute-start | bytes 393224 | tf_op jit(solution)/shard_map/ppermute | solution.py:44
  23.8 13.5 %collective-permute-start.2 = (bf16[128,512]{1,0:T(8,128)(2,1)}, bf16[128,512]{1,0:T(8,128)(2,1)S(1)}, u32[]{:S(2)}, u32[]{:S(2)}) collective-permute-start(bf16[128,512]{1,0:T(8,128)(2,1)} %q0.2), channel_id=1, source_target_pairs={{0,8},{8,0},{1,9},{9,1},{2,10},{10,2},{3,11},{11,3},{4,12},{12,4},... | collective-permute-start | bytes 393224 | tf_op jit(solution)/shard_map/ppermute | solution.py:44
  27.1 10.2 %collective-permute-start.3 = (bf16[128,512]{1,0:T(8,128)(2,1)S(1)}, bf16[128,512]{1,0:T(8,128)(2,1)S(1)}, u32[]{:S(2)}, u32[]{:S(2)}) collective-permute-start(bf16[128,512]{1,0:T(8,128)(2,1)S(1)} %collective-permute-done.1.q1), channel_id=1, source_target_pairs={{0,8},{8,0},{1,9},{9,1},{2,10},{10,2},{3,11},{11,3},{4,12},{12,4},... | collective-permute-start | bytes 393224 | tf_op jit(solution)/shard_map/ppermute | solution.py:44
  33.3 6.9 %collective-permute-start.7 = (bf16[128,512]{1,0:T(8,128)(2,1)S(1)}, bf16[128,512]{1,0:T(8,128)(2,1)S(1)}, u32[]{:S(2)}, u32[]{:S(2)}) collective-permute-start(bf16[128,512]{1,0:T(8,128)(2,1)S(1)} %upstream.1.u0), channel_id=1, source_target_pairs={{0,128},{128,0},{1,129},{129,1},{2,130},{130,2},{3,131},{131,3},{4... | collective-permute-start | bytes 393224 | tf_op jit(solution)/shard_map/ppermute | solution.py:44
  37.2 3.7 %collective-permute-start.8 = (bf16[128,512]{1,0:T(8,128)(2,1)S(1)}, bf16[128,512]{1,0:T(8,128)(2,1)S(1)}, u32[]{:S(2)}, u32[]{:S(2)}) collective-permute-start(bf16[128,512]{1,0:T(8,128)(2,1)S(1)} %upstream.1.u0), channel_id=1, source_target_pairs={{0,8},{8,0},{1,9},{9,1},{2,10},{10,2},{3,11},{11,3},{4,12},{12,4},... | collective-permute-start | bytes 393224 | tf_op jit(solution)/shard_map/ppermute | solution.py:44
  40.3 1.5 %collective-permute-start.9 = (bf16[128,512]{1,0:T(8,128)(2,1)S(1)}, bf16[128,512]{1,0:T(8,128)(2,1)S(1)}, u32[]{:S(2)}, u32[]{:S(2)}) collective-permute-start(bf16[128,512]{1,0:T(8,128)(2,1)S(1)} %collective-permute-done.7.u1), channel_id=1, source_target_pairs={{0,8},{8,0},{1,9},{9,1},{2,10},{10,2},{3,11},{11,3},{4,12},{12,4},... | collective-permute-start | bytes 393224 | tf_op jit(solution)/shard_map/ppermute | solution.py:44
  44.6 4.8 %collective-permute-start.12 = (f32[2,2048]{1,0:T(2,128)S(1)}, f32[2,2048]{1,0:T(2,128)S(1)}, u32[]{:S(2)}, u32[]{:S(2)}) collective-permute-start(f32[2,2048]{1,0:T(2,128)S(1)} %row_delta.1.s0), channel_id=1, source_target_pairs={{0,136},{8,128},{128,8},{136,0},{1,137},{9,129},{129,9},{137,1},{2... | collective-permute-start | bytes 49160 | tf_op jit(solution)/shard_map/ppermute | solution.py:44
  47.4 1.9 %collective-permute-start.11 = (f32[2,2048]{1,0:T(2,128)S(1)}, f32[2,2048]{1,0:T(2,128)S(1)}, u32[]{:S(2)}, u32[]{:S(2)}) collective-permute-start(f32[2,2048]{1,0:T(2,128)S(1)} %row_delta.1.s0), channel_id=1, source_target_pairs={{0,8},{8,0},{1,9},{9,1},{2,10},{10,2},{3,11},{11,3},{4,12},{12,4},... | collective-permute-start | bytes 49160 | tf_op jit(solution)/shard_map/ppermute | solution.py:44
  47.8 5.2 %collective-permute-start.10 = (f32[2,2048]{1,0:T(2,128)S(1)}, f32[2,2048]{1,0:T(2,128)S(1)}, u32[]{:S(2)}, u32[]{:S(2)}) collective-permute-start(f32[2,2048]{1,0:T(2,128)S(1)} %row_delta.1.s0), channel_id=1, source_target_pairs={{0,128},{128,0},{1,129},{129,1},{2,130},{130,2},{3,131},{131,3},{4... | collective-permute-start | bytes 49160 | tf_op jit(solution)/shard_map/ppermute | solution.py:44
  59.0 23.9 %all-to-all-start.1 = ((bf16[8,128,256]{2,1,0:T(8,128)(2,1)}), bf16[8,128,256]{2,1,0:T(8,128)(2,1)S(1)}, u32[]{:S(2)}, u32[]{:S(2)}) async-start(bf16[8,128,256]{2,1,0:T(8,128)(2,1)} %bitcast.13), calls=%async_computation.1 | async-start | bytes 1048576 | tf_op jit(solution)/shard_map/all_to_all | solution.py:266
  66.2 1.3 %collective-permute-start.14 = (bf16[128,512]{1,0:T(8,128)(2,1)S(1)}, bf16[128,512]{1,0:T(8,128)(2,1)S(1)}, u32[]{:S(2)}, u32[]{:S(2)}) collective-permute-start(bf16[128,512]{1,0:T(8,128)(2,1)S(1)} %get-tuple-element.17), channel_id=1, source_target_pairs={{0,8},{8,0},{1,9},{9,1},{2,10},{10,2},{3,11},{11,3},{4,12},{12,4},... | collective-permute-start | bytes 393224 | tf_op jit(solution)/shard_map/ppermute | solution.py:44
  66.2 2.0 %collective-permute-start.13 = (bf16[128,512]{1,0:T(8,128)(2,1)S(1)}, bf16[128,512]{1,0:T(8,128)(2,1)S(1)}, u32[]{:S(2)}, u32[]{:S(2)}) collective-permute-start(bf16[128,512]{1,0:T(8,128)(2,1)S(1)} %get-tuple-element.15), channel_id=1, source_target_pairs={{0,8},{8,0},{1,9},{9,1},{2,10},{10,2},{3,11},{11,3},{4,12},{12,4},... | collective-permute-start | bytes 393224 | tf_op jit(solution)/shard_map/ppermute | solution.py:44
  67.6 7.1 %collective-permute-start.15 = (bf16[128,512]{1,0:T(8,128)(2,1)S(1)}, bf16[128,512]{1,0:T(8,128)(2,1)S(1)}, u32[]{:S(2)}, u32[]{:S(2)}) collective-permute-start(bf16[128,512]{1,0:T(8,128)(2,1)S(1)} %add_convert_fusion), channel_id=1, source_target_pairs={{0,128},{128,0},{1,129},{129,1},{2,130},{130,2},{3,131},{131,3},{4... | collective-permute-start | bytes 393224 | tf_op jit(solution)/shard_map/ppermute | solution.py:44

commit v5 on v4

--- a/solution.py
+++ b/solution.py
@@ -170,6 +170,26 @@
     )(order, *parts, pltpu.with_memory_space_constraint(o_weight, pltpu.HBM))
 
 
+def pack_kernel(k, v, out):
+    rows = k.shape[0]
+    for at in range(0, out.shape[0], rows):
+        out[at : at + rows, :HEAD_DIM] = k[...]
+        out[at : at + rows, HEAD_DIM:] = v[...]
+
+
+def packed(key_states, value_states, copies):
+    rows, width = key_states.shape
+    vmem = pl.BlockSpec(memory_space=pltpu.VMEM)
+    return pl.pallas_call(
+        pack_kernel,
+        out_shape=jax.ShapeDtypeStruct((copies * rows, 2 * width), key_states.dtype),
+        in_specs=[vmem, vmem],
+        out_specs=vmem,
+        cost_estimate=pl.CostEstimate(flops=0, transcendentals=0, bytes_accessed=12 * key_states.size),
+        name="pack",
+    )(key_states, value_states)
+
+
 def local(queries, key_states, value_states, out_grad, o_weight, span_order):
     rows = queries.shape[0]
     nz = lax.axis_size("z")
@@ -180,10 +200,8 @@
     yh, z, c = lax.axis_index("yh"), lax.axis_index("z"), lax.axis_index("c")
     yl, x = lax.axis_index("yl"), lax.axis_index("x")
 
-    both = jnp.concatenate((key_states, value_states), axis=1)
-    kv = lax.all_to_all(
-        jnp.broadcast_to(both[None], (nz, *both.shape)), "z", 0, 0, tiled=True
-    ).reshape(keys, 2 * HEAD_DIM)
+    both = packed(key_states, value_states, nz).reshape(nz, rows, 2 * HEAD_DIM)
+    kv = lax.all_to_all(both, "z", 0, 0, tiled=True).reshape(keys, 2 * HEAD_DIM)
 
     pair = jnp.concatenate((out_grad, shift_by(out_grad, ("yl",), (1,))), axis=0)
     parts, sources = [], []
@@ -219,7 +237,7 @@
     wide = pltpu.VMEM((GROUPS * many, HEAD_DIM), bf16)
     params = pltpu.CompilerParams(vmem_limit_bytes=VMEM_LIMIT)
 
-    held, pair = lax.optimization_barrier((queries, pair))
+    held, pair, kpos, qpos = lax.optimization_barrier((queries, pair, kpos, qpos))
     q = shared(held)
     lse = pl.pallas_call(
         stats_kernel,

time: 84 us -> 83 us (0.988)
  Pallas kernels: 15 us -> 16.8 us
  starting transfers between devices: 33.6 us -> 32.3 us
  local copies, waits for them, and re-layouts: 3.93 us -> 2.92 us
    pallas_call x0 -> x1, Pallas kernels: none -> 1.65 us  [packed(): pl.pallas_call(pack_kernel, out_shape=jax.ShapeDtypeStruct((copies * rows...]
    ppermute x16, starting transfers between devices: 17.9 us -> 16.9 us  [shift_by(): return lax.ppermute(value, axes, pairs)]
    broadcast_in_dim x1 -> x0, local copies, waits for them, and re-layouts: 0.84 us -> none  [local(): jnp.broadcast_to(both[None], (nz, *both.shape))]
  transfers between devices with their start and end apart: 18 -> 18, of which waited for: 11 -> 10; matrix products, arithmetic and copies ran while one was open for 4% -> 4% of each run, Pallas kernels for 8% -> 10%
where the time goes in v5:
time: 83 us; the launch traced here: 82.6 us
  starting transfers between devices  32.3 us (39%)
  waiting for transfers between devices  28.8 us (35%)
  Pallas kernels  16.8 us (20%)
  local copies, waits for them, and re-layouts  2.92 us (4%)
  other arithmetic  1.08 us (1%)
    ppermute x16, waiting for transfers between devices, shift_by(): return lax.ppermute(value, axes, pairs)  21.4 us
    ppermute x16, starting transfers between devices, shift_by(): return lax.ppermute(value, axes, pairs)  16.9 us
    all_to_all x1, starting transfers between devices, local(): kv = lax.all_to_all(both, 'z', 0, 0, tiled=True).reshape(keys, 2 * HEAD_DIM)  8.47 us
    all_to_all x1, waiting for transfers between devices, local(): lax.all_to_all(terms.reshape(nz, rows, 2 * HEAD_DIM), 'z', 0, 0, tiled=True)  7.4 us
    all_to_all x1, starting transfers between devices, local(): lax.all_to_all(terms.reshape(nz, rows, 2 * HEAD_DIM), 'z', 0, 0, tiled=True)  6.93 us
    pallas_call x1, Pallas kernels, local(): pl.pallas_call(grad_kernel, out_shape=(jax.ShapeDtypeStruct(shape, f32),...  6.04 us
    pallas_call x1, Pallas kernels, upstream_of(): pl.pallas_call(upstream_kernel, out_shape=jax.ShapeDtypeStruct((rows, col...  3.51 us
    pallas_call x1, Pallas kernels, local(): pl.pallas_call(delta_kernel, out_shape=jax.ShapeDtypeStruct((2, GROUPS *...  2.82 us
  transfers between devices with their start and end apart: 18, of which 10 were waited for; matrix products, arithmetic and copies ran while one was open for 4% of the time, Pallas kernels for 10%

profile of v5, /device:TPU:2, one launch (start us, length us, event | category | flops | bytes accessed | tf_op | source)
XLA Modules:
  0.0 82.6 jit_solution(9835525657746466621)
XLA Ops:
  0.6 0.0 copy-start
  0.6 1.7 %collective-permute-start = (bf16[128,512]{1,0:T(8,128)(2,1)}, bf16[128,512]{1,0:T(8,128)(2,1)S(1)}, u32[]{:S(2)}, u32[]{:S(2)}) collective-permute-start(bf16[128,512]{1,0:T(8,128)(2,1)} %param.9), channel_id=1, source_target_pairs={{0,4},{4,0},{1,5},{5,1},{2,6},{6,2},{3,7},{7,3},{8,12},{12,8},{9,1... | collective-permute-start | bytes 393224 | tf_op jit(solution)/shard_map/ppermute | solution.py:44
  2.3 1.6 %pack.1 = bf16[1024,256]{1,0:T(8,128)(2,1)} custom-call(bf16[128,128]{1,0:T(8,128)(2,1)} %k.1, bf16[128,128]{1,0:T(8,128)(2,1)} %v.1), custom_call_target="tpu_custom_call" | custom-call | bytes 196608 | tf_op jit(solution)/shard_map/pack/pallas_call | solution.py:183
  4.0 8.5 %all-to-all-start = ((bf16[8,128,256]{2,1,0:T(8,128)(2,1)}), bf16[8,128,256]{2,1,0:T(8,128)(2,1)S(1)}, u32[]{:S(2)}, u32[]{:S(2)}) async-start(bf16[8,128,256]{2,1,0:T(8,128)(2,1)} %bitcast.22), calls=%async_computation | async-start | bytes 1048576 | tf_op jit(solution)/shard_map/all_to_all | solution.py:204
  12.4 0.8 reshape.120
  13.2 0.1 add_multiply_fusion
  13.3 0.1 iota_add_fusion.1
  13.4 0.1 mul.32
  13.5 0.1 add.133.qpos
  13.6 0.9 %constant_dynamic-update-slice_fusion.1 = bf16[256,512]{1,0:T(8,128)(2,1)S(1)} fusion(bf16[128,512]{1,0:T(8,128)(2,1)} %param.9), kind=kLoop, calls=%fused_computation.5 | loop fusion | bytes 262144
  14.5 2.2 %collective-permute-start.6 = (bf16[256,512]{1,0:T(8,128)(2,1)S(1)}, bf16[256,512]{1,0:T(8,128)(2,1)S(1)}, u32[]{:S(2)}, u32[]{:S(2)}) collective-permute-start(bf16[256,512]{1,0:T(8,128)(2,1)S(1)} %constant_dynamic-update-slice_fusion.refs_0_), channel_id=1, source_target_pairs={{0,2},{1,3},{2,0},{3,1},{4,6},{5,7},{6,4},{7,5},{8,10},{9,11},{10,... | collective-permute-start | bytes 786440 | tf_op jit(solution)/shard_map/ppermute | solution.py:44
  16.7 1.4 %collective-permute-start.5 = (bf16[256,512]{1,0:T(8,128)(2,1)S(1)}, bf16[256,512]{1,0:T(8,128)(2,1)S(1)}, u32[]{:S(2)}, u32[]{:S(2)}) collective-permute-start(bf16[256,512]{1,0:T(8,128)(2,1)S(1)} %constant_dynamic-update-slice_fusion.refs_0_), channel_id=1, source_target_pairs={{0,3},{1,0},{2,1},{3,2},{4,7},{5,4},{6,5},{7,6},{8,11},{9,8},{10,9... | collective-permute-start | bytes 786440 | tf_op jit(solution)/shard_map/ppermute | solution.py:44
  18.2 0.6 collective-permute-start.4
  18.7 0.1 iota_add_fusion
  18.8 0.1 add.126
  18.9 2.9 %collective-permute-start.1 = (bf16[128,512]{1,0:T(8,128)(2,1)}, bf16[128,512]{1,0:T(8,128)(2,1)S(1)}, u32[]{:S(2)}, u32[]{:S(2)}) collective-permute-start(bf16[128,512]{1,0:T(8,128)(2,1)} %q0.2), channel_id=1, source_target_pairs={{0,128},{128,0},{1,129},{129,1},{2,130},{130,2},{3,131},{131,3},{4... | collective-permute-start | bytes 393224 | tf_op jit(solution)/shard_map/ppermute | solution.py:44
  21.8 0.1 stack.35.order
  21.9 0.0 collective-permute-start.2
  21.9 3.7 %collective-permute-done.1.q1 = bf16[128,512]{1,0:T(8,128)(2,1)S(1)} collective-permute-done((bf16[128,512]{1,0:T(8,128)(2,1)}, bf16[128,512]{1,0:T(8,128)(2,1)S(1)}, u32[]{:S(2)}, u32[]{:S(2)}) %collective-permute-start.1) | collective-permute-done | bytes 131104 | tf_op jit(solution)/shard_map/ppermute | solution.py:44
  25.6 0.0 collective-permute-done.6.refs_3_
  25.6 3.6 %collective-permute-done.5.refs_2_ = bf16[256,512]{1,0:T(8,128)(2,1)S(1)} collective-permute-done((bf16[256,512]{1,0:T(8,128)(2,1)S(1)}, bf16[256,512]{1,0:T(8,128)(2,1)S(1)}, u32[]{:S(2)}, u32[]{:S(2)}) %collective-permute-start.5) | collective-permute-done | bytes 262176 | tf_op jit(solution)/shard_map/ppermute | solution.py:44
  29.2 0.1 collective-permute-done.4.refs_1_
  29.3 3.5 %upstream.1.u0 = bf16[128,512]{1,0:T(8,128)(2,1)S(1)} custom-call(s32[8]{0:T(128)S(1)} %stack.35.order, bf16[256,512]{1,0:T(8,128)(2,1)S(1)} %constant_dynamic-update-slice_fusion.refs_0_, bf16[256,512]{1,0:T(8,128)(2,1)S(1)} %collective-permute-done.4.refs_1_, bf16[256,512]{1,0:T(8,128)(2,1)S(1)} %collective-permute-done.5.refs_2_, ...), custom_call_target="tpu_custom_call" | custom-call | tf_op jit(solution)/shard_map/upstream/pallas_call | solution.py:157
  32.8 3.0 %collective-permute-start.7 = (bf16[128,512]{1,0:T(8,128)(2,1)S(1)}, bf16[128,512]{1,0:T(8,128)(2,1)S(1)}, u32[]{:S(2)}, u32[]{:S(2)}) collective-permute-start(bf16[128,512]{1,0:T(8,128)(2,1)S(1)} %upstream.1.u0), channel_id=1, source_target_pairs={{0,128},{128,0},{1,129},{129,1},{2,130},{130,2},{3,131},{131,3},{4... | collective-permute-start | bytes 393224 | tf_op jit(solution)/shard_map/ppermute | solution.py:44
  35.8 0.2 copy.11.kpos
  36.0 0.1 collective-permute-start.8
  36.1 0.0 collective-permute-done.2.q2
  36.1 2.8 %row_stats.1.lse_ref = f32[1,2048]{1,0:T(1,128)S(1)} custom-call(s32[1024,1]{1,0:T(8,128)S(1)} %copy.11.kpos, s32[1,512]{1,0:T(1,128)S(1)} %add.133.qpos, bf16[128,512]{1,0:T(8,128)(2,1)S(1)} %copy-done, bf16[128,512]{1,0:T(8,128)(2,1)S(1)} %collective-permute-done.1.q1, bf16[128,512]{1,0:T(8,128)(2,1)S(1)} %collective-permute-done.2.q2, ...), custom_call_target="tpu_custom_call" | custom-call | tf_op jit(solution)/shard_map/row_stats/pallas_call | solution.py:242
  38.9 0.8 collective-permute-done.7.u1
  39.7 0.0 collective-permute-start.9
  39.7 0.0 collective-permute-done.8.u2
  39.7 1.3 %collective-permute-done.9.u3 = bf16[128,512]{1,0:T(8,128)(2,1)S(1)} collective-permute-done((bf16[128,512]{1,0:T(8,128)(2,1)S(1)}, bf16[128,512]{1,0:T(8,128)(2,1)S(1)}, u32[]{:S(2)}, u32[]{:S(2)}) %collective-permute-start.9) | collective-permute-done | bytes 131104 | tf_op jit(solution)/shard_map/ppermute | solution.py:44
  41.1 2.8 %row_delta.1.s0 = f32[2,2048]{1,0:T(2,128)S(1)} custom-call(s32[1024,1]{1,0:T(8,128)S(1)} %copy.11.kpos, s32[1,512]{1,0:T(1,128)S(1)} %add.133.qpos, bf16[128,512]{1,0:T(8,128)(2,1)S(1)} %copy-done, bf16[128,512]{1,0:T(8,128)(2,1)S(1)} %collective-permute-done.1.q1, bf16[128,512]{1,0:T(8,128)(2,1)S(1)} %collective-permute-done.2.q2, ...), custom_call_target="tpu_custom_call" | custom-call | tf_op jit(solution)/shard_map/row_delta/pallas_call | solution.py:256
  43.9 2.7 %collective-permute-start.12 = (f32[2,2048]{1,0:T(2,128)S(1)}, f32[2,2048]{1,0:T(2,128)S(1)}, u32[]{:S(2)}, u32[]{:S(2)}) collective-permute-start(f32[2,2048]{1,0:T(2,128)S(1)} %row_delta.1.s0), channel_id=1, source_target_pairs={{0,136},{8,128},{128,8},{136,0},{1,137},{9,129},{129,9},{137,1},{2... | collective-permute-start | bytes 49160 | tf_op jit(solution)/shard_map/ppermute | solution.py:44
  46.6 0.4 collective-permute-start.11
  47.0 0.6 collective-permute-start.10
  47.6 1.0 %collective-permute-done.12.s3 = f32[2,2048]{1,0:T(2,128)S(1)} collective-permute-done((f32[2,2048]{1,0:T(2,128)S(1)}, f32[2,2048]{1,0:T(2,128)S(1)}, u32[]{:S(2)}, u32[]{:S(2)}) %collective-permute-start.12) | collective-permute-done | bytes 16416 | tf_op jit(solution)/shard_map/ppermute | solution.py:44
  48.7 3.6 %collective-permute-done.10.s1 = f32[2,2048]{1,0:T(2,128)S(1)} collective-permute-done((f32[2,2048]{1,0:T(2,128)S(1)}, f32[2,2048]{1,0:T(2,128)S(1)}, u32[]{:S(2)}, u32[]{:S(2)}) %collective-permute-start.10) | collective-permute-done | bytes 16416 | tf_op jit(solution)/shard_map/ppermute | solution.py:44
  52.3 6.0 %gradients.1 = (f32[128,512]{1,0:T(8,128)S(1)}, f32[128,512]{1,0:T(8,128)S(1)}, bf16[128,512]{1,0:T(8,128)(2,1)S(1)}, bf16[128,512]{1,0:T(8,128)(2,1)S(1)}, bf16[1024,256]{1,0:T(8,128)(2,1)}) custom-call(s32[1024,1]{1,0:T(8,128)S(1)} %copy.11.kpos, s32[1,512]{1,0:T(1,128)S(1)} %add.133.qpos, bf16[128,512]{1,0:T(8,128)(2,1)S(1)} %copy-done, ...), custom_call_target="tpu_custom_call" | custom-call | tf_op jit(solution)/shard_map/gradients/pallas_call | solution.py:268
  58.3 6.9 %all-to-all-start.1 = ((bf16[8,128,256]{2,1,0:T(8,128)(2,1)}), bf16[8,128,256]{2,1,0:T(8,128)(2,1)S(1)}, u32[]{:S(2)}, u32[]{:S(2)}) async-start(bf16[8,128,256]{2,1,0:T(8,128)(2,1)} %bitcast.14), calls=%async_computation.1 | async-start | bytes 1048576 | tf_op jit(solution)/shard_map/all_to_all | solution.py:284
  65.2 0.5 collective-permute-start.13
  65.7 0.8 %collective-permute-done.14 = bf16[128,512]{1,0:T(8,128)(2,1)S(1)} collective-permute-done((bf16[128,512]{1,0:T(8,128)(2,1)S(1)}, bf16[128,512]{1,0:T(8,128)(2,1)S(1)}, u32[]{:S(2)}, u32[]{:S(2)}) %collective-permute-start.14) | collective-permute-done | bytes 131104 | tf_op jit(solution)/shard_map/ppermute | solution.py:44
  66.6 0.7 collective-permute-start.15
  67.3 6.4 %collective-permute-done.15 = bf16[128,512]{1,0:T(8,128)(2,1)S(1)} collective-permute-done((bf16[128,512]{1,0:T(8,128)(2,1)S(1)}, bf16[128,512]{1,0:T(8,128)(2,1)S(1)}, u32[]{:S(2)}, u32[]{:S(2)}) %collective-permute-start.15) | collective-permute-done | bytes 131104 | tf_op jit(solution)/shard_map/ppermute | solution.py:44
  73.7 0.7 convert_add_fusion
  74.5 7.4 %all-to-all-done.1 = bf16[8,128,256]{2,1,0:T(8,128)(2,1)S(1)} async-done(((bf16[8,128,256]{2,1,0:T(8,128)(2,1)}), bf16[8,128,256]{2,1,0:T(8,128)(2,1)S(1)}, u32[]{:S(2)}, u32[]{:S(2)}) %all-to-all-start.1) | async-done | bytes 524320 | tf_op jit(solution)/shard_map/all_to_all | solution.py:284
  81.9 0.1 convert_reduce_fusion
  82.0 0.7 fusion.4
  (12 shorter events, 0.1 us)
Async XLA Ops:
  0.6 35.5 %copy-start = (bf16[128,512]{1,0:T(8,128)(2,1)S(1)}, bf16[128,512]{1,0:T(8,128)(2,1)}, u32[]{:S(2)}) copy-start(bf16[128,512]{1,0:T(8,128)(2,1)} %q0.2) | copy-start | bytes 393220
  0.6 13.8 %collective-permute-start = (bf16[128,512]{1,0:T(8,128)(2,1)}, bf16[128,512]{1,0:T(8,128)(2,1)S(1)}, u32[]{:S(2)}, u32[]{:S(2)}) collective-permute-start(bf16[128,512]{1,0:T(8,128)(2,1)} %param.9), channel_id=1, source_target_pairs={{0,4},{4,0},{1,5},{5,1},{2,6},{6,2},{3,7},{7,3},{8,12},{12,8},{9,1... | collective-permute-start | bytes 393224 | tf_op jit(solution)/shard_map/ppermute | solution.py:44
  4.0 32.2 %all-to-all-start = ((bf16[8,128,256]{2,1,0:T(8,128)(2,1)}), bf16[8,128,256]{2,1,0:T(8,128)(2,1)S(1)}, u32[]{:S(2)}, u32[]{:S(2)}) async-start(bf16[8,128,256]{2,1,0:T(8,128)(2,1)} %bitcast.22), calls=%async_computation | async-start | bytes 1048576 | tf_op jit(solution)/shard_map/all_to_all | solution.py:204
  14.5 11.1 %collective-permute-start.6 = (bf16[256,512]{1,0:T(8,128)(2,1)S(1)}, bf16[256,512]{1,0:T(8,128)(2,1)S(1)}, u32[]{:S(2)}, u32[]{:S(2)}) collective-permute-start(bf16[256,512]{1,0:T(8,128)(2,1)S(1)} %constant_dynamic-update-slice_fusion.refs_0_), channel_id=1, source_target_pairs={{0,2},{1,3},{2,0},{3,1},{4,6},{5,7},{6,4},{7,5},{8,10},{9,11},{10,... | collective-permute-start | bytes 786440 | tf_op jit(solution)/shard_map/ppermute | solution.py:44
  16.7 12.5 %collective-permute-start.5 = (bf16[256,512]{1,0:T(8,128)(2,1)S(1)}, bf16[256,512]{1,0:T(8,128)(2,1)S(1)}, u32[]{:S(2)}, u32[]{:S(2)}) collective-permute-start(bf16[256,512]{1,0:T(8,128)(2,1)S(1)} %constant_dynamic-update-slice_fusion.refs_0_), channel_id=1, source_target_pairs={{0,3},{1,0},{2,1},{3,2},{4,7},{5,4},{6,5},{7,6},{8,11},{9,8},{10,9... | collective-permute-start | bytes 786440 | tf_op jit(solution)/shard_map/ppermute | solution.py:44
  18.2 11.1 %collective-permute-start.4 = (bf16[256,512]{1,0:T(8,128)(2,1)S(1)}, bf16[256,512]{1,0:T(8,128)(2,1)S(1)}, u32[]{:S(2)}, u32[]{:S(2)}) collective-permute-start(bf16[256,512]{1,0:T(8,128)(2,1)S(1)} %constant_dynamic-update-slice_fusion.refs_0_), channel_id=1, source_target_pairs={{0,1},{1,2},{2,3},{3,0},{4,5},{5,6},{6,7},{7,4},{8,9},{9,10},{10,1... | collective-permute-start | bytes 786440 | tf_op jit(solution)/shard_map/ppermute | solution.py:44
  18.9 6.7 %collective-permute-start.1 = (bf16[128,512]{1,0:T(8,128)(2,1)}, bf16[128,512]{1,0:T(8,128)(2,1)S(1)}, u32[]{:S(2)}, u32[]{:S(2)}) collective-permute-start(bf16[128,512]{1,0:T(8,128)(2,1)} %q0.2), channel_id=1, source_target_pairs={{0,128},{128,0},{1,129},{129,1},{2,130},{130,2},{3,131},{131,3},{4... | collective-permute-start | bytes 393224 | tf_op jit(solution)/shard_map/ppermute | solution.py:44
  21.9 14.2 %collective-permute-start.2 = (bf16[128,512]{1,0:T(8,128)(2,1)}, bf16[128,512]{1,0:T(8,128)(2,1)S(1)}, u32[]{:S(2)}, u32[]{:S(2)}) collective-permute-start(bf16[128,512]{1,0:T(8,128)(2,1)} %q0.2), channel_id=1, source_target_pairs={{0,8},{8,0},{1,9},{9,1},{2,10},{10,2},{3,11},{11,3},{4,12},{12,4},... | collective-permute-start | bytes 393224 | tf_op jit(solution)/shard_map/ppermute | solution.py:44
  25.6 10.5 %collective-permute-start.3 = (bf16[128,512]{1,0:T(8,128)(2,1)S(1)}, bf16[128,512]{1,0:T(8,128)(2,1)S(1)}, u32[]{:S(2)}, u32[]{:S(2)}) collective-permute-start(bf16[128,512]{1,0:T(8,128)(2,1)S(1)} %collective-permute-done.1.q1), channel_id=1, source_target_pairs={{0,8},{8,0},{1,9},{9,1},{2,10},{10,2},{3,11},{11,3},{4,12},{12,4},... | collective-permute-start | bytes 393224 | tf_op jit(solution)/shard_map/ppermute | solution.py:44
  32.8 6.9 %collective-permute-start.7 = (bf16[128,512]{1,0:T(8,128)(2,1)S(1)}, bf16[128,512]{1,0:T(8,128)(2,1)S(1)}, u32[]{:S(2)}, u32[]{:S(2)}) collective-permute-start(bf16[128,512]{1,0:T(8,128)(2,1)S(1)} %upstream.1.u0), channel_id=1, source_target_pairs={{0,128},{128,0},{1,129},{129,1},{2,130},{130,2},{3,131},{131,3},{4... | collective-permute-start | bytes 393224 | tf_op jit(solution)/shard_map/ppermute | solution.py:44
  36.0 3.7 %collective-permute-start.8 = (bf16[128,512]{1,0:T(8,128)(2,1)S(1)}, bf16[128,512]{1,0:T(8,128)(2,1)S(1)}, u32[]{:S(2)}, u32[]{:S(2)}) collective-permute-start(bf16[128,512]{1,0:T(8,128)(2,1)S(1)} %upstream.1.u0), channel_id=1, source_target_pairs={{0,8},{8,0},{1,9},{9,1},{2,10},{10,2},{3,11},{11,3},{4,12},{12,4},... | collective-permute-start | bytes 393224 | tf_op jit(solution)/shard_map/ppermute | solution.py:44
  39.7 1.3 %collective-permute-start.9 = (bf16[128,512]{1,0:T(8,128)(2,1)S(1)}, bf16[128,512]{1,0:T(8,128)(2,1)S(1)}, u32[]{:S(2)}, u32[]{:S(2)}) collective-permute-start(bf16[128,512]{1,0:T(8,128)(2,1)S(1)} %collective-permute-done.7.u1), channel_id=1, source_target_pairs={{0,8},{8,0},{1,9},{9,1},{2,10},{10,2},{3,11},{11,3},{4,12},{12,4},... | collective-permute-start | bytes 393224 | tf_op jit(solution)/shard_map/ppermute | solution.py:44
  43.9 4.8 %collective-permute-start.12 = (f32[2,2048]{1,0:T(2,128)S(1)}, f32[2,2048]{1,0:T(2,128)S(1)}, u32[]{:S(2)}, u32[]{:S(2)}) collective-permute-start(f32[2,2048]{1,0:T(2,128)S(1)} %row_delta.1.s0), channel_id=1, source_target_pairs={{0,136},{8,128},{128,8},{136,0},{1,137},{9,129},{129,9},{137,1},{2... | collective-permute-start | bytes 49160 | tf_op jit(solution)/shard_map/ppermute | solution.py:44
  46.6 2.0 %collective-permute-start.11 = (f32[2,2048]{1,0:T(2,128)S(1)}, f32[2,2048]{1,0:T(2,128)S(1)}, u32[]{:S(2)}, u32[]{:S(2)}) collective-permute-start(f32[2,2048]{1,0:T(2,128)S(1)} %row_delta.1.s0), channel_id=1, source_target_pairs={{0,8},{8,0},{1,9},{9,1},{2,10},{10,2},{3,11},{11,3},{4,12},{12,4},... | collective-permute-start | bytes 49160 | tf_op jit(solution)/shard_map/ppermute | solution.py:44
  47.0 5.2 %collective-permute-start.10 = (f32[2,2048]{1,0:T(2,128)S(1)}, f32[2,2048]{1,0:T(2,128)S(1)}, u32[]{:S(2)}, u32[]{:S(2)}) collective-permute-start(f32[2,2048]{1,0:T(2,128)S(1)} %row_delta.1.s0), channel_id=1, source_target_pairs={{0,128},{128,0},{1,129},{129,1},{2,130},{130,2},{3,131},{131,3},{4... | collective-permute-start | bytes 49160 | tf_op jit(solution)/shard_map/ppermute | solution.py:44
  58.3 23.6 %all-to-all-start.1 = ((bf16[8,128,256]{2,1,0:T(8,128)(2,1)}), bf16[8,128,256]{2,1,0:T(8,128)(2,1)S(1)}, u32[]{:S(2)}, u32[]{:S(2)}) async-start(bf16[8,128,256]{2,1,0:T(8,128)(2,1)} %bitcast.14), calls=%async_computation.1 | async-start | bytes 1048576 | tf_op jit(solution)/shard_map/all_to_all | solution.py:284
  65.2 1.3 %collective-permute-start.14 = (bf16[128,512]{1,0:T(8,128)(2,1)S(1)}, bf16[128,512]{1,0:T(8,128)(2,1)S(1)}, u32[]{:S(2)}, u32[]{:S(2)}) collective-permute-start(bf16[128,512]{1,0:T(8,128)(2,1)S(1)} %get-tuple-element.21), channel_id=1, source_target_pairs={{0,8},{8,0},{1,9},{9,1},{2,10},{10,2},{3,11},{11,3},{4,12},{12,4},... | collective-permute-start | bytes 393224 | tf_op jit(solution)/shard_map/ppermute | solution.py:44
  65.2 2.1 %collective-permute-start.13 = (bf16[128,512]{1,0:T(8,128)(2,1)S(1)}, bf16[128,512]{1,0:T(8,128)(2,1)S(1)}, u32[]{:S(2)}, u32[]{:S(2)}) collective-permute-start(bf16[128,512]{1,0:T(8,128)(2,1)S(1)} %get-tuple-element.19), channel_id=1, source_target_pairs={{0,8},{8,0},{1,9},{9,1},{2,10},{10,2},{3,11},{11,3},{4,12},{12,4},... | collective-permute-start | bytes 393224 | tf_op jit(solution)/shard_map/ppermute | solution.py:44
  66.6 7.1 %collective-permute-start.15 = (bf16[128,512]{1,0:T(8,128)(2,1)S(1)}, bf16[128,512]{1,0:T(8,128)(2,1)S(1)}, u32[]{:S(2)}, u32[]{:S(2)}) collective-permute-start(bf16[128,512]{1,0:T(8,128)(2,1)S(1)} %add_convert_fusion), channel_id=1, source_target_pairs={{0,128},{128,0},{1,129},{129,1},{2,130},{130,2},{3,131},{131,3},{4... | collective-permute-start | bytes 393224 | tf_op jit(solution)/shard_map/ppermute | solution.py:44

commit v6 on v5

--- a/solution.py
+++ b/solution.py
@@ -83,19 +83,36 @@
     return own, pick(far, (1, 0, 3, 2)), pick(core, (2, 3, 0, 1)), pick(both, (3, 2, 1, 0))
 
 
-def delta_kernel(
-    kpos, qpos, q0, q1, q2, q3, u0, u1, u2, u3, kv, lse_ref, stats_ref, q_scr, u_scr
-):
-    q_scr[...] = by_heads((q0, q1, q2, q3))
-    u_scr[...] = by_heads((u0, u1, u2, u3))
-    lse = lse_ref[...]
+def half_delta(kpos, qpos, q_refs, u_refs, kv, lse, q_scr, u_scr, groups):
+    n = qpos.shape[1] // 4
+    q_scr[...] = by_heads(q_refs)
+    u_scr[...] = by_heads(u_refs)
+    places = jnp.concatenate([qpos[:, g * n : (g + 1) * n] for g in groups], axis=1)
+    lse = jnp.concatenate(
+        [lse[:, (4 * h + g) * n : (4 * h + g + 1) * n] for h in range(GROUPS) for g in groups],
+        axis=1,
+    )
     total = jnp.zeros_like(lse)
     for at in range(0, kv.shape[0], CHUNK):
-        w = jnp.exp2(chunk_scores(kv, kpos, qpos, q_scr[...], at) - lse)
+        w = jnp.exp2(chunk_scores(kv, kpos, places, q_scr[...], at) - lse)
         dp = mm(kv[pl.ds(at, CHUNK), HEAD_DIM:], u_scr[...], NT)
         total = total + jnp.sum(w * dp, axis=0, keepdims=True)
-    stats_ref[0:1, :] = lse
-    stats_ref[1:2, :] = total
+    return total
+
+
+def near_delta_kernel(kpos, qpos, q0, q2, u0, u2, kv, lse, out, q_scr, u_scr):
+    out[...] = half_delta(kpos, qpos, (q0, q2), (u0, u2), kv, lse, q_scr, u_scr, (0, 2))
+
+
+def far_delta_kernel(kpos, qpos, q1, q3, u1, u3, kv, lse, near, stats_ref, q_scr, u_scr):
+    far = half_delta(kpos, qpos, (q1, q3), (u1, u3), kv, lse, q_scr, u_scr, (1, 3))
+    n = qpos.shape[1] // 4
+    stats_ref[0:1, :] = lse[...]
+    for h in range(GROUPS):
+        for g in range(4):
+            half = far[:, :] if g % 2 else near[...]
+            at = 2 * h + g // 2
+            stats_ref[1:2, (4 * h + g) * n : (4 * h + g + 1) * n] = half[:, at * n : (at + 1) * n]
 
 
 def grad_kernel(
@@ -250,18 +267,28 @@
     )(kpos, qpos, *q, kv)
 
     upstream = upstream_of(parts, order, o_weight)
-    far = shift_by(upstream, ("yh",), (1,))
-    far, lse = lax.optimization_barrier((far, lse))
-    u = upstream, far, shift_by(upstream, ("c",), (1,)), shift_by(far, ("c",), (1,))
+    far, core = shift_by(upstream, ("yh",), (1,)), shift_by(upstream, ("c",), (1,))
+    narrow = pltpu.VMEM((GROUPS * many // 2, HEAD_DIM), bf16)
+    near_delta = pl.pallas_call(
+        near_delta_kernel,
+        out_shape=jax.ShapeDtypeStruct((1, GROUPS * many // 2), f32),
+        in_specs=[vmem] * 8,
+        out_specs=vmem,
+        scratch_shapes=[narrow, narrow],
+        compiler_params=params,
+        name="near_delta",
+    )(kpos, qpos, q[0], q[2], upstream, core, kv, lse)
+    far, near_delta = lax.optimization_barrier((far, near_delta))
+    u = upstream, far, core, shift_by(far, ("c",), (1,))
     stats = pl.pallas_call(
-        delta_kernel,
+        far_delta_kernel,
         out_shape=jax.ShapeDtypeStruct((2, GROUPS * many), f32),
-        in_specs=[vmem] * 12,
-        out_specs=vmem,
-        scratch_shapes=[wide, wide],
+        in_specs=[vmem] * 9,
+        out_specs=vmem,
+        scratch_shapes=[narrow, narrow],
         compiler_params=params,
-        name="row_delta",
-    )(kpos, qpos, *q, *u, kv, lse)
+        name="far_delta",
+    )(kpos, qpos, q[1], q[3], u[1], u[3], kv, lse, near_delta)
     stats_parts = everyone(stats)
 
     shape = (rows, GROUPS * HEAD_DIM)

time: 83 us -> 82.1 us (0.989)
  waiting for transfers between devices: 28.8 us -> 27.2 us
    ppermute x16, waiting for transfers between devices: 21.4 us -> 19.8 us  [shift_by(): return lax.ppermute(value, axes, pairs)]
    pallas_call x1 -> x2, Pallas kernels: 2.82 us -> 2.82 us  [the longest x1 1.41 us: local(): pl.pallas_call(near_delta_kernel, out_shape=jax.ShapeDtypeStruct((1, GROU...]
  transfers between devices with their start and end apart: 18 -> 18, of which waited for: 10 -> 9; matrix products, arithmetic and copies ran while one was open for 4% -> 4% of each run, Pallas kernels for 10% -> 11%
where the time goes in v6:
time: 82.1 us; the launch traced here: 81.8 us
  starting transfers between devices  33 us (40%)
  waiting for transfers between devices  27.2 us (33%)
  Pallas kernels  16.8 us (20%)
  local copies, waits for them, and re-layouts  2.92 us (4%)
  other arithmetic  1.08 us (1%)
    ppermute x16, waiting for transfers between devices, shift_by(): return lax.ppermute(value, axes, pairs)  19.8 us
    ppermute x16, starting transfers between devices, shift_by(): return lax.ppermute(value, axes, pairs)  17.6 us
    all_to_all x1, starting transfers between devices, local(): kv = lax.all_to_all(both, 'z', 0, 0, tiled=True).reshape(keys, 2 * HEAD_DIM)  8.47 us
    all_to_all x1, waiting for transfers between devices, local(): lax.all_to_all(terms.reshape(nz, rows, 2 * HEAD_DIM), 'z', 0, 0, tiled=True)  7.39 us
    all_to_all x1, starting transfers between devices, local(): lax.all_to_all(terms.reshape(nz, rows, 2 * HEAD_DIM), 'z', 0, 0, tiled=True)  6.92 us
    pallas_call x1, Pallas kernels, local(): pl.pallas_call(grad_kernel, out_shape=(jax.ShapeDtypeStruct(shape, f32),...  6.04 us
    pallas_call x1, Pallas kernels, upstream_of(): pl.pallas_call(upstream_kernel, out_shape=jax.ShapeDtypeStruct((rows, col...  3.51 us
    pallas_call x1, Pallas kernels, local(): pl.pallas_call(stats_kernel, out_shape=jax.ShapeDtypeStruct((1, GROUPS *...  2.77 us
  transfers between devices with their start and end apart: 18, of which 9 were waited for; matrix products, arithmetic and copies ran while one was open for 4% of the time, Pallas kernels for 11%

profile of v6, /device:TPU:2, one launch (start us, length us, event | category | flops | bytes accessed | tf_op | source)
XLA Modules:
  0.0 81.8 jit_solution(15468372029099157693)
XLA Ops:
  0.6 0.0 copy-start
  0.6 1.7 %collective-permute-start = (bf16[128,512]{1,0:T(8,128)(2,1)}, bf16[128,512]{1,0:T(8,128)(2,1)S(1)}, u32[]{:S(2)}, u32[]{:S(2)}) collective-permute-start(bf16[128,512]{1,0:T(8,128)(2,1)} %param.9), channel_id=1, source_target_pairs={{0,4},{4,0},{1,5},{5,1},{2,6},{6,2},{3,7},{7,3},{8,12},{12,8},{9,1... | collective-permute-start | bytes 393224 | tf_op jit(solution)/shard_map/ppermute | solution.py:44
  2.3 1.6 %pack.1 = bf16[1024,256]{1,0:T(8,128)(2,1)} custom-call(bf16[128,128]{1,0:T(8,128)(2,1)} %k.1, bf16[128,128]{1,0:T(8,128)(2,1)} %v.1), custom_call_target="tpu_custom_call" | custom-call | bytes 196608 | tf_op jit(solution)/shard_map/pack/pallas_call | solution.py:200
  4.0 8.5 %all-to-all-start = ((bf16[8,128,256]{2,1,0:T(8,128)(2,1)}), bf16[8,128,256]{2,1,0:T(8,128)(2,1)S(1)}, u32[]{:S(2)}, u32[]{:S(2)}) async-start(bf16[8,128,256]{2,1,0:T(8,128)(2,1)} %bitcast.23), calls=%async_computation | async-start | bytes 1048576 | tf_op jit(solution)/shard_map/all_to_all | solution.py:221
  12.4 0.8 reshape.120
  13.2 0.1 add_multiply_fusion
  13.3 0.1 iota_add_fusion.1
  13.4 0.1 mul.32
  13.5 0.1 add.133.qpos
  13.6 0.9 %constant_dynamic-update-slice_fusion.1 = bf16[256,512]{1,0:T(8,128)(2,1)S(1)} fusion(bf16[128,512]{1,0:T(8,128)(2,1)} %param.9), kind=kLoop, calls=%fused_computation.5 | loop fusion | bytes 262144
  14.5 0.0 collective-permute-done
  14.5 2.2 %collective-permute-start.6 = (bf16[256,512]{1,0:T(8,128)(2,1)S(1)}, bf16[256,512]{1,0:T(8,128)(2,1)S(1)}, u32[]{:S(2)}, u32[]{:S(2)}) collective-permute-start(bf16[256,512]{1,0:T(8,128)(2,1)S(1)} %constant_dynamic-update-slice_fusion.refs_0_), channel_id=1, source_target_pairs={{0,2},{1,3},{2,0},{3,1},{4,6},{5,7},{6,4},{7,5},{8,10},{9,11},{10,... | collective-permute-start | bytes 786440 | tf_op jit(solution)/shard_map/ppermute | solution.py:44
  16.7 1.4 %collective-permute-start.5 = (bf16[256,512]{1,0:T(8,128)(2,1)S(1)}, bf16[256,512]{1,0:T(8,128)(2,1)S(1)}, u32[]{:S(2)}, u32[]{:S(2)}) collective-permute-start(bf16[256,512]{1,0:T(8,128)(2,1)S(1)} %constant_dynamic-update-slice_fusion.refs_0_), channel_id=1, source_target_pairs={{0,3},{1,0},{2,1},{3,2},{4,7},{5,4},{6,5},{7,6},{8,11},{9,8},{10,9... | collective-permute-start | bytes 786440 | tf_op jit(solution)/shard_map/ppermute | solution.py:44
  18.2 0.6 collective-permute-start.4
  18.7 0.1 iota_add_fusion
  18.8 0.1 add.126
  18.9 2.9 %collective-permute-start.1 = (bf16[128,512]{1,0:T(8,128)(2,1)}, bf16[128,512]{1,0:T(8,128)(2,1)S(1)}, u32[]{:S(2)}, u32[]{:S(2)}) collective-permute-start(bf16[128,512]{1,0:T(8,128)(2,1)} %q0.2), channel_id=1, source_target_pairs={{0,128},{128,0},{1,129},{129,1},{2,130},{130,2},{3,131},{131,3},{4... | collective-permute-start | bytes 393224 | tf_op jit(solution)/shard_map/ppermute | solution.py:44
  21.8 0.1 stack.35.order
  21.9 0.0 collective-permute-start.2
  21.9 3.7 %collective-permute-done.1.q1 = bf16[128,512]{1,0:T(8,128)(2,1)S(1)} collective-permute-done((bf16[128,512]{1,0:T(8,128)(2,1)}, bf16[128,512]{1,0:T(8,128)(2,1)S(1)}, u32[]{:S(2)}, u32[]{:S(2)}) %collective-permute-start.1) | collective-permute-done | bytes 131104 | tf_op jit(solution)/shard_map/ppermute | solution.py:44
  25.6 0.0 collective-permute-start.3
  25.6 0.0 collective-permute-done.6.refs_3_
  25.6 3.6 %collective-permute-done.5.refs_2_ = bf16[256,512]{1,0:T(8,128)(2,1)S(1)} collective-permute-done((bf16[256,512]{1,0:T(8,128)(2,1)S(1)}, bf16[256,512]{1,0:T(8,128)(2,1)S(1)}, u32[]{:S(2)}, u32[]{:S(2)}) %collective-permute-start.5) | collective-permute-done | bytes 262176 | tf_op jit(solution)/shard_map/ppermute | solution.py:44
  29.2 0.1 collective-permute-done.4.refs_1_
  29.3 3.5 %upstream.1.u0 = bf16[128,512]{1,0:T(8,128)(2,1)S(1)} custom-call(s32[8]{0:T(128)S(1)} %stack.35.order, bf16[256,512]{1,0:T(8,128)(2,1)S(1)} %constant_dynamic-update-slice_fusion.refs_0_, bf16[256,512]{1,0:T(8,128)(2,1)S(1)} %collective-permute-done.4.refs_1_, bf16[256,512]{1,0:T(8,128)(2,1)S(1)} %collective-permute-done.5.refs_2_, ...), custom_call_target="tpu_custom_call" | custom-call | tf_op jit(solution)/shard_map/upstream/pallas_call | solution.py:174
  32.8 0.1 collective-permute-start.8
  32.9 3.0 %collective-permute-start.7 = (bf16[128,512]{1,0:T(8,128)(2,1)S(1)}, bf16[128,512]{1,0:T(8,128)(2,1)S(1)}, u32[]{:S(2)}, u32[]{:S(2)}) collective-permute-start(bf16[128,512]{1,0:T(8,128)(2,1)S(1)} %upstream.1.u0), channel_id=1, source_target_pairs={{0,128},{128,0},{1,129},{129,1},{2,130},{130,2},{3,131},{131,3},{4... | collective-permute-start | bytes 393224 | tf_op jit(solution)/shard_map/ppermute | solution.py:44
  35.9 0.2 copy.12.kpos
  36.1 2.8 %row_stats.1.lse = f32[1,2048]{1,0:T(1,128)S(1)} custom-call(s32[1024,1]{1,0:T(8,128)S(1)} %copy.12.kpos, s32[1,512]{1,0:T(1,128)S(1)} %add.133.qpos, bf16[128,512]{1,0:T(8,128)(2,1)S(1)} %copy-done, bf16[128,512]{1,0:T(8,128)(2,1)S(1)} %collective-permute-done.1.q1, bf16[128,512]{1,0:T(8,128)(2,1)S(1)} %collective-permute-done.2.q2, ...), custom_call_target="tpu_custom_call" | custom-call | tf_op jit(solution)/shard_map/row_stats/pallas_call | solution.py:259
  38.9 1.4 %near_delta.1.near = f32[1,1024]{1,0:T(1,128)S(1)} custom-call(s32[1024,1]{1,0:T(8,128)S(1)} %copy.12.kpos, s32[1,512]{1,0:T(1,128)S(1)} %add.133.qpos, bf16[128,512]{1,0:T(8,128)(2,1)S(1)} %copy-done, bf16[128,512]{1,0:T(8,128)(2,1)S(1)} %collective-permute-done.2.q2, bf16[128,512]{1,0:T(8,128)(2,1)S(1)} %upstream.1.u0, ...), custom_call_target="tpu_custom_call" | custom-call | tf_op jit(solution)/shard_map/near_delta/pallas_call | solution.py:272
  40.4 0.4 collective-permute-start.9
  40.8 1.2 %collective-permute-done.9.u3 = bf16[128,512]{1,0:T(8,128)(2,1)S(1)} collective-permute-done((bf16[128,512]{1,0:T(8,128)(2,1)S(1)}, bf16[128,512]{1,0:T(8,128)(2,1)S(1)}, u32[]{:S(2)}, u32[]{:S(2)}) %collective-permute-start.9) | collective-permute-done | bytes 131104 | tf_op jit(solution)/shard_map/ppermute | solution.py:44
  42.0 1.4 %far_delta.1.s0 = f32[2,2048]{1,0:T(2,128)S(1)} custom-call(s32[1024,1]{1,0:T(8,128)S(1)} %copy.12.kpos, s32[1,512]{1,0:T(1,128)S(1)} %add.133.qpos, bf16[128,512]{1,0:T(8,128)(2,1)S(1)} %collective-permute-done.1.q1, bf16[128,512]{1,0:T(8,128)(2,1)S(1)} %collective-permute-done.3.q3, bf16[128,512]{1,0:T(8,128)(2,1)S(1)} %collective-permute-done.7.u1, ...), custom_call_target="tpu_custom_call" | custom-call | tf_op jit(solution)/shard_map/far_delta/pallas_call | solution.py:283
  43.4 2.4 %collective-permute-start.12 = (f32[2,2048]{1,0:T(2,128)S(1)}, f32[2,2048]{1,0:T(2,128)S(1)}, u32[]{:S(2)}, u32[]{:S(2)}) collective-permute-start(f32[2,2048]{1,0:T(2,128)S(1)} %far_delta.1.s0), channel_id=1, source_target_pairs={{0,136},{8,128},{128,8},{136,0},{1,137},{9,129},{129,9},{137,1},{2... | collective-permute-start | bytes 49160 | tf_op jit(solution)/shard_map/ppermute | solution.py:44
  45.8 0.4 collective-permute-start.11
  46.2 0.9 %collective-permute-start.10 = (f32[2,2048]{1,0:T(2,128)S(1)}, f32[2,2048]{1,0:T(2,128)S(1)}, u32[]{:S(2)}, u32[]{:S(2)}) collective-permute-start(f32[2,2048]{1,0:T(2,128)S(1)} %far_delta.1.s0), channel_id=1, source_target_pairs={{0,128},{128,0},{1,129},{129,1},{2,130},{130,2},{3,131},{131,3},{4... | collective-permute-start | bytes 49160 | tf_op jit(solution)/shard_map/ppermute | solution.py:44
  47.1 1.0 %collective-permute-done.12.s3 = f32[2,2048]{1,0:T(2,128)S(1)} collective-permute-done((f32[2,2048]{1,0:T(2,128)S(1)}, f32[2,2048]{1,0:T(2,128)S(1)}, u32[]{:S(2)}, u32[]{:S(2)}) %collective-permute-start.12) | collective-permute-done | bytes 16416 | tf_op jit(solution)/shard_map/ppermute | solution.py:44
  48.1 3.3 %collective-permute-done.10.s1 = f32[2,2048]{1,0:T(2,128)S(1)} collective-permute-done((f32[2,2048]{1,0:T(2,128)S(1)}, f32[2,2048]{1,0:T(2,128)S(1)}, u32[]{:S(2)}, u32[]{:S(2)}) %collective-permute-start.10) | collective-permute-done | bytes 16416 | tf_op jit(solution)/shard_map/ppermute | solution.py:44
  51.4 6.0 %gradients.1 = (f32[128,512]{1,0:T(8,128)S(1)}, f32[128,512]{1,0:T(8,128)S(1)}, bf16[128,512]{1,0:T(8,128)(2,1)S(1)}, bf16[128,512]{1,0:T(8,128)(2,1)S(1)}, bf16[1024,256]{1,0:T(8,128)(2,1)}) custom-call(s32[1024,1]{1,0:T(8,128)S(1)} %copy.12.kpos, s32[1,512]{1,0:T(1,128)S(1)} %add.133.qpos, bf16[128,512]{1,0:T(8,128)(2,1)S(1)} %copy-done, ...), custom_call_target="tpu_custom_call" | custom-call | tf_op jit(solution)/shard_map/gradients/pallas_call | solution.py:295
  57.5 6.9 %all-to-all-start.1 = ((bf16[8,128,256]{2,1,0:T(8,128)(2,1)}), bf16[8,128,256]{2,1,0:T(8,128)(2,1)S(1)}, u32[]{:S(2)}, u32[]{:S(2)}) async-start(bf16[8,128,256]{2,1,0:T(8,128)(2,1)} %bitcast.14), calls=%async_computation.1 | async-start | bytes 1048576 | tf_op jit(solution)/shard_map/all_to_all | solution.py:311
  64.4 0.5 collective-permute-start.13
  64.9 0.8 %collective-permute-done.14 = bf16[128,512]{1,0:T(8,128)(2,1)S(1)} collective-permute-done((bf16[128,512]{1,0:T(8,128)(2,1)S(1)}, bf16[128,512]{1,0:T(8,128)(2,1)S(1)}, u32[]{:S(2)}, u32[]{:S(2)}) %collective-permute-start.14) | collective-permute-done | bytes 131104 | tf_op jit(solution)/shard_map/ppermute | solution.py:44
  65.8 1.0 %collective-permute-start.15 = (bf16[128,512]{1,0:T(8,128)(2,1)S(1)}, bf16[128,512]{1,0:T(8,128)(2,1)S(1)}, u32[]{:S(2)}, u32[]{:S(2)}) collective-permute-start(bf16[128,512]{1,0:T(8,128)(2,1)S(1)} %add_convert_fusion), channel_id=1, source_target_pairs={{0,128},{128,0},{1,129},{129,1},{2,130},{130,2},{3,131},{131,3},{4... | collective-permute-start | bytes 393224 | tf_op jit(solution)/shard_map/ppermute | solution.py:44
  66.8 6.1 %collective-permute-done.15 = bf16[128,512]{1,0:T(8,128)(2,1)S(1)} collective-permute-done((bf16[128,512]{1,0:T(8,128)(2,1)S(1)}, bf16[128,512]{1,0:T(8,128)(2,1)S(1)}, u32[]{:S(2)}, u32[]{:S(2)}) %collective-permute-start.15) | collective-permute-done | bytes 131104 | tf_op jit(solution)/shard_map/ppermute | solution.py:44
  72.9 0.7 convert_add_fusion
  73.7 7.4 %all-to-all-done.1 = bf16[8,128,256]{2,1,0:T(8,128)(2,1)S(1)} async-done(((bf16[8,128,256]{2,1,0:T(8,128)(2,1)}), bf16[8,128,256]{2,1,0:T(8,128)(2,1)S(1)}, u32[]{:S(2)}, u32[]{:S(2)}) %all-to-all-start.1) | async-done | bytes 524320 | tf_op jit(solution)/shard_map/all_to_all | solution.py:311
  81.0 0.1 convert_reduce_fusion
  81.1 0.7 fusion.4
  (13 shorter events, 0.1 us)
Async XLA Ops:
  0.6 35.5 %copy-start = (bf16[128,512]{1,0:T(8,128)(2,1)S(1)}, bf16[128,512]{1,0:T(8,128)(2,1)}, u32[]{:S(2)}) copy-start(bf16[128,512]{1,0:T(8,128)(2,1)} %q0.2) | copy-start | bytes 393220
  0.6 13.8 %collective-permute-start = (bf16[128,512]{1,0:T(8,128)(2,1)}, bf16[128,512]{1,0:T(8,128)(2,1)S(1)}, u32[]{:S(2)}, u32[]{:S(2)}) collective-permute-start(bf16[128,512]{1,0:T(8,128)(2,1)} %param.9), channel_id=1, source_target_pairs={{0,4},{4,0},{1,5},{5,1},{2,6},{6,2},{3,7},{7,3},{8,12},{12,8},{9,1... | collective-permute-start | bytes 393224 | tf_op jit(solution)/shard_map/ppermute | solution.py:44
  4.0 32.2 %all-to-all-start = ((bf16[8,128,256]{2,1,0:T(8,128)(2,1)}), bf16[8,128,256]{2,1,0:T(8,128)(2,1)S(1)}, u32[]{:S(2)}, u32[]{:S(2)}) async-start(bf16[8,128,256]{2,1,0:T(8,128)(2,1)} %bitcast.23), calls=%async_computation | async-start | bytes 1048576 | tf_op jit(solution)/shard_map/all_to_all | solution.py:221
  14.5 11.1 %collective-permute-start.6 = (bf16[256,512]{1,0:T(8,128)(2,1)S(1)}, bf16[256,512]{1,0:T(8,128)(2,1)S(1)}, u32[]{:S(2)}, u32[]{:S(2)}) collective-permute-start(bf16[256,512]{1,0:T(8,128)(2,1)S(1)} %constant_dynamic-update-slice_fusion.refs_0_), channel_id=1, source_target_pairs={{0,2},{1,3},{2,0},{3,1},{4,6},{5,7},{6,4},{7,5},{8,10},{9,11},{10,... | collective-permute-start | bytes 786440 | tf_op jit(solution)/shard_map/ppermute | solution.py:44
  16.7 12.5 %collective-permute-start.5 = (bf16[256,512]{1,0:T(8,128)(2,1)S(1)}, bf16[256,512]{1,0:T(8,128)(2,1)S(1)}, u32[]{:S(2)}, u32[]{:S(2)}) collective-permute-start(bf16[256,512]{1,0:T(8,128)(2,1)S(1)} %constant_dynamic-update-slice_fusion.refs_0_), channel_id=1, source_target_pairs={{0,3},{1,0},{2,1},{3,2},{4,7},{5,4},{6,5},{7,6},{8,11},{9,8},{10,9... | collective-permute-start | bytes 786440 | tf_op jit(solution)/shard_map/ppermute | solution.py:44
  18.2 11.1 %collective-permute-start.4 = (bf16[256,512]{1,0:T(8,128)(2,1)S(1)}, bf16[256,512]{1,0:T(8,128)(2,1)S(1)}, u32[]{:S(2)}, u32[]{:S(2)}) collective-permute-start(bf16[256,512]{1,0:T(8,128)(2,1)S(1)} %constant_dynamic-update-slice_fusion.refs_0_), channel_id=1, source_target_pairs={{0,1},{1,2},{2,3},{3,0},{4,5},{5,6},{6,7},{7,4},{8,9},{9,10},{10,1... | collective-permute-start | bytes 786440 | tf_op jit(solution)/shard_map/ppermute | solution.py:44
  18.9 6.7 %collective-permute-start.1 = (bf16[128,512]{1,0:T(8,128)(2,1)}, bf16[128,512]{1,0:T(8,128)(2,1)S(1)}, u32[]{:S(2)}, u32[]{:S(2)}) collective-permute-start(bf16[128,512]{1,0:T(8,128)(2,1)} %q0.2), channel_id=1, source_target_pairs={{0,128},{128,0},{1,129},{129,1},{2,130},{130,2},{3,131},{131,3},{4... | collective-permute-start | bytes 393224 | tf_op jit(solution)/shard_map/ppermute | solution.py:44
  21.9 14.2 %collective-permute-start.2 = (bf16[128,512]{1,0:T(8,128)(2,1)}, bf16[128,512]{1,0:T(8,128)(2,1)S(1)}, u32[]{:S(2)}, u32[]{:S(2)}) collective-permute-start(bf16[128,512]{1,0:T(8,128)(2,1)} %q0.2), channel_id=1, source_target_pairs={{0,8},{8,0},{1,9},{9,1},{2,10},{10,2},{3,11},{11,3},{4,12},{12,4},... | collective-permute-start | bytes 393224 | tf_op jit(solution)/shard_map/ppermute | solution.py:44
  25.6 10.5 %collective-permute-start.3 = (bf16[128,512]{1,0:T(8,128)(2,1)S(1)}, bf16[128,512]{1,0:T(8,128)(2,1)S(1)}, u32[]{:S(2)}, u32[]{:S(2)}) collective-permute-start(bf16[128,512]{1,0:T(8,128)(2,1)S(1)} %collective-permute-done.1.q1), channel_id=1, source_target_pairs={{0,8},{8,0},{1,9},{9,1},{2,10},{10,2},{3,11},{11,3},{4,12},{12,4},... | collective-permute-start | bytes 393224 | tf_op jit(solution)/shard_map/ppermute | solution.py:44
  32.8 6.1 %collective-permute-start.8 = (bf16[128,512]{1,0:T(8,128)(2,1)S(1)}, bf16[128,512]{1,0:T(8,128)(2,1)S(1)}, u32[]{:S(2)}, u32[]{:S(2)}) collective-permute-start(bf16[128,512]{1,0:T(8,128)(2,1)S(1)} %upstream.1.u0), channel_id=1, source_target_pairs={{0,8},{8,0},{1,9},{9,1},{2,10},{10,2},{3,11},{11,3},{4,12},{12,4},... | collective-permute-start | bytes 393224 | tf_op jit(solution)/shard_map/ppermute | solution.py:44
  32.9 7.5 %collective-permute-start.7 = (bf16[128,512]{1,0:T(8,128)(2,1)S(1)}, bf16[128,512]{1,0:T(8,128)(2,1)S(1)}, u32[]{:S(2)}, u32[]{:S(2)}) collective-permute-start(bf16[128,512]{1,0:T(8,128)(2,1)S(1)} %upstream.1.u0), channel_id=1, source_target_pairs={{0,128},{128,0},{1,129},{129,1},{2,130},{130,2},{3,131},{131,3},{4... | collective-permute-start | bytes 393224 | tf_op jit(solution)/shard_map/ppermute | solution.py:44
  40.4 1.6 %collective-permute-start.9 = (bf16[128,512]{1,0:T(8,128)(2,1)S(1)}, bf16[128,512]{1,0:T(8,128)(2,1)S(1)}, u32[]{:S(2)}, u32[]{:S(2)}) collective-permute-start(bf16[128,512]{1,0:T(8,128)(2,1)S(1)} %collective-permute-done.7.u1), channel_id=1, source_target_pairs={{0,8},{8,0},{1,9},{9,1},{2,10},{10,2},{3,11},{11,3},{4,12},{12,4},... | collective-permute-start | bytes 393224 | tf_op jit(solution)/shard_map/ppermute | solution.py:44
  43.4 4.8 %collective-permute-start.12 = (f32[2,2048]{1,0:T(2,128)S(1)}, f32[2,2048]{1,0:T(2,128)S(1)}, u32[]{:S(2)}, u32[]{:S(2)}) collective-permute-start(f32[2,2048]{1,0:T(2,128)S(1)} %far_delta.1.s0), channel_id=1, source_target_pairs={{0,136},{8,128},{128,8},{136,0},{1,137},{9,129},{129,9},{137,1},{2... | collective-permute-start | bytes 49160 | tf_op jit(solution)/shard_map/ppermute | solution.py:44
  45.8 2.3 %collective-permute-start.11 = (f32[2,2048]{1,0:T(2,128)S(1)}, f32[2,2048]{1,0:T(2,128)S(1)}, u32[]{:S(2)}, u32[]{:S(2)}) collective-permute-start(f32[2,2048]{1,0:T(2,128)S(1)} %far_delta.1.s0), channel_id=1, source_target_pairs={{0,8},{8,0},{1,9},{9,1},{2,10},{10,2},{3,11},{11,3},{4,12},{12,4},... | collective-permute-start | bytes 49160 | tf_op jit(solution)/shard_map/ppermute | solution.py:44
  46.2 5.2 %collective-permute-start.10 = (f32[2,2048]{1,0:T(2,128)S(1)}, f32[2,2048]{1,0:T(2,128)S(1)}, u32[]{:S(2)}, u32[]{:S(2)}) collective-permute-start(f32[2,2048]{1,0:T(2,128)S(1)} %far_delta.1.s0), channel_id=1, source_target_pairs={{0,128},{128,0},{1,129},{129,1},{2,130},{130,2},{3,131},{131,3},{4... | collective-permute-start | bytes 49160 | tf_op jit(solution)/shard_map/ppermute | solution.py:44
  57.5 23.6 %all-to-all-start.1 = ((bf16[8,128,256]{2,1,0:T(8,128)(2,1)}), bf16[8,128,256]{2,1,0:T(8,128)(2,1)S(1)}, u32[]{:S(2)}, u32[]{:S(2)}) async-start(bf16[8,128,256]{2,1,0:T(8,128)(2,1)} %bitcast.14), calls=%async_computation.1 | async-start | bytes 1048576 | tf_op jit(solution)/shard_map/all_to_all | solution.py:311
  64.4 1.3 %collective-permute-start.14 = (bf16[128,512]{1,0:T(8,128)(2,1)S(1)}, bf16[128,512]{1,0:T(8,128)(2,1)S(1)}, u32[]{:S(2)}, u32[]{:S(2)}) collective-permute-start(bf16[128,512]{1,0:T(8,128)(2,1)S(1)} %get-tuple-element.21), channel_id=1, source_target_pairs={{0,8},{8,0},{1,9},{9,1},{2,10},{10,2},{3,11},{11,3},{4,12},{12,4},... | collective-permute-start | bytes 393224 | tf_op jit(solution)/shard_map/ppermute | solution.py:44
  64.4 2.4 %collective-permute-start.13 = (bf16[128,512]{1,0:T(8,128)(2,1)S(1)}, bf16[128,512]{1,0:T(8,128)(2,1)S(1)}, u32[]{:S(2)}, u32[]{:S(2)}) collective-permute-start(bf16[128,512]{1,0:T(8,128)(2,1)S(1)} %get-tuple-element.19), channel_id=1, source_target_pairs={{0,8},{8,0},{1,9},{9,1},{2,10},{10,2},{3,11},{11,3},{4,12},{12,4},... | collective-permute-start | bytes 393224 | tf_op jit(solution)/shard_map/ppermute | solution.py:44
  65.8 7.1 %collective-permute-start.15 = (bf16[128,512]{1,0:T(8,128)(2,1)S(1)}, bf16[128,512]{1,0:T(8,128)(2,1)S(1)}, u32[]{:S(2)}, u32[]{:S(2)}) collective-permute-start(bf16[128,512]{1,0:T(8,128)(2,1)S(1)} %add_convert_fusion), channel_id=1, source_target_pairs={{0,128},{128,0},{1,129},{129,1},{2,130},{130,2},{3,131},{131,3},{4... | collective-permute-start | bytes 393224 | tf_op jit(solution)/shard_map/ppermute | solution.py:44

commit v7 on v6

--- a/solution.py
+++ b/solution.py
@@ -19,7 +19,8 @@
 SCALE2 = FACTOR * math.log2(math.e)
 MASKED = -1e30
 CHUNK = 512
-VMEM_LIMIT = 32 * 1024 * 1024
+GRAD_CHUNK = 1024
+VMEM_LIMIT = 40 * 1024 * 1024
 NT = (((1,), (1,)), ((), ()))
 NN = (((1,), (0,)), ((), ()))
 
@@ -50,8 +51,8 @@
     )
 
 
-def chunk_scores(k, kpos, qpos, q, at):
-    rows = pl.ds(at, CHUNK)
+def chunk_scores(k, kpos, qpos, q, at, size=CHUNK):
+    rows = pl.ds(at, size)
     bias = jnp.where(kpos[rows, :] <= qpos[...], 0.0, MASKED)
     bias = jnp.concatenate([bias] * GROUPS, axis=1)
     return mm(k[rows, :HEAD_DIM], q, NT) * SCALE2 + bias
@@ -130,9 +131,9 @@
     lse = peak + jnp.log2(whole_share)
     delta = sum(p[1:] * share for p, share in zip(parts, shares)) / whole_share
 
-    for at in range(0, kv.shape[0], CHUNK):
-        rows = pl.ds(at, CHUNK)
-        w = jnp.exp2(chunk_scores(kv, kpos, qpos, q_scr[...], at) - lse)
+    for at in range(0, kv.shape[0], GRAD_CHUNK):
+        rows = pl.ds(at, GRAD_CHUNK)
+        w = jnp.exp2(chunk_scores(kv, kpos, qpos, q_scr[...], at, GRAD_CHUNK) - lse)
         dp = mm(kv[rows, HEAD_DIM:], u_scr[...], NT)
         ds = (w * (dp - delta)).astype(jnp.bfloat16)
         terms_ref[rows, HEAD_DIM:] = mm(w.astype(jnp.bfloat16), u_scr[...], NN).astype(jnp.bfloat16)

time: 82.1 us -> 81.9 us (level)
  no operation moved by 1% of the time
where the time goes in v7:
time: 81.9 us; the launch traced here: 81.6 us
  starting transfers between devices  33 us (40%)
  waiting for transfers between devices  27.2 us (33%)
  Pallas kernels  16.6 us (20%)
  local copies, waits for them, and re-layouts  2.92 us (4%)
  other arithmetic  1.08 us (1%)
    ppermute x16, waiting for transfers between devices, shift_by(): return lax.ppermute(value, axes, pairs)  19.8 us
    ppermute x16, starting transfers between devices, shift_by(): return lax.ppermute(value, axes, pairs)  17.6 us
    all_to_all x1, starting transfers between devices, local(): kv = lax.all_to_all(both, 'z', 0, 0, tiled=True).reshape(keys, 2 * HEAD_DIM)  8.47 us
    all_to_all x1, waiting for transfers between devices, local(): lax.all_to_all(terms.reshape(nz, rows, 2 * HEAD_DIM), 'z', 0, 0, tiled=True)  7.38 us
    all_to_all x1, starting transfers between devices, local(): lax.all_to_all(terms.reshape(nz, rows, 2 * HEAD_DIM), 'z', 0, 0, tiled=True)  6.92 us
    pallas_call x1, Pallas kernels, local(): pl.pallas_call(grad_kernel, out_shape=(jax.ShapeDtypeStruct(shape, f32),...  5.86 us
    pallas_call x1, Pallas kernels, upstream_of(): pl.pallas_call(upstream_kernel, out_shape=jax.ShapeDtypeStruct((rows, col...  3.51 us
    pallas_call x1, Pallas kernels, local(): pl.pallas_call(stats_kernel, out_shape=jax.ShapeDtypeStruct((1, GROUPS *...  2.77 us
  transfers between devices with their start and end apart: 18, of which 9 were waited for; matrix products, arithmetic and copies ran while one was open for 4% of the time, Pallas kernels for 11%

profile of v7, /device:TPU:2, one launch (start us, length us, event | category | flops | bytes accessed | tf_op | source)
XLA Modules:
  0.0 81.6 jit_solution(900077115387566496)
XLA Ops:
  0.6 0.0 copy-start
  0.6 1.7 %collective-permute-start = (bf16[128,512]{1,0:T(8,128)(2,1)}, bf16[128,512]{1,0:T(8,128)(2,1)S(1)}, u32[]{:S(2)}, u32[]{:S(2)}) collective-permute-start(bf16[128,512]{1,0:T(8,128)(2,1)} %param.9), channel_id=1, source_target_pairs={{0,4},{4,0},{1,5},{5,1},{2,6},{6,2},{3,7},{7,3},{8,12},{12,8},{9,1... | collective-permute-start | bytes 393224 | tf_op jit(solution)/shard_map/ppermute | solution.py:45
  2.3 1.6 %pack.1 = bf16[1024,256]{1,0:T(8,128)(2,1)} custom-call(bf16[128,128]{1,0:T(8,128)(2,1)} %k.1, bf16[128,128]{1,0:T(8,128)(2,1)} %v.1), custom_call_target="tpu_custom_call" | custom-call | bytes 196608 | tf_op jit(solution)/shard_map/pack/pallas_call | solution.py:201
  4.0 8.5 %all-to-all-start = ((bf16[8,128,256]{2,1,0:T(8,128)(2,1)}), bf16[8,128,256]{2,1,0:T(8,128)(2,1)S(1)}, u32[]{:S(2)}, u32[]{:S(2)}) async-start(bf16[8,128,256]{2,1,0:T(8,128)(2,1)} %bitcast.23), calls=%async_computation | async-start | bytes 1048576 | tf_op jit(solution)/shard_map/all_to_all | solution.py:222
  12.4 0.8 reshape.120
  13.2 0.1 add_multiply_fusion
  13.3 0.1 iota_add_fusion.1
  13.4 0.1 mul.32
  13.5 0.1 add.133.qpos
  13.6 0.9 %constant_dynamic-update-slice_fusion.1 = bf16[256,512]{1,0:T(8,128)(2,1)S(1)} fusion(bf16[128,512]{1,0:T(8,128)(2,1)} %param.9), kind=kLoop, calls=%fused_computation.5 | loop fusion | bytes 262144
  14.5 2.2 %collective-permute-start.6 = (bf16[256,512]{1,0:T(8,128)(2,1)S(1)}, bf16[256,512]{1,0:T(8,128)(2,1)S(1)}, u32[]{:S(2)}, u32[]{:S(2)}) collective-permute-start(bf16[256,512]{1,0:T(8,128)(2,1)S(1)} %constant_dynamic-update-slice_fusion.refs_0_), channel_id=1, source_target_pairs={{0,2},{1,3},{2,0},{3,1},{4,6},{5,7},{6,4},{7,5},{8,10},{9,11},{10,... | collective-permute-start | bytes 786440 | tf_op jit(solution)/shard_map/ppermute | solution.py:45
  16.7 1.4 %collective-permute-start.5 = (bf16[256,512]{1,0:T(8,128)(2,1)S(1)}, bf16[256,512]{1,0:T(8,128)(2,1)S(1)}, u32[]{:S(2)}, u32[]{:S(2)}) collective-permute-start(bf16[256,512]{1,0:T(8,128)(2,1)S(1)} %constant_dynamic-update-slice_fusion.refs_0_), channel_id=1, source_target_pairs={{0,3},{1,0},{2,1},{3,2},{4,7},{5,4},{6,5},{7,6},{8,11},{9,8},{10,9... | collective-permute-start | bytes 786440 | tf_op jit(solution)/shard_map/ppermute | solution.py:45
  18.2 0.6 collective-permute-start.4
  18.7 0.1 iota_add_fusion
  18.8 0.1 add.126
  18.9 2.9 %collective-permute-start.1 = (bf16[128,512]{1,0:T(8,128)(2,1)}, bf16[128,512]{1,0:T(8,128)(2,1)S(1)}, u32[]{:S(2)}, u32[]{:S(2)}) collective-permute-start(bf16[128,512]{1,0:T(8,128)(2,1)} %q0.2), channel_id=1, source_target_pairs={{0,128},{128,0},{1,129},{129,1},{2,130},{130,2},{3,131},{131,3},{4... | collective-permute-start | bytes 393224 | tf_op jit(solution)/shard_map/ppermute | solution.py:45
  21.8 0.1 stack.35.order
  21.9 0.0 collective-permute-start.2
  21.9 3.7 %collective-permute-done.1.q1 = bf16[128,512]{1,0:T(8,128)(2,1)S(1)} collective-permute-done((bf16[128,512]{1,0:T(8,128)(2,1)}, bf16[128,512]{1,0:T(8,128)(2,1)S(1)}, u32[]{:S(2)}, u32[]{:S(2)}) %collective-permute-start.1) | collective-permute-done | bytes 131104 | tf_op jit(solution)/shard_map/ppermute | solution.py:45
  25.6 3.6 %collective-permute-done.5.refs_2_ = bf16[256,512]{1,0:T(8,128)(2,1)S(1)} collective-permute-done((bf16[256,512]{1,0:T(8,128)(2,1)S(1)}, bf16[256,512]{1,0:T(8,128)(2,1)S(1)}, u32[]{:S(2)}, u32[]{:S(2)}) %collective-permute-start.5) | collective-permute-done | bytes 262176 | tf_op jit(solution)/shard_map/ppermute | solution.py:45
  29.2 0.1 collective-permute-done.4.refs_1_
  29.3 3.5 %upstream.1.u0 = bf16[128,512]{1,0:T(8,128)(2,1)S(1)} custom-call(s32[8]{0:T(128)S(1)} %stack.35.order, bf16[256,512]{1,0:T(8,128)(2,1)S(1)} %constant_dynamic-update-slice_fusion.refs_0_, bf16[256,512]{1,0:T(8,128)(2,1)S(1)} %collective-permute-done.4.refs_1_, bf16[256,512]{1,0:T(8,128)(2,1)S(1)} %collective-permute-done.5.refs_2_, ...), custom_call_target="tpu_custom_call" | custom-call | tf_op jit(solution)/shard_map/upstream/pallas_call | solution.py:175
  32.8 0.1 collective-permute-start.8
  32.9 3.0 %collective-permute-start.7 = (bf16[128,512]{1,0:T(8,128)(2,1)S(1)}, bf16[128,512]{1,0:T(8,128)(2,1)S(1)}, u32[]{:S(2)}, u32[]{:S(2)}) collective-permute-start(bf16[128,512]{1,0:T(8,128)(2,1)S(1)} %upstream.1.u0), channel_id=1, source_target_pairs={{0,128},{128,0},{1,129},{129,1},{2,130},{130,2},{3,131},{131,3},{4... | collective-permute-start | bytes 393224 | tf_op jit(solution)/shard_map/ppermute | solution.py:45
  35.9 0.2 copy.12.kpos
  36.1 0.0 collective-permute-done.2.q2
  36.1 0.0 all-to-all-done
  36.1 2.8 %row_stats.1.lse = f32[1,2048]{1,0:T(1,128)S(1)} custom-call(s32[1024,1]{1,0:T(8,128)S(1)} %copy.12.kpos, s32[1,512]{1,0:T(1,128)S(1)} %add.133.qpos, bf16[128,512]{1,0:T(8,128)(2,1)S(1)} %copy-done, bf16[128,512]{1,0:T(8,128)(2,1)S(1)} %collective-permute-done.1.q1, bf16[128,512]{1,0:T(8,128)(2,1)S(1)} %collective-permute-done.2.q2, ...), custom_call_target="tpu_custom_call" | custom-call | tf_op jit(solution)/shard_map/row_stats/pallas_call | solution.py:260
  38.9 0.0 collective-permute-done.8.u2
  38.9 1.4 %near_delta.1.near = f32[1,1024]{1,0:T(1,128)S(1)} custom-call(s32[1024,1]{1,0:T(8,128)S(1)} %copy.12.kpos, s32[1,512]{1,0:T(1,128)S(1)} %add.133.qpos, bf16[128,512]{1,0:T(8,128)(2,1)S(1)} %copy-done, bf16[128,512]{1,0:T(8,128)(2,1)S(1)} %collective-permute-done.2.q2, bf16[128,512]{1,0:T(8,128)(2,1)S(1)} %upstream.1.u0, ...), custom_call_target="tpu_custom_call" | custom-call | tf_op jit(solution)/shard_map/near_delta/pallas_call | solution.py:273
  40.4 0.4 collective-permute-start.9
  40.8 1.2 %collective-permute-done.9.u3 = bf16[128,512]{1,0:T(8,128)(2,1)S(1)} collective-permute-done((bf16[128,512]{1,0:T(8,128)(2,1)S(1)}, bf16[128,512]{1,0:T(8,128)(2,1)S(1)}, u32[]{:S(2)}, u32[]{:S(2)}) %collective-permute-start.9) | collective-permute-done | bytes 131104 | tf_op jit(solution)/shard_map/ppermute | solution.py:45
  42.0 1.4 %far_delta.1.s0 = f32[2,2048]{1,0:T(2,128)S(1)} custom-call(s32[1024,1]{1,0:T(8,128)S(1)} %copy.12.kpos, s32[1,512]{1,0:T(1,128)S(1)} %add.133.qpos, bf16[128,512]{1,0:T(8,128)(2,1)S(1)} %collective-permute-done.1.q1, bf16[128,512]{1,0:T(8,128)(2,1)S(1)} %collective-permute-done.3.q3, bf16[128,512]{1,0:T(8,128)(2,1)S(1)} %collective-permute-done.7.u1, ...), custom_call_target="tpu_custom_call" | custom-call | tf_op jit(solution)/shard_map/far_delta/pallas_call | solution.py:284
  43.4 2.4 %collective-permute-start.12 = (f32[2,2048]{1,0:T(2,128)S(1)}, f32[2,2048]{1,0:T(2,128)S(1)}, u32[]{:S(2)}, u32[]{:S(2)}) collective-permute-start(f32[2,2048]{1,0:T(2,128)S(1)} %far_delta.1.s0), channel_id=1, source_target_pairs={{0,136},{8,128},{128,8},{136,0},{1,137},{9,129},{129,9},{137,1},{2... | collective-permute-start | bytes 49160 | tf_op jit(solution)/shard_map/ppermute | solution.py:45
  45.8 0.4 collective-permute-start.11
  46.2 0.9 %collective-permute-start.10 = (f32[2,2048]{1,0:T(2,128)S(1)}, f32[2,2048]{1,0:T(2,128)S(1)}, u32[]{:S(2)}, u32[]{:S(2)}) collective-permute-start(f32[2,2048]{1,0:T(2,128)S(1)} %far_delta.1.s0), channel_id=1, source_target_pairs={{0,128},{128,0},{1,129},{129,1},{2,130},{130,2},{3,131},{131,3},{4... | collective-permute-start | bytes 49160 | tf_op jit(solution)/shard_map/ppermute | solution.py:45
  47.1 1.0 %collective-permute-done.12.s3 = f32[2,2048]{1,0:T(2,128)S(1)} collective-permute-done((f32[2,2048]{1,0:T(2,128)S(1)}, f32[2,2048]{1,0:T(2,128)S(1)}, u32[]{:S(2)}, u32[]{:S(2)}) %collective-permute-start.12) | collective-permute-done | bytes 16416 | tf_op jit(solution)/shard_map/ppermute | solution.py:45
  48.1 3.3 %collective-permute-done.10.s1 = f32[2,2048]{1,0:T(2,128)S(1)} collective-permute-done((f32[2,2048]{1,0:T(2,128)S(1)}, f32[2,2048]{1,0:T(2,128)S(1)}, u32[]{:S(2)}, u32[]{:S(2)}) %collective-permute-start.10) | collective-permute-done | bytes 16416 | tf_op jit(solution)/shard_map/ppermute | solution.py:45
  51.4 5.9 %gradients.1 = (f32[128,512]{1,0:T(8,128)S(1)}, f32[128,512]{1,0:T(8,128)S(1)}, bf16[128,512]{1,0:T(8,128)(2,1)S(1)}, bf16[128,512]{1,0:T(8,128)(2,1)S(1)}, bf16[1024,256]{1,0:T(8,128)(2,1)}) custom-call(s32[1024,1]{1,0:T(8,128)S(1)} %copy.12.kpos, s32[1,512]{1,0:T(1,128)S(1)} %add.133.qpos, bf16[128,512]{1,0:T(8,128)(2,1)S(1)} %copy-done, ...), custom_call_target="tpu_custom_call" | custom-call | tf_op jit(solution)/shard_map/gradients/pallas_call | solution.py:296
  57.3 6.9 %all-to-all-start.1 = ((bf16[8,128,256]{2,1,0:T(8,128)(2,1)}), bf16[8,128,256]{2,1,0:T(8,128)(2,1)S(1)}, u32[]{:S(2)}, u32[]{:S(2)}) async-start(bf16[8,128,256]{2,1,0:T(8,128)(2,1)} %bitcast.14), calls=%async_computation.1 | async-start | bytes 1048576 | tf_op jit(solution)/shard_map/all_to_all | solution.py:312
  64.2 0.5 collective-permute-start.13
  64.7 0.8 %collective-permute-done.14 = bf16[128,512]{1,0:T(8,128)(2,1)S(1)} collective-permute-done((bf16[128,512]{1,0:T(8,128)(2,1)S(1)}, bf16[128,512]{1,0:T(8,128)(2,1)S(1)}, u32[]{:S(2)}, u32[]{:S(2)}) %collective-permute-start.14) | collective-permute-done | bytes 131104 | tf_op jit(solution)/shard_map/ppermute | solution.py:45
  65.6 1.0 %collective-permute-start.15 = (bf16[128,512]{1,0:T(8,128)(2,1)S(1)}, bf16[128,512]{1,0:T(8,128)(2,1)S(1)}, u32[]{:S(2)}, u32[]{:S(2)}) collective-permute-start(bf16[128,512]{1,0:T(8,128)(2,1)S(1)} %add_convert_fusion), channel_id=1, source_target_pairs={{0,128},{128,0},{1,129},{129,1},{2,130},{130,2},{3,131},{131,3},{4... | collective-permute-start | bytes 393224 | tf_op jit(solution)/shard_map/ppermute | solution.py:45
  66.6 6.1 %collective-permute-done.15 = bf16[128,512]{1,0:T(8,128)(2,1)S(1)} collective-permute-done((bf16[128,512]{1,0:T(8,128)(2,1)S(1)}, bf16[128,512]{1,0:T(8,128)(2,1)S(1)}, u32[]{:S(2)}, u32[]{:S(2)}) %collective-permute-start.15) | collective-permute-done | bytes 131104 | tf_op jit(solution)/shard_map/ppermute | solution.py:45
  72.7 0.7 convert_add_fusion
  73.5 7.4 %all-to-all-done.1 = bf16[8,128,256]{2,1,0:T(8,128)(2,1)S(1)} async-done(((bf16[8,128,256]{2,1,0:T(8,128)(2,1)}), bf16[8,128,256]{2,1,0:T(8,128)(2,1)S(1)}, u32[]{:S(2)}, u32[]{:S(2)}) %all-to-all-start.1) | async-done | bytes 524320 | tf_op jit(solution)/shard_map/all_to_all | solution.py:312
  80.9 0.1 convert_reduce_fusion
  80.9 0.7 fusion.4
  (13 shorter events, 0.1 us)
Async XLA Ops:
  0.6 35.5 %copy-start = (bf16[128,512]{1,0:T(8,128)(2,1)S(1)}, bf16[128,512]{1,0:T(8,128)(2,1)}, u32[]{:S(2)}) copy-start(bf16[128,512]{1,0:T(8,128)(2,1)} %q0.2) | copy-start | bytes 393220
  0.6 13.8 %collective-permute-start = (bf16[128,512]{1,0:T(8,128)(2,1)}, bf16[128,512]{1,0:T(8,128)(2,1)S(1)}, u32[]{:S(2)}, u32[]{:S(2)}) collective-permute-start(bf16[128,512]{1,0:T(8,128)(2,1)} %param.9), channel_id=1, source_target_pairs={{0,4},{4,0},{1,5},{5,1},{2,6},{6,2},{3,7},{7,3},{8,12},{12,8},{9,1... | collective-permute-start | bytes 393224 | tf_op jit(solution)/shard_map/ppermute | solution.py:45
  4.0 32.2 %all-to-all-start = ((bf16[8,128,256]{2,1,0:T(8,128)(2,1)}), bf16[8,128,256]{2,1,0:T(8,128)(2,1)S(1)}, u32[]{:S(2)}, u32[]{:S(2)}) async-start(bf16[8,128,256]{2,1,0:T(8,128)(2,1)} %bitcast.23), calls=%async_computation | async-start | bytes 1048576 | tf_op jit(solution)/shard_map/all_to_all | solution.py:222
  14.5 11.1 %collective-permute-start.6 = (bf16[256,512]{1,0:T(8,128)(2,1)S(1)}, bf16[256,512]{1,0:T(8,128)(2,1)S(1)}, u32[]{:S(2)}, u32[]{:S(2)}) collective-permute-start(bf16[256,512]{1,0:T(8,128)(2,1)S(1)} %constant_dynamic-update-slice_fusion.refs_0_), channel_id=1, source_target_pairs={{0,2},{1,3},{2,0},{3,1},{4,6},{5,7},{6,4},{7,5},{8,10},{9,11},{10,... | collective-permute-start | bytes 786440 | tf_op jit(solution)/shard_map/ppermute | solution.py:45
  16.7 12.5 %collective-permute-start.5 = (bf16[256,512]{1,0:T(8,128)(2,1)S(1)}, bf16[256,512]{1,0:T(8,128)(2,1)S(1)}, u32[]{:S(2)}, u32[]{:S(2)}) collective-permute-start(bf16[256,512]{1,0:T(8,128)(2,1)S(1)} %constant_dynamic-update-slice_fusion.refs_0_), channel_id=1, source_target_pairs={{0,3},{1,0},{2,1},{3,2},{4,7},{5,4},{6,5},{7,6},{8,11},{9,8},{10,9... | collective-permute-start | bytes 786440 | tf_op jit(solution)/shard_map/ppermute | solution.py:45
  18.2 11.1 %collective-permute-start.4 = (bf16[256,512]{1,0:T(8,128)(2,1)S(1)}, bf16[256,512]{1,0:T(8,128)(2,1)S(1)}, u32[]{:S(2)}, u32[]{:S(2)}) collective-permute-start(bf16[256,512]{1,0:T(8,128)(2,1)S(1)} %constant_dynamic-update-slice_fusion.refs_0_), channel_id=1, source_target_pairs={{0,1},{1,2},{2,3},{3,0},{4,5},{5,6},{6,7},{7,4},{8,9},{9,10},{10,1... | collective-permute-start | bytes 786440 | tf_op jit(solution)/shard_map/ppermute | solution.py:45
  18.9 6.7 %collective-permute-start.1 = (bf16[128,512]{1,0:T(8,128)(2,1)}, bf16[128,512]{1,0:T(8,128)(2,1)S(1)}, u32[]{:S(2)}, u32[]{:S(2)}) collective-permute-start(bf16[128,512]{1,0:T(8,128)(2,1)} %q0.2), channel_id=1, source_target_pairs={{0,128},{128,0},{1,129},{129,1},{2,130},{130,2},{3,131},{131,3},{4... | collective-permute-start | bytes 393224 | tf_op jit(solution)/shard_map/ppermute | solution.py:45
  21.9 14.2 %collective-permute-start.2 = (bf16[128,512]{1,0:T(8,128)(2,1)}, bf16[128,512]{1,0:T(8,128)(2,1)S(1)}, u32[]{:S(2)}, u32[]{:S(2)}) collective-permute-start(bf16[128,512]{1,0:T(8,128)(2,1)} %q0.2), channel_id=1, source_target_pairs={{0,8},{8,0},{1,9},{9,1},{2,10},{10,2},{3,11},{11,3},{4,12},{12,4},... | collective-permute-start | bytes 393224 | tf_op jit(solution)/shard_map/ppermute | solution.py:45
  25.6 10.5 %collective-permute-start.3 = (bf16[128,512]{1,0:T(8,128)(2,1)S(1)}, bf16[128,512]{1,0:T(8,128)(2,1)S(1)}, u32[]{:S(2)}, u32[]{:S(2)}) collective-permute-start(bf16[128,512]{1,0:T(8,128)(2,1)S(1)} %collective-permute-done.1.q1), channel_id=1, source_target_pairs={{0,8},{8,0},{1,9},{9,1},{2,10},{10,2},{3,11},{11,3},{4,12},{12,4},... | collective-permute-start | bytes 393224 | tf_op jit(solution)/shard_map/ppermute | solution.py:45
  32.8 6.1 %collective-permute-start.8 = (bf16[128,512]{1,0:T(8,128)(2,1)S(1)}, bf16[128,512]{1,0:T(8,128)(2,1)S(1)}, u32[]{:S(2)}, u32[]{:S(2)}) collective-permute-start(bf16[128,512]{1,0:T(8,128)(2,1)S(1)} %upstream.1.u0), channel_id=1, source_target_pairs={{0,8},{8,0},{1,9},{9,1},{2,10},{10,2},{3,11},{11,3},{4,12},{12,4},... | collective-permute-start | bytes 393224 | tf_op jit(solution)/shard_map/ppermute | solution.py:45
  32.9 7.5 %collective-permute-start.7 = (bf16[128,512]{1,0:T(8,128)(2,1)S(1)}, bf16[128,512]{1,0:T(8,128)(2,1)S(1)}, u32[]{:S(2)}, u32[]{:S(2)}) collective-permute-start(bf16[128,512]{1,0:T(8,128)(2,1)S(1)} %upstream.1.u0), channel_id=1, source_target_pairs={{0,128},{128,0},{1,129},{129,1},{2,130},{130,2},{3,131},{131,3},{4... | collective-permute-start | bytes 393224 | tf_op jit(solution)/shard_map/ppermute | solution.py:45
  40.4 1.6 %collective-permute-start.9 = (bf16[128,512]{1,0:T(8,128)(2,1)S(1)}, bf16[128,512]{1,0:T(8,128)(2,1)S(1)}, u32[]{:S(2)}, u32[]{:S(2)}) collective-permute-start(bf16[128,512]{1,0:T(8,128)(2,1)S(1)} %collective-permute-done.7.u1), channel_id=1, source_target_pairs={{0,8},{8,0},{1,9},{9,1},{2,10},{10,2},{3,11},{11,3},{4,12},{12,4},... | collective-permute-start | bytes 393224 | tf_op jit(solution)/shard_map/ppermute | solution.py:45
  43.4 4.8 %collective-permute-start.12 = (f32[2,2048]{1,0:T(2,128)S(1)}, f32[2,2048]{1,0:T(2,128)S(1)}, u32[]{:S(2)}, u32[]{:S(2)}) collective-permute-start(f32[2,2048]{1,0:T(2,128)S(1)} %far_delta.1.s0), channel_id=1, source_target_pairs={{0,136},{8,128},{128,8},{136,0},{1,137},{9,129},{129,9},{137,1},{2... | collective-permute-start | bytes 49160 | tf_op jit(solution)/shard_map/ppermute | solution.py:45
  45.8 2.3 %collective-permute-start.11 = (f32[2,2048]{1,0:T(2,128)S(1)}, f32[2,2048]{1,0:T(2,128)S(1)}, u32[]{:S(2)}, u32[]{:S(2)}) collective-permute-start(f32[2,2048]{1,0:T(2,128)S(1)} %far_delta.1.s0), channel_id=1, source_target_pairs={{0,8},{8,0},{1,9},{9,1},{2,10},{10,2},{3,11},{11,3},{4,12},{12,4},... | collective-permute-start | bytes 49160 | tf_op jit(solution)/shard_map/ppermute | solution.py:45
  46.2 5.2 %collective-permute-start.10 = (f32[2,2048]{1,0:T(2,128)S(1)}, f32[2,2048]{1,0:T(2,128)S(1)}, u32[]{:S(2)}, u32[]{:S(2)}) collective-permute-start(f32[2,2048]{1,0:T(2,128)S(1)} %far_delta.1.s0), channel_id=1, source_target_pairs={{0,128},{128,0},{1,129},{129,1},{2,130},{130,2},{3,131},{131,3},{4... | collective-permute-start | bytes 49160 | tf_op jit(solution)/shard_map/ppermute | solution.py:45
  57.3 23.6 %all-to-all-start.1 = ((bf16[8,128,256]{2,1,0:T(8,128)(2,1)}), bf16[8,128,256]{2,1,0:T(8,128)(2,1)S(1)}, u32[]{:S(2)}, u32[]{:S(2)}) async-start(bf16[8,128,256]{2,1,0:T(8,128)(2,1)} %bitcast.14), calls=%async_computation.1 | async-start | bytes 1048576 | tf_op jit(solution)/shard_map/all_to_all | solution.py:312
  64.2 1.3 %collective-permute-start.14 = (bf16[128,512]{1,0:T(8,128)(2,1)S(1)}, bf16[128,512]{1,0:T(8,128)(2,1)S(1)}, u32[]{:S(2)}, u32[]{:S(2)}) collective-permute-start(bf16[128,512]{1,0:T(8,128)(2,1)S(1)} %get-tuple-element.21), channel_id=1, source_target_pairs={{0,8},{8,0},{1,9},{9,1},{2,10},{10,2},{3,11},{11,3},{4,12},{12,4},... | collective-permute-start | bytes 393224 | tf_op jit(solution)/shard_map/ppermute | solution.py:45
  64.2 2.4 %collective-permute-start.13 = (bf16[128,512]{1,0:T(8,128)(2,1)S(1)}, bf16[128,512]{1,0:T(8,128)(2,1)S(1)}, u32[]{:S(2)}, u32[]{:S(2)}) collective-permute-start(bf16[128,512]{1,0:T(8,128)(2,1)S(1)} %get-tuple-element.19), channel_id=1, source_target_pairs={{0,8},{8,0},{1,9},{9,1},{2,10},{10,2},{3,11},{11,3},{4,12},{12,4},... | collective-permute-start | bytes 393224 | tf_op jit(solution)/shard_map/ppermute | solution.py:45
  65.6 7.1 %collective-permute-start.15 = (bf16[128,512]{1,0:T(8,128)(2,1)S(1)}, bf16[128,512]{1,0:T(8,128)(2,1)S(1)}, u32[]{:S(2)}, u32[]{:S(2)}) collective-permute-start(bf16[128,512]{1,0:T(8,128)(2,1)S(1)} %add_convert_fusion), channel_id=1, source_target_pairs={{0,128},{128,0},{1,129},{129,1},{2,130},{130,2},{3,131},{131,3},{4... | collective-permute-start | bytes 393224 | tf_op jit(solution)/shard_map/ppermute | solution.py:45
